TPU v7x, 32 devices: a whole 2x2x4 slice. The times are simulated.
32 devices in a mesh: tile: 8 (over y, x, core), sect: 2 (over z_hi), lev: 2 (over z_lo).
Axes of the slice: x: 2, y: 2, z: 4 (z_hi: 2, z_lo: 2; z = z_hi * 2 + z_lo), core: 2. Of those that a mesh axis runs over, the one named last changes fastest.
Arguments:
- adjoint: float32 [2, 8, 64, 128, 128], P('sect', 'tile', 'lev'), may hold values from -6 to 6
- diffusion: float32 [2, 8, 128, 128], P('sect', 'tile'), may hold values from 0.02 to 0.12
- wet_mask: int32 [2, 8, 128, 128], P('sect', 'tile'), may hold values 0 or 1
- remap: int32 [2, 8, 128], P('sect', 'tile'), may hold values from 0 to 127
- coupling: float32 [2, 64], P('sect', 'lev'), may hold values from 0.1 to 0.5
- vert_inverse: float32 [2, 8, 64, 64], P('sect', 'tile')
- nbr_tile: int32 [8, 4], P('tile'), may hold values from -1 to 7, as said below
- nbr_side: int32 [8, 4], P('tile'), may hold values from 0 to 3
- nbr_flip: int32 [8, 4], P('tile'), may hold values from 0 to 1
Outputs:
- result: float32 [2, 8, 64, 128, 128], P('sect', 'tile', 'lev')
Inputs may be any that keep to these rules, and one draw needn't show every extreme that they name: `nbr_tile`: A side with a neighbour is named back by that neighbour's named side with the same flip.
All inputs are finite; a program needn't handle non-finite values. No bound on the sum of `wet_mask` on one device may be relied on, other than what follows from the above.
Results may differ from a plain program's by a relative error of at most 0.0001.
Values sent between devices are 32-bit elements; how exact they have to be, the bound alone decides.
No kernel may reach another device: no remote copies, remote signals or barrier semaphores. Data moves between devices by JAX's collectives and lax.ppermute only.
A program may use at most 64 MiB of HBM per device.

v0:
```python
import jax
import jax.numpy as jnp
from jax import lax
from jax.sharding import PartitionSpec as P


def swapped(block, axis, bit):
    count = lax.axis_size(axis)
    route = []
    for low in range(count):
        high = low | 1 << bit
        if high != low and high < count:
            route += [(low, high), (high, low)]
    return lax.ppermute(block, axis, route)


def edge_rows(field):
    return jnp.stack(
        [field[..., 0, :], field[..., -1, :], field[..., :, 0], field[..., :, -1]], axis=-3
    )


def oriented(picked, flips):
    return jnp.where((flips == 1)[:, :, None, None], picked[..., ::-1], picked)


def laplace(field, halo):
    side_cells = field.shape[3]
    position = lax.broadcasted_iota(jnp.int32, (1, 1, 1, side_cells), 3)
    upper = jnp.concatenate([halo[:, 0][:, :, None, :], field[:, :, :-1, :]], axis=2)
    lower = jnp.concatenate([field[:, :, 1:, :], halo[:, 1][:, :, None, :]], axis=2)
    left_side = jnp.pad(field[:, :, :, :-1], ((0, 0), (0, 0), (0, 0), (1, 0)))
    left_side = left_side + jnp.where(position == 0, halo[:, 2][:, :, :, None], jnp.float32(0.0))
    right_side = jnp.pad(field[:, :, :, 1:], ((0, 0), (0, 0), (0, 0), (0, 1)))
    right_side = right_side + jnp.where(
        position == side_cells - 1, halo[:, 3][:, :, :, None], jnp.float32(0.0)
    )
    return upper + lower + left_side + right_side - 4.0 * field


def pick_tile_rows(field, rows):
    return field[:, rows, :]


def on_device(
    adjoint, diffusion, wet_mask, remap, coupling, vert_inverse, nbr_tile, nbr_side, nbr_flip
):
    current = adjoint[0]
    diffusivity = diffusion[0]
    wet_cells = wet_mask[0].astype(jnp.float32)
    remap_rows = remap[0]
    level_gain = coupling[0]
    inverse = vert_inverse[0]
    level_rows = current.shape[1]
    my_first = lax.axis_index("lev") * level_rows
    for step in range(2):
        partner = swapped(current, "sect", 0)
        pulled = jax.vmap(pick_tile_rows)(partner, remap_rows)
        coupled = current + level_gain[None, :, None, None] * pulled
        whole = lax.all_gather(coupled, "lev", axis=1, tiled=True)
        own_columns = lax.dynamic_slice_in_dim(inverse, my_first, level_rows, 2)
        column = jnp.einsum("tkl,tkxy->tlxy", own_columns, whole, precision=lax.Precision.HIGHEST)
        flux = wet_cells[:, None] * diffusivity[:, None] * column
        edges = edge_rows(flux)
        all_edges = lax.all_gather(edges, "tile", axis=0, tiled=True)
        picked = all_edges[jnp.maximum(nbr_tile, 0), nbr_side]
        halo = jnp.where(
            (nbr_tile >= 0)[:, :, None, None], oriented(picked, nbr_flip), jnp.float32(0.0)
        )
        current = wet_cells[:, None] * (column + laplace(flux, halo))
    return current[None]


def solution(mesh):
    in_specs = (
        P("sect", "tile", "lev", None, None),
        P("sect", "tile", None, None),
        P("sect", "tile", None, None),
        P("sect", "tile", None),
        P("sect", "lev"),
        P("sect", "tile", None, None),
        P("tile", None),
        P("tile", None),
        P("tile", None),
    )
    out_specs = P("sect", "tile", "lev", None, None)
    return jax.shard_map(
        on_device, mesh=mesh, in_specs=in_specs, out_specs=out_specs, check_vma=False
    )
```

profile of v0, /device:TPU:8, one launch (start us, length us, event | category | flops | bytes accessed | tf_op | source)
XLA Modules:
  0.0 403.4 jit_solution(2878523833001333384)
XLA Ops:
  6.5 2.8 copy.65
  12.1 89.7 %collective-permute-done = f32[1,32,128,128]{3,1,2,0:T(8,128)} collective-permute-done((f32[1,32,128,128]{3,1,2,0:T(8,128)S(1)}, f32[1,32,128,128]{3,1,2,0:T(8,128)}, u32[]{:S(2)}, u32[]{:S(2)}) %collective-permute-start) | collective-permute-done | bytes 2097184 | tf_op jit(solution)/shard_map/ppermute | solution.py:14
  101.7 3.6 gather_fusion.2
  105.3 4.2 %fusion.16 = f32[1,32,128,128]{3,1,2,0:T(8,128)} fusion(f32[128,32,128]{2,1,0:T(8,128)} %gather_fusion.2, f32[32]{0:T(128)S(1)} %bitcast.114, f32[1,1,32,128,128]{4,3,2,1,0:T(8,128)S(1)} %copy-done.3), kind=kLoop, calls=%fused_computation.24 | loop fusion | flops 1048576 | bytes 6291584 | tf_op jit(solution)/shard_map/add | solution.py:59
  110.5 56.9 %all-gather.3.cloned.1.call-done = f32[1,64,128,128]{3,1,2,0:T(8,128)} async-done(((f32[1,32,128,128]{3,1,2,0:T(8,128)}), f32[1,64,128,128]{3,1,2,0:T(8,128)}) %all-gather.3.cloned.1.call-update) | async-done | bytes 4194320 | tf_op jit(solution)/shard_map/all_gather | solution.py:60
  167.4 4.0 fusion.2
  171.8 2.7 fusion.30
  174.5 2.8 fusion.31
  177.2 2.7 fusion.29
  180.0 2.7 copy.54
  182.6 2.7 copy.53
  185.3 10.2 %all_gather.13 = f32[8,4,32,128]{3,2,1,0:T(8,128)S(1)} all-gather(f32[1,4,32,128]{3,2,1,0:T(8,128)S(1)} %pad_maximum_fusion), channel_id=1, replica_groups=mesh['tile'=8,'sect'=2,'lev'=2] {'tile'}, dimensions={0}, use_global_device_ids=true | all-gather | bytes 589824 | tf_op jit(solution)/shard_map/all_gather | solution.py:65
  196.5 5.3 %fusion.8 = f32[1,32,128,128]{3,1,2,0:T(8,128)S(1)} fusion(f32[1,32,127,128]{3,1,2,0:T(8,128)} %get-tuple-element.16, f32[1,32,1,128]{3,1,2,0:T(8,128)S(1)} %get-tuple-element.28, f32[1,32,1,128]{3,1,2,0:T(8,128)S(1)} %get-tuple-element.27, f32[1,32,127,128]{3,1,2,0:T(8,128)} %get-tuple-element.15, f32[32,128,128]{2,0,1:T(8,128)S(1)} %fusion.2, ...), kind=kLoop, calls=%fused_computation.13 | loop fusion | flops 7340032 | bytes 12714240 | tf_op jit(solution)/shard_map/mul | solution.py:70
  205.5 90.3 %collective-permute-done.1 = f32[1,32,128,128]{3,1,2,0:T(8,128)} collective-permute-done((f32[1,32,128,128]{3,1,2,0:T(8,128)S(1)}, f32[1,32,128,128]{3,1,2,0:T(8,128)}, u32[]{:S(2)}, u32[]{:S(2)}) %collective-permute-start.1) | collective-permute-done | bytes 2097184 | tf_op jit(solution)/shard_map/ppermute | solution.py:14
  295.9 3.6 gather_fusion.3
  299.5 3.5 fusion.15
  303.0 56.8 %all-gather.5.cloned.1.call-done = f32[1,64,128,128]{3,1,2,0:T(8,128)} async-done(((f32[1,32,128,128]{3,1,2,0:T(8,128)}), f32[1,64,128,128]{3,1,2,0:T(8,128)}) %all-gather.5.cloned.1.call-update) | async-done | bytes 4194320 | tf_op jit(solution)/shard_map/all_gather | solution.py:60
  359.8 4.0 fusion
  364.2 2.7 fusion.27
  366.8 2.8 fusion.28
  369.6 2.7 fusion.26
  372.3 2.7 copy.58
  377.7 10.1 %all_gather.15 = f32[8,4,32,128]{3,2,1,0:T(8,128)S(1)} all-gather(f32[1,4,32,128]{3,2,1,0:T(8,128)S(1)} %pad_maximum_fusion.1), channel_id=1, replica_groups=mesh['tile'=8,'sect'=2,'lev'=2] {'tile'}, dimensions={0}, use_global_device_ids=true | all-gather | bytes 589824 | tf_op jit(solution)/shard_map/all_gather | solution.py:65
  388.7 5.3 %fusion.14 = f32[1,1,32,128,128]{4,2,3,1,0:T(8,128)S(1)} fusion(f32[1,32,127,128]{3,1,2,0:T(8,128)} %get-tuple-element.8, f32[1,32,1,128]{3,1,2,0:T(8,128)S(1)} %get-tuple-element.24, f32[1,32,1,128]{3,1,2,0:T(8,128)S(1)} %get-tuple-element.23, f32[1,32,127,128]{3,1,2,0:T(8,128)} %get-tuple-element.7, f32[32,128,128]{2,0,1:T(8,128)S(1)} %fusion, ...), kind=kLoop, calls=%fused_computation.20 | loop fusion | flops 7340032 | bytes 12714240 | tf_op jit(solution)/shard_map/broadcast_in_dim | solution.py:71
  (58 shorter events, 15.0 us)
Async XLA Ops:
  6.5 160.9 %copy-start = (f32[1,1,64,64]{3,2,1,0:T(8,128)S(1)}, f32[1,1,64,64]{3,2,1,0:T(8,128)}, u32[]{:S(2)}) copy-start(f32[1,1,64,64]{3,2,1,0:T(8,128)} %param.14) | copy-start | bytes 49156
  6.5 5.5 %copy-start.10 = (s32[1,1,128]{2,1,0:T(1,128)S(1)}, s32[1,1,128]{2,1,0:T(1,128)}, u32[]{:S(2)}) copy-start(s32[1,1,128]{2,1,0:T(1,128)} %param.12) | copy-start | bytes 1540
  6.5 160.9 %all-gather.3.cloned.1.call-start = ((), (), s32[]{:S(2)}) async-start(), calls=%async_computation | async-start | bytes 6291456 | tf_op jit(solution)/shard_map/all_gather | solution.py:60
  9.4 92.4 %collective-permute-start = (f32[1,32,128,128]{3,1,2,0:T(8,128)S(1)}, f32[1,32,128,128]{3,1,2,0:T(8,128)}, u32[]{:S(2)}, u32[]{:S(2)}) collective-permute-start(f32[1,32,128,128]{3,1,2,0:T(8,128)S(1)} %bitcast.109), channel_id=1, source_target_pairs={{0,2},{2,0},{1,3},{3,1},{4,6},{6,4},{5,7},{7,5},{8,10},{10,8},{9,1... | collective-permute-start | bytes 6291464 | tf_op jit(solution)/shard_map/ppermute | solution.py:14
  12.1 93.3 %copy-start.3 = (f32[1,1,32,128,128]{4,3,2,1,0:T(8,128)S(1)}, f32[1,1,32,128,128]{4,3,2,1,0:T(8,128)}, u32[]{:S(2)}) copy-start(f32[1,1,32,128,128]{4,3,2,1,0:T(8,128)} %param.9) | copy-start | bytes 6291460
  12.1 93.3 %copy-start.6 = (f32[1,32]{1,0:T(1,128)S(1)}, f32[1,32]{1,0:T(1,128)}, u32[]{:S(2)}) copy-start(f32[1,32]{1,0:T(1,128)} %param.13) | copy-start | bytes 388
  109.6 0.7 copy-start.7
  109.6 0.7 copy-start.8
  109.6 0.7 copy-start.9
  109.6 0.9 copy-start.4
  109.6 0.9 copy-start.5
  109.6 250.2 %all-gather.5.cloned.1.call-start = ((), (), s32[]{:S(2)}) async-start(), calls=%async_computation.1 | async-start | bytes 6291456 | tf_op jit(solution)/shard_map/all_gather | solution.py:60
  201.8 1.3 copy-start.1
  203.1 92.8 %collective-permute-start.1 = (f32[1,32,128,128]{3,1,2,0:T(8,128)S(1)}, f32[1,32,128,128]{3,1,2,0:T(8,128)}, u32[]{:S(2)}, u32[]{:S(2)}) collective-permute-start(f32[1,32,128,128]{3,1,2,0:T(8,128)S(1)} %fusion.8), channel_id=1, source_target_pairs={{0,2},{2,0},{1,3},{3,1},{4,6},{6,4},{5,7},{7,5},{8,10},{10,8},{9,1... | collective-permute-start | bytes 6291464 | tf_op jit(solution)/shard_map/ppermute | solution.py:14
  205.5 93.9 %copy-start.2 = (f32[1,32,128,128]{3,1,2,0:T(8,128)S(1)}, f32[1,32,128,128]{3,1,2,0:T(8,128)}, u32[]{:S(2)}) copy-start(f32[1,32,128,128]{3,1,2,0:T(8,128)} %copy-done.1) | copy-start | bytes 6291460
Sparse Core Ops, SparseCore 0:
  109.7 57.6 all-gather.2
  303.1 56.6 all-gather.4
where the time goes:
time: 406 us; the launch traced here: 403 us
  waiting for transfers between devices  294 us (72%)
  local copies, waits for them, and re-layouts  43.3 us (11%)
  blocking collectives  20.3 us (5%)
  other arithmetic  19.3 us (5%)
  between operations  13.6 us (3%)
  matrix products  8.01 us (2%)
  starting transfers between devices  5.11 us (1%)
    ppermute x2, waiting for transfers between devices, swapped(): return lax.ppermute(block, axis, route)  180 us
    all_gather x2, waiting for transfers between devices, on_device(): whole = lax.all_gather(coupled, 'lev', axis=1, tiled=True)  114 us
    all_gather x2, blocking collectives, on_device(): all_edges = lax.all_gather(edges, 'tile', axis=0, tiled=True)  20.3 us
    slice x4, local copies, waits for them, and re-layouts, edge_rows(): field[..., :, 0]  10.8 us
  transfers between devices with their start and end apart: 4, of which 4 were waited for; matrix products, arithmetic and copies ran while one was open for 0% of the time, Pallas kernels for 0%

commit v1 on v0

v1 whole, which is shorter than its diff:
```python
import jax
import jax.numpy as jnp
from jax import lax
from jax.experimental import pallas as pl
from jax.experimental.pallas import tpu as pltpu
from jax.sharding import PartitionSpec as P

Z = ("sect", "lev")
PARTS = 4
HIGHEST = lax.Precision.HIGHEST


def exchanged(block, bits):
    return lax.ppermute(block, Z, [(at, at ^ bits) for at in range(PARTS)])


def split_kernel(place, field, *outs_and_scratch):
    outs, turned = outs_and_scratch[:PARTS], outs_and_scratch[PARTS]
    levels, rows, cols = field.shape
    width = cols // PARTS
    zero = jnp.zeros((levels, rows), jnp.float32)
    turned[0:levels, :] = zero
    turned[(cols + 1) * levels : (cols + 2) * levels, :] = zero
    for level in range(levels):
        turned[pl.ds(levels + level, cols, stride=levels), :] = field[level].T
    for bits, out in enumerate(outs):
        first = (place[0] ^ bits) * (width * levels)
        out[...] = turned[pl.ds(pl.multiple_of(first, 8), (width + 2) * levels), :].reshape(out.shape)


def split_columns(field, place):
    levels, rows, cols = field.shape
    part = jax.ShapeDtypeStruct((cols // PARTS + 2, levels, rows), jnp.float32)
    return pl.pallas_call(
        split_kernel,
        out_shape=[part] * PARTS,
        in_specs=[
            pl.BlockSpec(memory_space=pltpu.SMEM),
            pl.BlockSpec(memory_space=pltpu.VMEM),
        ],
        out_specs=[pl.BlockSpec(memory_space=pltpu.VMEM)] * PARTS,
        scratch_shapes=[pltpu.VMEM(((cols + 2) * levels, rows), jnp.float32)],
        name="split_columns",
    )(place, field)


def join_kernel(place, p0, p1, p2, p3, sides, top_bottom, out, turned):
    levels, rows, cols = out.shape
    width = cols // PARTS
    for bits, part in enumerate((p0, p1, p2, p3)):
        first = (place[0] ^ bits) * (width * levels)
        turned[pl.ds(pl.multiple_of(first, 8), width * levels), :] = part[...].reshape(width * levels, rows)
    for part in range(PARTS):
        for side in range(2):
            at = (part * width + side * (width - 1)) * levels
            turned[at : at + levels, :] = turned[at : at + levels, :] + sides[part, side]
    row = lax.broadcasted_iota(jnp.int32, (rows, cols), 0)
    for level in range(levels):
        plane = turned[pl.ds(level, cols, stride=levels), :].T
        top = top_bottom[0, level : level + 1, :]
        bottom = top_bottom[1, level : level + 1, :]
        out[level] = plane + jnp.where(row == 0, top, jnp.where(row == rows - 1, bottom, 0.0))


def join_columns(parts, place, sides, top_bottom):
    width, levels, rows = parts[0].shape
    cols = width * PARTS
    return pl.pallas_call(
        join_kernel,
        out_shape=jax.ShapeDtypeStruct((levels, rows, cols), jnp.float32),
        in_specs=[pl.BlockSpec(memory_space=pltpu.SMEM)] + [pl.BlockSpec(memory_space=pltpu.VMEM)] * 6,
        out_specs=pl.BlockSpec(memory_space=pltpu.VMEM),
        scratch_shapes=[pltpu.VMEM((cols * levels, rows), jnp.float32)],
        name="join_columns",
    )(place, *parts, sides, top_bottom)


def halves(value):
    high = value.astype(jnp.bfloat16)
    low = (value - high.astype(jnp.float32)).astype(jnp.bfloat16)
    return high, low


def steps_kernel(
    place, x0, x1, x2, x3, weights, gains, rows_from, wet, spread, h0, h1, h2, h3,
    r0, r1, r2, r3, e0, e1, e2, e3, column, flux, state,
):
    ins, halos, outs, edges = (x0, x1, x2, x3), (h0, h1, h2, h3), (r0, r1, r2, r3), (e0, e1, e2, e3)
    width, half, rows = r0.shape
    levels = 2 * half
    lane = lax.broadcasted_iota(jnp.int32, (levels, rows), 1)
    mixes, picks = [], []
    for comp in range(2):
        high, low = halves(weights[comp])
        mixes.append(jnp.concatenate([high, low, high], axis=1))
        picks.append(jnp.broadcast_to(rows_from[comp : comp + 1, :], (levels, rows)))

    def picked(value, index):
        return jnp.take_along_axis(value, index, axis=1, mode="promise_in_bounds")

    def solve(blocks, at):
        for comp in range(2):
            rights = []
            for block in blocks:
                coupled = block[comp] + gains[comp] * picked(block[1 - comp], picks[comp])
                high, low = halves(coupled)
                rights.append(jnp.concatenate([high, high, low], axis=0))
            solved = jnp.dot(
                mixes[comp], jnp.concatenate(rights, axis=1), preferred_element_type=jnp.float32
            )
            for b in range(len(blocks)):
                one = solved[:, b * rows : (b + 1) * rows]
                column[comp, at + b] = one
                flux[comp, at + b] = one * spread[comp, pl.ds(at + b, 1), :]

    def first_solve(pair, carry):
        at = 2 * pair
        blocks = []
        for b in range(2):
            blocks.append(
                [jnp.concatenate([ins[2 * c][at + b], ins[2 * c + 1][at + b]], axis=0) for c in range(2)]
            )
        solve(blocks, at)
        return carry

    lax.fori_loop(0, (width + 2) // 2, first_solve, 0)

    def side(comp, slot):
        return jnp.concatenate([halos[2 * comp][slot], halos[2 * comp + 1][slot]], axis=0)

    @pl.when(place[0] == 0)
    def _():
        for comp in range(2):
            flux[comp, 0] = side(comp, 0)

    @pl.when(place[0] == PARTS - 1)
    def _():
        for comp in range(2):
            flux[comp, width + 1] = side(comp, 0)

    ends = [side(comp, 1) for comp in range(2)]

    def first_spread(j, carry):
        for comp in range(2):
            mid = flux[comp, j + 1]
            above = jnp.where(lane == 0, picked(ends[comp], jnp.full((levels, rows), j)), pltpu.roll(mid, 1, 1))
            below = jnp.where(
                lane == rows - 1,
                picked(ends[comp], jnp.full((levels, rows), j + width)),
                pltpu.roll(mid, rows - 1, 1),
            )
            total = above + below + flux[comp, j] + flux[comp, j + 2] - 4.0 * mid
            state[comp, j] = wet[comp, pl.ds(j + 1, 1), :] * (column[comp, j + 1] + total)
        return carry

    lax.fori_loop(0, width, first_spread, 0)

    def second_solve(pair, carry):
        at = 2 * pair
        solve([[state[c, at + b] for c in range(2)] for b in range(2)], at + 1)
        return carry

    lax.fori_loop(0, width // 2, second_solve, 0)
    for comp in range(2):
        flux[comp, 0] = jnp.zeros((levels, rows), jnp.float32)
        flux[comp, width + 1] = jnp.zeros((levels, rows), jnp.float32)

    def second_spread(j, carry):
        kept = []
        for comp in range(2):
            mid = flux[comp, j + 1]
            above = jnp.where(lane == 0, 0.0, pltpu.roll(mid, 1, 1))
            below = jnp.where(lane == rows - 1, 0.0, pltpu.roll(mid, rows - 1, 1))
            total = above + below + flux[comp, j] + flux[comp, j + 2] - 4.0 * mid
            done = wet[comp, pl.ds(j + 1, 1), :] * (column[comp, j + 1] + total)
            outs[2 * comp][j] = done[:half]
            outs[2 * comp + 1][j] = done[half:]
            top = picked(mid, jnp.zeros((levels, rows), jnp.int32))
            bottom = picked(mid, jnp.full((levels, rows), rows - 1))
            kept.append(jnp.where(lane == j, top, jnp.where(lane == j + width, bottom, carry[comp])))
        return tuple(kept)

    empty = jnp.zeros((levels, rows), jnp.float32)
    tops = lax.fori_loop(0, width, second_spread, (empty, empty))
    for comp in range(2):
        for part in range(2):
            edge = edges[2 * comp + part]
            span = slice(part * half, (part + 1) * half)
            edge[0] = flux[comp, 1, span, :]
            edge[1] = flux[comp, width, span, :]
            edge[2] = tops[comp][span]


def two_steps(place, parts, weights, gains, rows_from, wet, spread, halos):
    wide, half, rows = parts[0].shape
    width = wide - 2
    part = jax.ShapeDtypeStruct((width, half, rows), jnp.float32)
    edge = jax.ShapeDtypeStruct((3, half, rows), jnp.float32)
    outs = pl.pallas_call(
        steps_kernel,
        out_shape=[part] * PARTS + [edge] * PARTS,
        in_specs=[pl.BlockSpec(memory_space=pltpu.SMEM)] + [pl.BlockSpec(memory_space=pltpu.VMEM)] * 13,
        out_specs=[pl.BlockSpec(memory_space=pltpu.VMEM)] * (2 * PARTS),
        scratch_shapes=[
            pltpu.VMEM((2, wide, 2 * half, rows), jnp.float32),
            pltpu.VMEM((2, wide, 2 * half, rows), jnp.float32),
            pltpu.VMEM((2, width, 2 * half, rows), jnp.float32),
        ],
        name="two_steps",
    )(place, *parts, weights, gains, rows_from, wet, spread, *halos)
    return outs[:PARTS], outs[PARTS:]


def tile_halo(edges, nbr_tile, nbr_side, nbr_flip):
    every = lax.all_gather(edges, "tile", axis=0)
    picked = every[jnp.maximum(nbr_tile, 0), nbr_side]
    turned = jnp.where((nbr_flip == 1)[:, None, None], picked[..., ::-1], picked)
    return jnp.where((nbr_tile >= 0)[:, None, None], turned, jnp.float32(0.0))


def on_device(
    adjoint, diffusion, wet_mask, remap, coupling, vert_inverse, nbr_tile, nbr_side, nbr_flip
):
    field = adjoint[0, 0]
    half, rows, cols = field.shape
    width = cols // PARTS
    level_at = lax.axis_index("lev")
    spot = lax.axis_index("sect") * 2 + level_at
    place = spot[None].astype(jnp.int32)
    wet = wet_mask[0, 0].astype(jnp.float32)
    spread = wet * diffusion[0, 0]
    near = (nbr_tile[0], nbr_side[0], nbr_flip[0])

    parts = split_columns(field, place)
    arrived = [parts[0]] + [exchanged(parts[bits], bits) for bits in range(1, PARTS)]

    order = vert_inverse[0, 0]
    order = jnp.where(level_at == 0, order, jnp.roll(order, half, axis=0))
    order = jnp.where(level_at == 0, order, jnp.roll(order, half, axis=1))
    gain = jnp.concatenate([coupling[0], exchanged(coupling[0], 1)])
    my_rows = remap[0, 0]
    other_rows = exchanged(my_rows, 2)

    def padded(plane):
        return jnp.pad(plane.T, ((1, 1), (0, 0)))

    wet_cols, spread_cols = padded(wet), padded(spread)

    def cut(plane, part):
        return lax.dynamic_slice_in_dim(plane, part * width, width + 2, 0)

    pack = jnp.concatenate(
        [
            cut(wet_cols, spot ^ 2),
            cut(spread_cols, spot ^ 2),
            order.reshape(-1, rows),
            jnp.pad(gain, (0, rows - gain.shape[0]))[None],
        ]
    )
    pack = exchanged(pack, 2)
    tall = width + 2
    both_wet = jnp.stack([cut(wet_cols, spot), pack[:tall]])
    both_spread = jnp.stack([cut(spread_cols, spot), pack[tall : 2 * tall]])
    other_order = pack[2 * tall : -1].reshape(order.shape)
    weights = jnp.stack([order.T, other_order.T])
    gains = jnp.stack([gain, pack[-1, : gain.shape[0]]])
    gains = jnp.broadcast_to(gains[:, :, None], gains.shape + (rows,))
    rows_from = jnp.stack([my_rows, other_rows])

    side_columns = [field[:, :, 0], field[:, :, cols - 1]]
    own = jnp.stack([field[:, 0, :], field[:, rows - 1, :]] + side_columns)
    lent = jnp.stack(
        [
            lax.dynamic_index_in_dim(field, other_rows[0], 1, False),
            lax.dynamic_index_in_dim(field, other_rows[rows - 1], 1, False),
        ]
        + side_columns
    )
    own_all = jnp.concatenate([own, exchanged(own, 1)], axis=1)
    pulled = jnp.concatenate([exchanged(lent, 2), exchanged(lent, 3)], axis=1)
    choose = (jnp.arange(rows)[:, None] == my_rows[None, :]).astype(jnp.float32)
    pulled_columns = jnp.einsum("slq,qr->slr", pulled[2:], choose, precision=HIGHEST)
    coupled = own_all + gain[None, :, None] * jnp.concatenate([pulled[:2], pulled_columns])
    solved = jnp.einsum("kl,skx->slx", order[:, :half], coupled, precision=HIGHEST)

    def border(plane):
        return jnp.stack([plane[0], plane[rows - 1], plane[:, 0], plane[:, cols - 1]])[:, None, :]

    halo = tile_halo(solved * border(spread), *near)
    blocks = []
    for part in range(PARTS):
        span = slice(part * width, (part + 1) * width)
        ends = jnp.concatenate([halo[0][:, span], halo[1][:, span]], axis=1)
        ends = jnp.pad(ends, ((0, 0), (0, rows - 2 * width)))
        blocks.append(jnp.stack([halo[2] if part == 0 else halo[3], ends]))
    blocks = jnp.stack(blocks)
    halos = [blocks[spot]] + [exchanged(blocks[spot ^ bits], bits) for bits in range(1, PARTS)]

    results, edges = two_steps(
        place, arrived, weights, gains, rows_from, both_wet, both_spread, halos
    )

    edges = [edges[0]] + [exchanged(edges[bits], bits) for bits in range(1, PARTS)]
    results = [results[0]] + [exchanged(results[bits], bits) for bits in range(1, PARTS)]
    edges = jnp.stack(edges)[spot ^ jnp.arange(PARTS)]
    top = jnp.concatenate([edges[part, 2, :, :width] for part in range(PARTS)], axis=1)
    bottom = jnp.concatenate([edges[part, 2, :, width : 2 * width] for part in range(PARTS)], axis=1)
    halo = tile_halo(jnp.stack([top, bottom, edges[0, 0], edges[PARTS - 1, 1]]), *near)
    sides = []
    for part in range(PARTS):
        left = halo[2] if part == 0 else edges[part - 1, 1]
        right = halo[3] if part == PARTS - 1 else edges[part + 1, 0]
        sides.append(
            jnp.stack([left * wet[:, part * width], right * wet[:, (part + 1) * width - 1]])
        )
    top_bottom = jnp.stack([halo[0] * wet[0], halo[1] * wet[rows - 1]])
    return join_columns(results, place, jnp.stack(sides), top_bottom)[None, None]


def solution(mesh):
    in_specs = (
        P("sect", "tile", "lev", None, None),
        P("sect", "tile", None, None),
        P("sect", "tile", None, None),
        P("sect", "tile", None),
        P("sect", "lev"),
        P("sect", "tile", None, None),
        P("tile", None),
        P("tile", None),
        P("tile", None),
    )
    out_specs = P("sect", "tile", "lev", None, None)
    return jax.shard_map(
        on_device, mesh=mesh, in_specs=in_specs, out_specs=out_specs, check_vma=False
    )
```

time: 406 us -> 177 us (0.44)
  waiting for transfers between devices: 294 us -> 55.2 us
  Pallas kernels: 0 us -> 31 us
  starting transfers between devices: 5.11 us -> 32.9 us
  local copies, waits for them, and re-layouts: 43.3 us -> 16.8 us
  between operations: 13.6 us -> 4.09 us
  matrix products: 8.01 us -> 1.88 us
  other arithmetic: 19.3 us -> 14.6 us
    ppermute x2 -> x18, waiting for transfers between devices: 180 us -> 55.2 us  [exchanged(): return lax.ppermute(block, Z, [(at, at ^ bits) for at in range(PARTS)])]
    all_gather x2 -> x0, waiting for transfers between devices: 114 us -> none  [on_device(): whole = lax.all_gather(coupled, 'lev', axis=1, tiled=True)]
    pallas_call x0 -> x3, Pallas kernels: none -> 31 us  [the longest x1 22.2 us: two_steps(): pl.pallas_call(steps_kernel, out_shape=[part] * PARTS + [edge] * PARTS, i...]
    ppermute x2 -> x18, starting transfers between devices: 5.06 us -> 32.9 us  [exchanged(): return lax.ppermute(block, Z, [(at, at ^ bits) for at in range(PARTS)])]
    slice x10 -> x15, local copies, waits for them, and re-layouts: 27 us -> 5.46 us  [the longest x1 2.31 us: on_device(): side_columns = [field[:, :, 0], field[:, :, cols - 1]]]
    another operation x2 -> x25, other arithmetic: 0.01 us -> 8.71 us  [the longest x1 1.39 us: on_device(): weights = jnp.stack([order.T, other_order.T])]
    add x2 -> x0, other arithmetic: 7.71 us -> none  [on_device(): coupled = current + level_gain[None, :, None, None] * pulled]
    gather x5 -> x3, local copies, waits for them, and re-layouts: 8.32 us -> 1.68 us  [the longest x2 1.12 us: tile_halo(): picked = every[jnp.maximum(nbr_tile, 0), nbr_side]]
  transfers between devices with their start and end apart: 4 -> 18, of which waited for: 4 -> 7; matrix products, arithmetic and copies ran while one was open for 0% -> 18% of each run, Pallas kernels for 0% -> 3%
where the time goes in v1:
time: 177 us; the launch traced here: 176 us
  waiting for transfers between devices  55.2 us (31%)
  starting transfers between devices  32.9 us (19%)
  Pallas kernels  31 us (18%)
  blocking collectives  19.7 us (11%)
  local copies, waits for them, and re-layouts  16.8 us (9%)
  other arithmetic  14.6 us (8%)
  between operations  4.09 us (2%)
  matrix products  1.88 us (1%)
    ppermute x18, waiting for transfers between devices, exchanged(): return lax.ppermute(block, Z, [(at, at ^ bits) for at in range(PARTS)])  55.2 us
    ppermute x18, starting transfers between devices, exchanged(): return lax.ppermute(block, Z, [(at, at ^ bits) for at in range(PARTS)])  32.9 us
    pallas_call x1, Pallas kernels, two_steps(): pl.pallas_call(steps_kernel, out_shape=[part] * PARTS + [edge] * PARTS, i...  22.2 us
    all_gather x2, blocking collectives, tile_halo(): every = lax.all_gather(edges, 'tile', axis=0)  19.7 us
    pallas_call x1, Pallas kernels, split_columns(): pl.pallas_call(split_kernel, out_shape=[part] * PARTS, in_specs=[pl.Block...  4.54 us
    pallas_call x1, Pallas kernels, join_columns(): pl.pallas_call(join_kernel, out_shape=jax.ShapeDtypeStruct((levels, rows,...  4.28 us
  transfers between devices with their start and end apart: 18, of which 7 were waited for; matrix products, arithmetic and copies ran while one was open for 18% of the time, Pallas kernels for 3%

profile of v1, /device:TPU:8, one launch (start us, length us, event | category | flops | bytes accessed | tf_op | source)
XLA Modules:
  0.0 176.3 jit_solution(15607939090007829356)
XLA Ops:
  0.0 3.0 %collective-permute-start.5 = (s32[128]{0:T(128)}, s32[128]{0:T(128)}, u32[]{:S(2)}, u32[]{:S(2)}) collective-permute-start(s32[128]{0:T(128)} %bitcast.209), channel_id=1, source_target_pairs={{0,2},{1,3},{2,0},{3,1},{4,6},{5,7},{6,4},{7,5},{8,10},{9,11},{10,... | collective-permute-start | bytes 1544 | tf_op jit(solution)/shard_map/ppermute | solution.py:14
  3.0 4.5 %split_columns.1 = (f32[34,32,128]{2,1,0:T(8,128)}, f32[34,32,128]{2,1,0:T(8,128)}, f32[34,32,128]{2,1,0:T(8,128)}, f32[34,32,128]{2,1,0:T(8,128)}) custom-call(s32[1]{0:T(128)} %bitcast.place, f32[32,128,128]{2,1,0:T(8,128)} %bitcast.187), custom_call_target="tpu_custom_call" | custom-call | tf_op jit(solution)/shard_map/split_columns/pallas_call | solution.py:34
  7.6 1.6 collective-permute-start
  9.5 1.6 collective-permute-start.2
  12.4 2.3 %slice_reduce_fusion.1 = (f32[32,128]{1,0:T(8,128)S(1)}, f32[32,128]{1,0:T(8,128)}) fusion(f32[32,128,128]{2,1,0:T(8,128)S(1)} %bitcast.188), kind=kLoop, calls=%fused_computation.4 | loop fusion | bytes 65536 | tf_op jit(solution)/shard_map/slice | solution.py:270
  35.8 3.0 %collective-permute-start.8 = (f32[4,32,128]{2,1,0:T(8,128)S(1)}, f32[4,32,128]{2,1,0:T(8,128)S(1)}, u32[]{:S(2)}, u32[]{:S(2)}) collective-permute-start(f32[4,32,128]{2,1,0:T(8,128)S(1)} %get-tuple-element.88), channel_id=1, source_target_pairs={{0,3},{1,2},{2,1},{3,0},{4,7},{5,6},{6,5},{7,4},{8,11},{9,10},{10,... | collective-permute-start | bytes 196616 | tf_op jit(solution)/shard_map/ppermute | solution.py:14
  40.0 21.1 %collective-permute-done.4 = f32[101,128]{1,0:T(8,128)S(1)} collective-permute-done((f32[101,128]{1,0:T(8,128)}, f32[101,128]{1,0:T(8,128)S(1)}, u32[]{:S(2)}, u32[]{:S(2)}) %collective-permute-start.4) | collective-permute-done | bytes 51744 | tf_op jit(solution)/shard_map/ppermute | solution.py:14
  61.1 3.3 %collective-permute-start.7 = (f32[4,32,128]{2,1,0:T(8,128)S(1)}, f32[4,32,128]{2,1,0:T(8,128)S(1)}, u32[]{:S(2)}, u32[]{:S(2)}) collective-permute-start(f32[4,32,128]{2,1,0:T(8,128)S(1)} %get-tuple-element.88), channel_id=1, source_target_pairs={{0,2},{1,3},{2,0},{3,1},{4,6},{5,7},{6,4},{7,5},{8,10},{9,11},{10,... | collective-permute-start | bytes 196616 | tf_op jit(solution)/shard_map/ppermute | solution.py:14
  64.5 1.4 pad_maximum_fusion.7.weights
  66.8 3.6 %collective-permute-start.6 = (f32[4,32,128]{2,1,0:T(8,128)S(1)}, f32[4,32,128]{2,1,0:T(8,128)S(1)}, u32[]{:S(2)}, u32[]{:S(2)}) collective-permute-start(f32[4,32,128]{2,1,0:T(8,128)S(1)} %get-tuple-element.89), channel_id=1, source_target_pairs={{0,1},{1,0},{2,3},{3,2},{4,5},{5,4},{6,7},{7,6},{8,9},{9,8},{10,11... | collective-permute-start | bytes 196616 | tf_op jit(solution)/shard_map/ppermute | solution.py:14
  73.7 9.9 %all-gather = f32[32,32,128]{2,1,0:T(8,128)S(1)} all-gather(f32[4,32,128]{2,1,0:T(8,128)S(1)} %fusion), channel_id=2, replica_groups=mesh['tile'=8,'sect'=2,'lev'=2] {'tile'}, dimensions={0}, use_global_device_ids=true | all-gather | bytes 589824 | tf_op jit(solution)/shard_map/all_gather | solution.py:215
  87.0 3.5 %collective-permute-start.10 = (f32[2,32,128]{2,1,0:T(8,128)S(1)}, f32[2,32,128]{2,1,0:T(8,128)S(1)}, u32[]{:S(2)}, u32[]{:S(2)}) collective-permute-start(f32[2,32,128]{2,1,0:T(8,128)S(1)} %get-tuple-element.56), channel_id=1, source_target_pairs={{0,2},{1,3},{2,0},{3,1},{4,6},{5,7},{6,4},{7,5},{8,10},{9,11},{10,... | collective-permute-start | bytes 98312 | tf_op jit(solution)/shard_map/ppermute | solution.py:14
  90.5 3.1 %collective-permute-start.9 = (f32[2,32,128]{2,1,0:T(8,128)S(1)}, f32[2,32,128]{2,1,0:T(8,128)S(1)}, u32[]{:S(2)}, u32[]{:S(2)}) collective-permute-start(f32[2,32,128]{2,1,0:T(8,128)S(1)} %get-tuple-element.57), channel_id=1, source_target_pairs={{0,1},{1,0},{2,3},{3,2},{4,5},{5,4},{6,7},{7,6},{8,9},{9,8},{10,11... | collective-permute-start | bytes 98312 | tf_op jit(solution)/shard_map/ppermute | solution.py:14
  93.6 1.9 %collective-permute-done.9.h1 = f32[2,32,128]{2,1,0:T(8,128)S(1)} collective-permute-done((f32[2,32,128]{2,1,0:T(8,128)S(1)}, f32[2,32,128]{2,1,0:T(8,128)S(1)}, u32[]{:S(2)}, u32[]{:S(2)}) %collective-permute-start.9) | collective-permute-done | bytes 32800 | tf_op jit(solution)/shard_map/ppermute | solution.py:14
  96.6 22.2 %two_steps.1 = (f32[32,32,128]{2,1,0:T(8,128)}, f32[32,32,128]{2,1,0:T(8,128)}, f32[32,32,128]{2,1,0:T(8,128)}, f32[32,32,128]{2,1,0:T(8,128)}, f32[3,32,128]{2,...) custom-call(s32[1]{0:T(128)} %bitcast.place, ...), custom_call_target="tpu_custom_call" | custom-call | tf_op jit(solution)/shard_map/two_steps/pallas_call | solution.py:199
  118.8 2.1 %collective-permute-start.15 = (f32[3,32,128]{2,1,0:T(8,128)}, f32[3,32,128]{2,1,0:T(8,128)S(1)}, u32[]{:S(2)}, u32[]{:S(2)}) collective-permute-start(f32[3,32,128]{2,1,0:T(8,128)} %get-tuple-element.26), channel_id=1, source_target_pairs={{0,1},{1,0},{2,3},{3,2},{4,5},{5,4},{6,7},{7,6},{8,9},{9,8},{10,11... | collective-permute-start | bytes 147464 | tf_op jit(solution)/shard_map/ppermute | solution.py:14
  120.9 1.5 collective-permute-start.17
  122.4 2.9 %collective-permute-start.12 = (f32[32,32,128]{2,1,0:T(8,128)}, f32[32,32,128]{2,1,0:T(8,128)S(1)}, u32[]{:S(2)}, u32[]{:S(2)}) collective-permute-start(f32[32,32,128]{2,1,0:T(8,128)} %get-tuple-element.22), channel_id=1, source_target_pairs={{0,1},{1,0},{2,3},{3,2},{4,5},{5,4},{6,7},{7,6},{8,9},{9,8},{10,11... | collective-permute-start | bytes 1572872 | tf_op jit(solution)/shard_map/ppermute | solution.py:14
  125.3 1.5 collective-permute-start.14
  128.5 9.8 %all-gather.1 = f32[32,32,128]{2,1,0:T(8,128)S(1)} all-gather(f32[4,32,128]{2,1,0:T(8,128)S(1)} %pad_maximum_fusion.8), channel_id=3, replica_groups=mesh['tile'=8,'sect'=2,'lev'=2] {'tile'}, dimensions={0}, use_global_device_ids=true | all-gather | bytes 589824 | tf_op jit(solution)/shard_map/all_gather | solution.py:215
  140.6 5.7 %collective-permute-done.12.p1 = f32[32,32,128]{2,1,0:T(8,128)S(1)} collective-permute-done((f32[32,32,128]{2,1,0:T(8,128)}, f32[32,32,128]{2,1,0:T(8,128)S(1)}, u32[]{:S(2)}, u32[]{:S(2)}) %collective-permute-start.12) | collective-permute-done | bytes 524320 | tf_op jit(solution)/shard_map/ppermute | solution.py:14
  146.3 14.5 %collective-permute-done.13.p2 = f32[32,32,128]{2,1,0:T(8,128)S(1)} collective-permute-done((f32[32,32,128]{2,1,0:T(8,128)}, f32[32,32,128]{2,1,0:T(8,128)S(1)}, u32[]{:S(2)}, u32[]{:S(2)}) %collective-permute-start.13) | collective-permute-done | bytes 524320 | tf_op jit(solution)/shard_map/ppermute | solution.py:14
  160.7 10.5 %collective-permute-done.14.p3 = f32[32,32,128]{2,1,0:T(8,128)S(1)} collective-permute-done((f32[32,32,128]{2,1,0:T(8,128)}, f32[32,32,128]{2,1,0:T(8,128)S(1)}, u32[]{:S(2)}, u32[]{:S(2)}) %collective-permute-start.14) | collective-permute-done | bytes 524320 | tf_op jit(solution)/shard_map/ppermute | solution.py:14
  172.0 4.3 %join_columns.1 = f32[32,128,128]{2,1,0:T(8,128)} custom-call(s32[1]{0:T(128)} %bitcast.place, f32[32,32,128]{2,1,0:T(8,128)} %get-tuple-element.21.p0, f32[32,32,128]{2,1,0:T(8,128)} %copy-done.3, f32[32,32,128]{2,1,0:T(8,128)} %copy-done.4, f32[32,32,128]{2,1,0:T(8,128)} %copy-done.5, f32[4,2,32,128]{3,2,1,0:T(8,128)} %pad_maximum_fusion.2.sides, ...), custom_call_target="tpu_custom_call" | custom-call | tf_op jit(solution)/shard_map/join_columns/pallas_call | solution.py:68
  (161 shorter events, 33.5 us)
Async XLA Ops:
  0.0 26.9 %collective-permute-start.3 = (f32[32]{0:T(128)}, f32[32]{0:T(128)}, u32[]{:S(2)}, u32[]{:S(2)}) collective-permute-start(f32[32]{0:T(128)} %bitcast.212), channel_id=1, source_target_pairs={{0,1},{1,0},{2,3},{3,2},{4,5},{5,4},{6,7},{7,6},{8,9},{9,8},{10,11... | collective-permute-start | bytes 392 | tf_op jit(solution)/shard_map/ppermute | solution.py:14
  0.0 30.1 %collective-permute-start.5 = (s32[128]{0:T(128)}, s32[128]{0:T(128)}, u32[]{:S(2)}, u32[]{:S(2)}) collective-permute-start(s32[128]{0:T(128)} %bitcast.209), channel_id=1, source_target_pairs={{0,2},{1,3},{2,0},{3,1},{4,6},{5,7},{6,4},{7,5},{8,10},{9,11},{10,... | collective-permute-start | bytes 1544 | tf_op jit(solution)/shard_map/ppermute | solution.py:14
  7.6 87.9 %collective-permute-start = (f32[34,32,128]{2,1,0:T(8,128)}, f32[34,32,128]{2,1,0:T(8,128)S(1)}, u32[]{:S(2)}, u32[]{:S(2)}) collective-permute-start(f32[34,32,128]{2,1,0:T(8,128)} %get-tuple-element.18), channel_id=1, source_target_pairs={{0,1},{1,0},{2,3},{3,2},{4,5},{5,4},{6,7},{7,6},{8,9},{9,8},{10,11... | collective-permute-start | bytes 1671176 | tf_op jit(solution)/shard_map/ppermute | solution.py:14
  9.2 86.3 %collective-permute-start.1 = (f32[34,32,128]{2,1,0:T(8,128)}, f32[34,32,128]{2,1,0:T(8,128)S(1)}, u32[]{:S(2)}, u32[]{:S(2)}) collective-permute-start(f32[34,32,128]{2,1,0:T(8,128)} %get-tuple-element.19), channel_id=1, source_target_pairs={{0,2},{1,3},{2,0},{3,1},{4,6},{5,7},{6,4},{7,5},{8,10},{9,11},{10,... | collective-permute-start | bytes 1671176 | tf_op jit(solution)/shard_map/ppermute | solution.py:14
  9.5 86.0 %collective-permute-start.2 = (f32[34,32,128]{2,1,0:T(8,128)}, f32[34,32,128]{2,1,0:T(8,128)}, u32[]{:S(2)}, u32[]{:S(2)}) collective-permute-start(f32[34,32,128]{2,1,0:T(8,128)} %get-tuple-element.20), channel_id=1, source_target_pairs={{0,3},{1,2},{2,1},{3,0},{4,7},{5,6},{6,5},{7,4},{8,11},{9,10},{10,... | collective-permute-start | bytes 1671176 | tf_op jit(solution)/shard_map/ppermute | solution.py:14
  20.9 51.7 %copy-start.7 = (f32[64,64]{0,1:T(8,128)S(1)}, f32[64,64]{0,1:T(8,128)}, u32[]{:S(2)}) copy-start(f32[64,64]{0,1:T(8,128)} %get-tuple-element.90) | copy-start | bytes 49156
  22.4 61.1 %copy-start.10 = (s32[4]{0:T(128)S(1)}, s32[4]{0:T(128)}, u32[]{:S(2)}) copy-start(s32[4]{0:T(128)} %fusion.35) | copy-start | bytes 52
  26.2 58.0 %copy-start.14 = (pred[4]{0:T(512)(128)(4,1)S(1)}, pred[4]{0:T(512)(128)(4,1)}, u32[]{:S(2)}) copy-start(pred[4]{0:T(512)(128)(4,1)} %get-tuple-element.111) | copy-start | bytes 16
  26.2 58.0 %copy-start.15 = (pred[4]{0:T(512)(128)(4,1)S(1)}, pred[4]{0:T(512)(128)(4,1)}, u32[]{:S(2)}) copy-start(pred[4]{0:T(512)(128)(4,1)} %get-tuple-element.112) | copy-start | bytes 16
  28.3 32.8 %collective-permute-start.4 = (f32[101,128]{1,0:T(8,128)}, f32[101,128]{1,0:T(8,128)S(1)}, u32[]{:S(2)}, u32[]{:S(2)}) collective-permute-start(f32[101,128]{1,0:T(8,128)} %pad_maximum_fusion.9), channel_id=1, source_target_pairs={{0,2},{1,3},{2,0},{3,1},{4,6},{5,7},{6,4},{7,5},{8,10},{9,11},{10,... | collective-permute-start | bytes 155144 | tf_op jit(solution)/shard_map/ppermute | solution.py:14
  35.8 34.6 %collective-permute-start.8 = (f32[4,32,128]{2,1,0:T(8,128)S(1)}, f32[4,32,128]{2,1,0:T(8,128)S(1)}, u32[]{:S(2)}, u32[]{:S(2)}) collective-permute-start(f32[4,32,128]{2,1,0:T(8,128)S(1)} %get-tuple-element.88), channel_id=1, source_target_pairs={{0,3},{1,2},{2,1},{3,0},{4,7},{5,6},{6,5},{7,4},{8,11},{9,10},{10,... | collective-permute-start | bytes 196616 | tf_op jit(solution)/shard_map/ppermute | solution.py:14
  61.1 5.7 %collective-permute-start.7 = (f32[4,32,128]{2,1,0:T(8,128)S(1)}, f32[4,32,128]{2,1,0:T(8,128)S(1)}, u32[]{:S(2)}, u32[]{:S(2)}) collective-permute-start(f32[4,32,128]{2,1,0:T(8,128)S(1)} %get-tuple-element.88), channel_id=1, source_target_pairs={{0,2},{1,3},{2,0},{3,1},{4,6},{5,7},{6,4},{7,5},{8,10},{9,11},{10,... | collective-permute-start | bytes 196616 | tf_op jit(solution)/shard_map/ppermute | solution.py:14
  66.8 5.8 %collective-permute-start.6 = (f32[4,32,128]{2,1,0:T(8,128)S(1)}, f32[4,32,128]{2,1,0:T(8,128)S(1)}, u32[]{:S(2)}, u32[]{:S(2)}) collective-permute-start(f32[4,32,128]{2,1,0:T(8,128)S(1)} %get-tuple-element.89), channel_id=1, source_target_pairs={{0,1},{1,0},{2,3},{3,2},{4,5},{5,4},{6,7},{7,6},{8,9},{9,8},{10,11... | collective-permute-start | bytes 196616 | tf_op jit(solution)/shard_map/ppermute | solution.py:14
  85.5 5.0 %collective-permute-start.11 = (f32[2,32,128]{2,1,0:T(8,128)S(1)}, f32[2,32,128]{2,1,0:T(8,128)S(1)}, u32[]{:S(2)}, u32[]{:S(2)}) collective-permute-start(f32[2,32,128]{2,1,0:T(8,128)S(1)} %get-tuple-element.55), channel_id=1, source_target_pairs={{0,3},{1,2},{2,1},{3,0},{4,7},{5,6},{6,5},{7,4},{8,11},{9,10},{10,... | collective-permute-start | bytes 98312 | tf_op jit(solution)/shard_map/ppermute | solution.py:14
  87.0 6.7 %collective-permute-start.10 = (f32[2,32,128]{2,1,0:T(8,128)S(1)}, f32[2,32,128]{2,1,0:T(8,128)S(1)}, u32[]{:S(2)}, u32[]{:S(2)}) collective-permute-start(f32[2,32,128]{2,1,0:T(8,128)S(1)} %get-tuple-element.56), channel_id=1, source_target_pairs={{0,2},{1,3},{2,0},{3,1},{4,6},{5,7},{6,4},{7,5},{8,10},{9,11},{10,... | collective-permute-start | bytes 98312 | tf_op jit(solution)/shard_map/ppermute | solution.py:14
  90.5 5.0 %collective-permute-start.9 = (f32[2,32,128]{2,1,0:T(8,128)S(1)}, f32[2,32,128]{2,1,0:T(8,128)S(1)}, u32[]{:S(2)}, u32[]{:S(2)}) collective-permute-start(f32[2,32,128]{2,1,0:T(8,128)S(1)} %get-tuple-element.57), channel_id=1, source_target_pairs={{0,1},{1,0},{2,3},{3,2},{4,5},{5,4},{6,7},{7,6},{8,9},{9,8},{10,11... | collective-permute-start | bytes 98312 | tf_op jit(solution)/shard_map/ppermute | solution.py:14
  96.6 42.6 %copy-start.16 = (f32[128]{0:T(128)S(1)}, f32[128]{0:T(128)}, u32[]{:S(2)}) copy-start(f32[128]{0:T(128)} %get-tuple-element.31) | copy-start | bytes 1540
  96.6 42.6 %copy-start.17 = (f32[128]{0:T(128)S(1)}, f32[128]{0:T(128)}, u32[]{:S(2)}) copy-start(f32[128]{0:T(128)} %get-tuple-element.32) | copy-start | bytes 1540
  118.8 6.5 %collective-permute-start.15 = (f32[3,32,128]{2,1,0:T(8,128)}, f32[3,32,128]{2,1,0:T(8,128)S(1)}, u32[]{:S(2)}, u32[]{:S(2)}) collective-permute-start(f32[3,32,128]{2,1,0:T(8,128)} %get-tuple-element.26), channel_id=1, source_target_pairs={{0,1},{1,0},{2,3},{3,2},{4,5},{5,4},{6,7},{7,6},{8,9},{9,8},{10,11... | collective-permute-start | bytes 147464 | tf_op jit(solution)/shard_map/ppermute | solution.py:14
  120.8 6.0 %collective-permute-start.16 = (f32[3,32,128]{2,1,0:T(8,128)}, f32[3,32,128]{2,1,0:T(8,128)S(1)}, u32[]{:S(2)}, u32[]{:S(2)}) collective-permute-start(f32[3,32,128]{2,1,0:T(8,128)} %get-tuple-element.27), channel_id=1, source_target_pairs={{0,2},{1,3},{2,0},{3,1},{4,6},{5,7},{6,4},{7,5},{8,10},{9,11},{10,... | collective-permute-start | bytes 147464 | tf_op jit(solution)/shard_map/ppermute | solution.py:14
  120.9 6.0 %collective-permute-start.17 = (f32[3,32,128]{2,1,0:T(8,128)}, f32[3,32,128]{2,1,0:T(8,128)S(1)}, u32[]{:S(2)}, u32[]{:S(2)}) collective-permute-start(f32[3,32,128]{2,1,0:T(8,128)} %get-tuple-element.28), channel_id=1, source_target_pairs={{0,3},{1,2},{2,1},{3,0},{4,7},{5,6},{6,5},{7,4},{8,11},{9,10},{10,... | collective-permute-start | bytes 147464 | tf_op jit(solution)/shard_map/ppermute | solution.py:14
  122.4 23.9 %collective-permute-start.12 = (f32[32,32,128]{2,1,0:T(8,128)}, f32[32,32,128]{2,1,0:T(8,128)S(1)}, u32[]{:S(2)}, u32[]{:S(2)}) collective-permute-start(f32[32,32,128]{2,1,0:T(8,128)} %get-tuple-element.22), channel_id=1, source_target_pairs={{0,1},{1,0},{2,3},{3,2},{4,5},{5,4},{6,7},{7,6},{8,9},{9,8},{10,11... | collective-permute-start | bytes 1572872 | tf_op jit(solution)/shard_map/ppermute | solution.py:14
  125.3 35.4 %collective-permute-start.13 = (f32[32,32,128]{2,1,0:T(8,128)}, f32[32,32,128]{2,1,0:T(8,128)S(1)}, u32[]{:S(2)}, u32[]{:S(2)}) collective-permute-start(f32[32,32,128]{2,1,0:T(8,128)} %get-tuple-element.23), channel_id=1, source_target_pairs={{0,2},{1,3},{2,0},{3,1},{4,6},{5,7},{6,4},{7,5},{8,10},{9,11},{10,... | collective-permute-start | bytes 1572872 | tf_op jit(solution)/shard_map/ppermute | solution.py:14
  125.3 45.9 %collective-permute-start.14 = (f32[32,32,128]{2,1,0:T(8,128)}, f32[32,32,128]{2,1,0:T(8,128)S(1)}, u32[]{:S(2)}, u32[]{:S(2)}) collective-permute-start(f32[32,32,128]{2,1,0:T(8,128)} %get-tuple-element.24), channel_id=1, source_target_pairs={{0,3},{1,2},{2,1},{3,0},{4,7},{5,6},{6,5},{7,4},{8,11},{9,10},{10,... | collective-permute-start | bytes 1572872 | tf_op jit(solution)/shard_map/ppermute | solution.py:14
  (24 other events, 470.8 us)

commit v2 on v0

v2 whole, which is shorter than its diff:
```python
import jax
import jax.numpy as jnp
from jax import lax
from jax.experimental import pallas as pl
from jax.experimental.pallas import tpu as pltpu
from jax.sharding import PartitionSpec as P

Z = ("sect", "lev")
PARTS = 4
HIGHEST = lax.Precision.HIGHEST
SMEM = pl.BlockSpec(memory_space=pltpu.SMEM)
VMEM = pl.BlockSpec(memory_space=pltpu.VMEM)


def traded(blocks):
    return lax.all_to_all(blocks, Z, 0, 0)


def exchanged(block, bits):
    return lax.ppermute(block, Z, [(at, at ^ bits) for at in range(PARTS)])


def all_exchanged(blocks):
    return [blocks[0]] + [exchanged(blocks[bits], bits) for bits in range(1, PARTS)]


def split_kernel(place, lent_rows, field, gain, p0, p1, p2, p3, borders, turned):
    levels, rows, cols = field.shape
    width = cols // PARTS
    turned[0] = jnp.zeros((levels, rows), jnp.float32)
    turned[cols + 1] = jnp.zeros((levels, rows), jnp.float32)
    flat = turned.reshape((cols + 2) * levels, rows)
    for level in range(levels):
        flat[pl.ds(levels + level, cols, stride=levels), :] = field[level].T
    for bits, part in enumerate((p0, p1, p2, p3)):
        part[...] = turned[pl.ds((place[0] ^ bits) * width, width + 2)]
    component = place[0] // 2
    for at in range(PARTS):
        lent = component != at // 2
        for slot, fixed in enumerate((0, rows - 1)):
            row = jnp.where(lent, lent_rows[fixed], fixed)
            borders[at, slot * levels : (slot + 1) * levels, :] = field[:, pl.ds(row, 1), :].reshape(levels, cols)
        borders[at, 2 * levels : 3 * levels, :] = turned[1]
        borders[at, 3 * levels : 4 * levels, :] = turned[cols]
        borders[at, 4 * levels :, :] = gain[...]


def split_columns(place, lent_rows, field, gain):
    levels, rows, cols = field.shape
    part = jax.ShapeDtypeStruct((cols // PARTS + 2, levels, rows), jnp.float32)
    *parts, borders = pl.pallas_call(
        split_kernel,
        out_shape=[part] * PARTS + [jax.ShapeDtypeStruct((PARTS, 4 * levels + 1, rows), jnp.float32)],
        in_specs=[SMEM, SMEM, VMEM, VMEM],
        out_specs=[VMEM] * (PARTS + 1),
        scratch_shapes=[pltpu.VMEM((cols + 2, levels, rows), jnp.float32)],
        name="split_columns",
    )(place, lent_rows, field, gain)
    return parts, borders


def join_kernel(place, p0, p1, p2, p3, sides, top_bottom, out, turned):
    levels, rows, cols = out.shape
    width = cols // PARTS
    for bits, part in enumerate((p0, p1, p2, p3)):
        turned[pl.ds((place[0] ^ bits) * width, width)] = part[...]
    for part in range(PARTS):
        for side in range(2):
            at = part * width + side * (width - 1)
            turned[at] = turned[at] + sides[part, side]
    flat = turned.reshape(cols * levels, rows)
    row = lax.broadcasted_iota(jnp.int32, (rows, cols), 0)
    for level in range(levels):
        plane = flat[pl.ds(level, cols, stride=levels), :].T
        top = top_bottom[0, level : level + 1, :]
        bottom = top_bottom[1, level : level + 1, :]
        out[level] = plane + jnp.where(row == 0, top, jnp.where(row == rows - 1, bottom, 0.0))


def join_columns(place, parts, sides, top_bottom):
    width, levels, rows = parts[0].shape
    cols = width * PARTS
    return pl.pallas_call(
        join_kernel,
        out_shape=jax.ShapeDtypeStruct((levels, rows, cols), jnp.float32),
        in_specs=[SMEM] + [VMEM] * 6,
        out_specs=VMEM,
        scratch_shapes=[pltpu.VMEM((cols, levels, rows), jnp.float32)],
        name="join_columns",
    )(place, *parts, sides, top_bottom)


def halves(value):
    high = value.astype(jnp.bfloat16)
    low = (value - high.astype(jnp.float32)).astype(jnp.bfloat16)
    return high, low


def picked(value, index):
    return jnp.take_along_axis(value, index, axis=1, mode="promise_in_bounds")


def steps_kernel(
    place, p0, p1, p2, p3, weights, gains, rows_from, wet, spread, halos,
    o0, o1, o2, o3, edges, column, state,
):
    parts, outs = (p0, p1, p2, p3), (o0, o1, o2, o3)
    wide, half, rows = p0.shape
    spot = place[0]
    component, swap = spot // 2, spot % 2
    comps = [component, 1 - component]
    width = wide - 2
    levels = 2 * half
    at_once, few = 16, 8
    lane = lax.broadcasted_iota(jnp.int32, (levels, rows), 1)
    mixes, picks = [], []
    for comp in range(2):
        mix = weights[comps[comp]]
        turned = jnp.concatenate([mix[half:], mix[:half]], axis=0)
        turned = jnp.concatenate([turned[:, half:], turned[:, :half]], axis=1)
        high, low = halves(jnp.where(swap == 0, mix, turned))
        mixes.append(jnp.concatenate([high, low, high], axis=1))
        picks.append(jnp.broadcast_to(rows_from[pl.ds(comps[comp], 1), :], (levels, rows)))

    def joined(blocks, comp, *at):
        return jnp.concatenate(
            [blocks[(spot ^ (2 * comp + part),) + at] for part in range(2)], axis=0
        )

    gain = [joined(gains, comp) for comp in range(2)]

    def solve(load, first, store, count):
        for comp in range(2):
            rights = []
            for at in range(count):
                coupled = load(comp, first + at)
                coupled = coupled + gain[comp] * picked(load(1 - comp, first + at), picks[comp])
                high, low = halves(coupled)
                rights.append(jnp.concatenate([high, high, low], axis=0))
            for at in range(0, count, 2):
                pair = jnp.concatenate(rights[at : at + 2], axis=1)
                solved = jnp.dot(mixes[comp], pair, preferred_element_type=jnp.float32)
                for side in range(2):
                    column[comp, store + at + side] = solved[:, side * rows : (side + 1) * rows]

    def flux(comp, at):
        return column[comp, at] * spread[comps[comp], pl.ds(at, 1), :]

    def lap(around, ends):
        mid = around[1]
        above = jnp.where(lane == 0, ends, pltpu.roll(mid, 1, 1))
        below = jnp.where(lane == rows - 1, ends, pltpu.roll(mid, rows - 1, 1))
        return above + below + around[0] + around[2] - 4.0 * mid

    def arrived(comp, at):
        return jnp.concatenate([parts[2 * comp][at], parts[2 * comp + 1][at]], axis=0)

    def first_solve(step, carry):
        solve(arrived, step * at_once, step * at_once, at_once)
        return carry

    whole, rest = divmod(wide, at_once)
    lax.fori_loop(0, whole, first_solve, 0)
    if rest:
        solve(arrived, whole * at_once, whole * at_once, rest)
    tops = [joined(halos, comp, 1) for comp in range(2)]
    outer = []
    for comp in range(2):
        across = joined(halos, comp, 0)
        outer.append(
            (
                jnp.where(place[0] == 0, across, flux(comp, 0)),
                jnp.where(place[0] == PARTS - 1, across, flux(comp, width + 1)),
            )
        )

    def spread_first(first, left, right):
        for comp in range(2):
            fluxes = [flux(comp, first + at) for at in range(few + 2)]
            if left:
                fluxes[0] = outer[comp][0]
            if right:
                fluxes[-1] = outer[comp][1]
            for at in range(few):
                j = first + at
                ends = picked(tops[comp], jnp.where(lane == 0, j, j + width))
                total = column[comp, j + 1] + lap(fluxes[at : at + 3], ends)
                state[comp, j] = wet[comps[comp], pl.ds(j + 1, 1), :] * total

    for first in range(0, width, few):
        spread_first(first, first == 0, first + few == width)

    def held(comp, at):
        return state[comp, at]

    def second_solve(step, carry):
        solve(held, step * at_once, step * at_once + 1, at_once)
        return carry

    lax.fori_loop(0, width // at_once, second_solve, 0)
    for comp in range(2):
        column[comp, 0] = jnp.zeros((levels, rows), jnp.float32)
        column[comp, width + 1] = jnp.zeros((levels, rows), jnp.float32)

    def second_spread(step, carry):
        kept = []
        for comp in range(2):
            first = step * few
            fluxes = [flux(comp, first + at) for at in range(few + 2)]
            both = carry[comp]
            for at in range(few):
                j = first + at
                total = column[comp, j + 1] + lap(fluxes[at : at + 3], 0.0)
                done = wet[comps[comp], pl.ds(j + 1, 1), :] * total
                outs[2 * comp][j] = done[:half]
                outs[2 * comp + 1][j] = done[half:]
                ends = picked(fluxes[at + 1], jnp.where(lane == j, 0, rows - 1))
                both = jnp.where((lane == j) | (lane == j + width), ends, both)
            kept.append(both)
        return tuple(kept)

    empty = jnp.zeros((levels, rows), jnp.float32)
    both = lax.fori_loop(0, width // few, second_spread, (empty, empty))
    for comp in range(2):
        for slot, value in enumerate((flux(comp, 1), flux(comp, width), both[comp])):
            edges[spot ^ (2 * comp), slot] = value[:half]
            edges[spot ^ (2 * comp + 1), slot] = value[half:]


def two_steps(place, parts, weights, gains, rows_from, wet, spread, halos):
    wide, half, rows = parts[0].shape
    width = wide - 2
    part = jax.ShapeDtypeStruct((width, half, rows), jnp.float32)
    *results, edges = pl.pallas_call(
        steps_kernel,
        out_shape=[part] * PARTS + [jax.ShapeDtypeStruct((PARTS, 3, half, rows), jnp.float32)],
        in_specs=[SMEM] + [VMEM] * 10,
        out_specs=[VMEM] * (PARTS + 1),
        scratch_shapes=[
            pltpu.VMEM((2, wide, 2 * half, rows), jnp.float32),
            pltpu.VMEM((2, width, 2 * half, rows), jnp.float32),
        ],
        name="two_steps",
    )(place, *parts, weights, gains, rows_from, wet, spread, halos)
    return results, edges


def tile_halo(edges, nbr_tile, nbr_side, nbr_flip):
    every = lax.all_gather(edges, "tile", axis=0)
    found = every[jnp.maximum(nbr_tile, 0), nbr_side]
    turned = jnp.where((nbr_flip == 1)[:, None, None], found[..., ::-1], found)
    return jnp.where((nbr_tile >= 0)[:, None, None], turned, jnp.float32(0.0))


def on_device(
    adjoint, diffusion, wet_mask, remap, coupling, vert_inverse, nbr_tile, nbr_side, nbr_flip
):
    field = adjoint[0, 0]
    half, rows, cols = field.shape
    width = cols // PARTS
    component, level_at = lax.axis_index("sect"), lax.axis_index("lev")
    spot = component * 2 + level_at
    place = spot[None].astype(jnp.int32)
    wet = wet_mask[0, 0].astype(jnp.float32)
    spread = wet * diffusion[0, 0]
    near = (nbr_tile[0], nbr_side[0], nbr_flip[0])
    inverse = vert_inverse[0, 0]
    my_rows = remap[0, 0]

    def both(mine, other):
        return jnp.where(component == 0, jnp.stack([mine, other]), jnp.stack([other, mine]))

    other_rows = exchanged(my_rows, 2)

    def padded(plane):
        return jnp.pad(plane.T, ((1, 1), (0, 0)))

    wet_cols, spread_cols = padded(wet), padded(spread)

    def cut(plane, part):
        return lax.dynamic_slice_in_dim(plane, part * width, width + 2, 0)

    def packed(part):
        return jnp.concatenate([cut(wet_cols, part), cut(spread_cols, part), inverse.reshape(-1, rows)])

    packs = both(packed(spot), exchanged(packed(spot ^ 2), 2))
    tall = width + 2
    both_wet, both_spread = packs[:, :tall], packs[:, tall : 2 * tall]
    weights = packs[:, 2 * tall :].reshape((2,) + inverse.shape).transpose(0, 2, 1)
    rows_from = both(my_rows, other_rows)

    gain = jnp.pad(coupling, ((0, 0), (0, rows - half)))
    parts, borders = split_columns(place, other_rows, field, gain)
    borders = traded(borders)
    parts = all_exchanged(parts)

    gains = borders[:, -1, :half].reshape(2, 2 * half)
    borders = borders[:, :-1].reshape(2, 2, 4, half, rows)
    borders = borders.transpose(0, 2, 1, 3, 4).reshape(2, 4, 2 * half, rows)
    own, pulled = [jnp.where(component == comp, borders[0], borders[1]) for comp in range(2)]
    my_gain = jnp.where(component == 0, gains[0], gains[1])
    choose = (jnp.arange(rows)[:, None] == my_rows[None, :]).astype(jnp.float32)
    pulled_columns = jnp.einsum("slq,qr->slr", pulled[2:], choose, precision=HIGHEST)
    coupled = own + my_gain[None, :, None] * jnp.concatenate([pulled[:2], pulled_columns])
    mine = lax.dynamic_slice_in_dim(inverse, level_at * half, half, 1)
    solved = jnp.einsum("kl,skx->slx", mine, coupled, precision=HIGHEST)

    def border(plane):
        return jnp.stack([plane[0], plane[rows - 1], plane[:, 0], plane[:, cols - 1]])[:, None, :]

    halo = tile_halo(solved * border(spread), *near)
    blocks = []
    for part in range(PARTS):
        span = slice(part * width, (part + 1) * width)
        ends = jnp.concatenate([halo[0][:, span], halo[1][:, span]], axis=1)
        ends = jnp.pad(ends, ((0, 0), (0, rows - 2 * width)))
        blocks.append(jnp.stack([halo[2] if part == 0 else halo[3], ends]))
    halos = traded(jnp.stack(blocks))

    gains = jnp.broadcast_to(gains.reshape(PARTS, half, 1), (PARTS, half, rows))
    results, edges = two_steps(
        place, parts, weights, gains, rows_from, both_wet, both_spread, halos
    )

    edges = traded(edges)
    results = all_exchanged(results)
    top = jnp.concatenate([edges[part, 2, :, :width] for part in range(PARTS)], axis=1)
    bottom = jnp.concatenate([edges[part, 2, :, width : 2 * width] for part in range(PARTS)], axis=1)
    halo = tile_halo(jnp.stack([top, bottom, edges[0, 0], edges[PARTS - 1, 1]]), *near)
    sides = []
    for part in range(PARTS):
        left = halo[2] if part == 0 else edges[part - 1, 1]
        right = halo[3] if part == PARTS - 1 else edges[part + 1, 0]
        sides.append(
            jnp.stack([left * wet[:, part * width], right * wet[:, (part + 1) * width - 1]])
        )
    top_bottom = jnp.stack([halo[0] * wet[0], halo[1] * wet[rows - 1]])
    return join_columns(place, results, jnp.stack(sides), top_bottom)[None, None]


def solution(mesh):
    in_specs = (
        P("sect", "tile", "lev", None, None),
        P("sect", "tile", None, None),
        P("sect", "tile", None, None),
        P("sect", "tile", None),
        P("sect", "lev"),
        P("sect", "tile", None, None),
        P("tile", None),
        P("tile", None),
        P("tile", None),
    )
    out_specs = P("sect", "tile", "lev", None, None)
    return jax.shard_map(
        on_device, mesh=mesh, in_specs=in_specs, out_specs=out_specs, check_vma=False
    )
```

time: 406 us -> 147 us (0.36)
  waiting for transfers between devices: 294 us -> 68.3 us
  local copies, waits for them, and re-layouts: 43.3 us -> 9.45 us
  starting transfers between devices: 5.11 us -> 25.1 us
  Pallas kernels: 0 us -> 18.3 us
  other arithmetic: 19.3 us -> 4.8 us
  between operations: 13.6 us -> 0.3 us
  matrix products: 8.01 us -> 0.51 us
    ppermute x2 -> x8, waiting for transfers between devices: 180 us -> 61.4 us  [exchanged(): return lax.ppermute(block, Z, [(at, at ^ bits) for at in range(PARTS)])]
    all_gather x2 -> x0, waiting for transfers between devices: 114 us -> none  [on_device(): whole = lax.all_gather(coupled, 'lev', axis=1, tiled=True)]
    slice x10 -> x13, local copies, waits for them, and re-layouts: 27 us -> 1.25 us  [the longest x1 0.65 us: on_device(): both_wet, both_spread = (packs[:, :tall], packs[:, tall:2 * tall])]
    pallas_call x0 -> x3, Pallas kernels: none -> 18.3 us  [the longest x1 9.36 us: two_steps(): pl.pallas_call(steps_kernel, out_shape=[part] * PARTS + [jax.ShapeDtypeSt...]
    all_to_all x0 -> x3, starting transfers between devices: none -> 15 us  [traded(): return lax.all_to_all(blocks, Z, 0, 0)]
    add x2 -> x1, other arithmetic: 7.71 us -> 0.08 us  [on_device(): own + my_gain[None, :, None] * jnp.concatenate([pulled[:2], pulled_columns])]
    dot_general x2, matrix products: 8.01 us -> 0.51 us  [the longest x1 0.33 us: on_device(): solved = jnp.einsum('kl,skx->slx', mine, coupled, precision=HIGHEST)]
    gather x5 -> x2, local copies, waits for them, and re-layouts: 8.32 us -> 1.12 us  [tile_halo(): found = every[jnp.maximum(nbr_tile, 0), nbr_side]]
  transfers between devices with their start and end apart: 4 -> 11, of which waited for: 4 -> 9; matrix products, arithmetic and copies ran while one was open for 0% -> 9% of each run, Pallas kernels for 0% -> 3%
where the time goes in v2:
time: 147 us; the launch traced here: 146 us
  waiting for transfers between devices  68.3 us (46%)
  starting transfers between devices  25.1 us (17%)
  blocking collectives  19.7 us (13%)
  Pallas kernels  18.3 us (12%)
  local copies, waits for them, and re-layouts  9.45 us (6%)
  other arithmetic  4.8 us (3%)
    ppermute x8, waiting for transfers between devices, exchanged(): return lax.ppermute(block, Z, [(at, at ^ bits) for at in range(PARTS)])  61.4 us
    all_gather x2, blocking collectives, tile_halo(): every = lax.all_gather(edges, 'tile', axis=0)  19.7 us
    all_to_all x3, starting transfers between devices, traded(): return lax.all_to_all(blocks, Z, 0, 0)  15 us
    ppermute x8, starting transfers between devices, exchanged(): return lax.ppermute(block, Z, [(at, at ^ bits) for at in range(PARTS)])  10.1 us
    pallas_call x1, Pallas kernels, two_steps(): pl.pallas_call(steps_kernel, out_shape=[part] * PARTS + [jax.ShapeDtypeSt...  9.36 us
    all_to_all x3, waiting for transfers between devices, traded(): return lax.all_to_all(blocks, Z, 0, 0)  6.97 us
    pallas_call x1, Pallas kernels, split_columns(): pl.pallas_call(split_kernel, out_shape=[part] * PARTS + [jax.ShapeDtypeSt...  4.62 us
    pallas_call x1, Pallas kernels, join_columns(): pl.pallas_call(join_kernel, out_shape=jax.ShapeDtypeStruct((levels, rows,...  4.28 us
  transfers between devices with their start and end apart: 11, of which 9 were waited for; matrix products, arithmetic and copies ran while one was open for 9% of the time, Pallas kernels for 3%

profile of v2, /device:TPU:8, one launch (start us, length us, event | category | flops | bytes accessed | tf_op | source)
XLA Modules:
  0.0 146.5 jit_solution(18334154802052140726)
XLA Ops:
  0.0 2.6 %collective-permute-start = (s32[128]{0:T(128)}, s32[128]{0:T(128)S(1)}, u32[]{:S(2)}, u32[]{:S(2)}) collective-permute-start(s32[128]{0:T(128)} %bitcast.167), channel_id=1, source_target_pairs={{0,2},{1,3},{2,0},{3,1},{4,6},{5,7},{6,4},{7,5},{8,10},{9,11},{10,... | collective-permute-start | bytes 1544 | tf_op jit(solution)/shard_map/ppermute | solution.py:20
  2.6 0.8 reshape_squeeze.2
  3.4 1.0 copy.30
  4.4 0.9 copy.31
  6.8 1.2 pad.24.gain
  8.6 4.6 %split_columns.1 = (f32[34,32,128]{2,1,0:T(8,128)}, f32[34,32,128]{2,1,0:T(8,128)}, f32[34,32,128]{2,1,0:T(8,128)}, f32[34,32,128]{2,1,0:T(8,128)}, f32[4,129,128]{2,1,0:T(8,128)}) custom-call(s32[1]{0:T(128)} %bitcast.place, s32[128]{0:T(128)} %copy-done.9, f32[32,128,128]{2,1,0:T(8,128)} %bitcast.156, f32[1,128]{1,0:T(1,128)} %pad.24.gain), custom_call_target="tpu_custom_call" | custom-call | tf_op jit(solution)/shard_map/split_columns/pallas_call | solution.py:51
  13.2 5.4 %all-to-all-start = ((f32[4,129,128]{2,1,0:T(8,128)}), f32[4,129,128]{2,1,0:T(8,128)S(1)}, u32[]{:S(2)}, u32[]{:S(2)}) async-start(f32[4,129,128]{2,1,0:T(8,128)} %get-tuple-element.19), calls=%async_computation | async-start | bytes 557056 | tf_op jit(solution)/shard_map/all_to_all | solution.py:16
  18.7 2.9 %collective-permute-start.2 = (f32[34,32,128]{2,1,0:T(8,128)}, f32[34,32,128]{2,1,0:T(8,128)S(1)}, u32[]{:S(2)}, u32[]{:S(2)}) collective-permute-start(f32[34,32,128]{2,1,0:T(8,128)} %get-tuple-element.17), channel_id=1, source_target_pairs={{0,2},{1,3},{2,0},{3,1},{4,6},{5,7},{6,4},{7,5},{8,10},{9,11},{10,... | collective-permute-start | bytes 1671176 | tf_op jit(solution)/shard_map/ppermute | solution.py:20
  22.2 1.3 add_select_fusion.rows_from
  24.3 3.0 %all-to-all-done = f32[4,129,128]{2,1,0:T(8,128)S(1)} async-done(((f32[4,129,128]{2,1,0:T(8,128)}), f32[4,129,128]{2,1,0:T(8,128)S(1)}, u32[]{:S(2)}, u32[]{:S(2)}) %all-to-all-start) | async-done | bytes 264224 | tf_op jit(solution)/shard_map/all_to_all | solution.py:16
  28.0 9.9 %all-gather = f32[32,32,128]{2,1,0:T(8,128)S(1)} all-gather(f32[4,32,128]{2,1,0:T(8,128)S(1)} %fusion), channel_id=2, replica_groups=mesh['tile'=8,'sect'=2,'lev'=2] {'tile'}, dimensions={0}, use_global_device_ids=true | all-gather | bytes 589824 | tf_op jit(solution)/shard_map/all_gather | solution.py:249
  39.8 4.4 %all-to-all-start.1 = ((f32[4,2,32,128]{3,2,1,0:T(8,128)}), f32[4,2,32,128]{3,2,1,0:T(8,128)S(1)}, u32[]{:S(2)}, u32[]{:S(2)}) async-start(f32[4,2,32,128]{3,2,1,0:T(8,128)} %pad_maximum_fusion), calls=%async_computation.1 | async-start | bytes 262144 | tf_op jit(solution)/shard_map/all_to_all | solution.py:16
  44.9 1.0 collective-permute-done.1.p1
  45.9 16.2 %collective-permute-done.2.p2 = f32[34,32,128]{2,1,0:T(8,128)S(1)} collective-permute-done((f32[34,32,128]{2,1,0:T(8,128)}, f32[34,32,128]{2,1,0:T(8,128)S(1)}, u32[]{:S(2)}, u32[]{:S(2)}) %collective-permute-start.2) | collective-permute-done | bytes 557088 | tf_op jit(solution)/shard_map/ppermute | solution.py:20
  62.0 13.7 %collective-permute-done.3.p3 = f32[34,32,128]{2,1,0:T(8,128)S(1)} collective-permute-done((f32[34,32,128]{2,1,0:T(8,128)}, f32[34,32,128]{2,1,0:T(8,128)S(1)}, u32[]{:S(2)}, u32[]{:S(2)}) %collective-permute-start.3) | collective-permute-done | bytes 557088 | tf_op jit(solution)/shard_map/ppermute | solution.py:20
  76.8 9.4 %two_steps.1 = (f32[32,32,128]{2,1,0:T(8,128)}, f32[32,32,128]{2,1,0:T(8,128)}, f32[32,32,128]{2,1,0:T(8,128)}, f32[32,32,128]{2,1,0:T(8,128)}, f32[4,3,32,128]{3,2,1,0:T(8,128)}) custom-call(s32[1]{0:T(128)} %bitcast.place, f32[34,32,128]{2,1,0:T(8,128)} %get-tuple-element.15.p0, f32[34,32,128]{2,1,0:T(8,128)} %copy-done, f32[34,32,128]{2,1,0:T(8,128)} %copy-done.1, ...), custom_call_target="tpu_custom_call" | custom-call | tf_op jit(solution)/shard_map/two_steps/pallas_call | solution.py:234
  86.2 5.1 %all-to-all-start.2 = ((f32[4,3,32,128]{3,2,1,0:T(8,128)}), f32[4,3,32,128]{3,2,1,0:T(8,128)S(1)}, u32[]{:S(2)}, u32[]{:S(2)}) async-start(f32[4,3,32,128]{3,2,1,0:T(8,128)} %get-tuple-element.24), calls=%async_computation.2 | async-start | bytes 393216 | tf_op jit(solution)/shard_map/all_to_all | solution.py:16
  91.6 2.9 %collective-permute-start.6 = (f32[32,32,128]{2,1,0:T(8,128)}, f32[32,32,128]{2,1,0:T(8,128)S(1)}, u32[]{:S(2)}, u32[]{:S(2)}) collective-permute-start(f32[32,32,128]{2,1,0:T(8,128)} %get-tuple-element.22), channel_id=1, source_target_pairs={{0,2},{1,3},{2,0},{3,1},{4,6},{5,7},{6,4},{7,5},{8,10},{9,11},{10,... | collective-permute-start | bytes 1572872 | tf_op jit(solution)/shard_map/ppermute | solution.py:20
  95.1 3.6 %all-to-all-done.2 = f32[4,3,32,128]{3,2,1,0:T(8,128)S(1)} async-done(((f32[4,3,32,128]{3,2,1,0:T(8,128)}), f32[4,3,32,128]{3,2,1,0:T(8,128)S(1)}, u32[]{:S(2)}, u32[]{:S(2)}) %all-to-all-start.2) | async-done | bytes 196640 | tf_op jit(solution)/shard_map/all_to_all | solution.py:16
  98.9 9.9 %all-gather.1 = f32[32,32,128]{2,1,0:T(8,128)S(1)} all-gather(f32[4,32,128]{2,1,0:T(8,128)S(1)} %pad_maximum_fusion.4), channel_id=3, replica_groups=mesh['tile'=8,'sect'=2,'lev'=2] {'tile'}, dimensions={0}, use_global_device_ids=true | all-gather | bytes 589824 | tf_op jit(solution)/shard_map/all_gather | solution.py:249
  110.9 4.3 %collective-permute-done.5.p1 = f32[32,32,128]{2,1,0:T(8,128)S(1)} collective-permute-done((f32[32,32,128]{2,1,0:T(8,128)}, f32[32,32,128]{2,1,0:T(8,128)S(1)}, u32[]{:S(2)}, u32[]{:S(2)}) %collective-permute-start.5) | collective-permute-done | bytes 524320 | tf_op jit(solution)/shard_map/ppermute | solution.py:20
  115.2 14.5 %collective-permute-done.6.p2 = f32[32,32,128]{2,1,0:T(8,128)S(1)} collective-permute-done((f32[32,32,128]{2,1,0:T(8,128)}, f32[32,32,128]{2,1,0:T(8,128)S(1)}, u32[]{:S(2)}, u32[]{:S(2)}) %collective-permute-start.6) | collective-permute-done | bytes 524320 | tf_op jit(solution)/shard_map/ppermute | solution.py:20
  129.7 11.8 %collective-permute-done.7.p3 = f32[32,32,128]{2,1,0:T(8,128)S(1)} collective-permute-done((f32[32,32,128]{2,1,0:T(8,128)}, f32[32,32,128]{2,1,0:T(8,128)S(1)}, u32[]{:S(2)}, u32[]{:S(2)}) %collective-permute-start.7) | collective-permute-done | bytes 524320 | tf_op jit(solution)/shard_map/ppermute | solution.py:20
  142.2 4.3 %join_columns.1 = f32[32,128,128]{2,1,0:T(8,128)} custom-call(s32[1]{0:T(128)} %bitcast.place, f32[32,32,128]{2,1,0:T(8,128)} %get-tuple-element.20.p0, f32[32,32,128]{2,1,0:T(8,128)} %copy-done.3, f32[32,32,128]{2,1,0:T(8,128)} %copy-done.4, f32[32,32,128]{2,1,0:T(8,128)} %copy-done.5, f32[4,2,32,128]{3,2,1,0:T(8,128)} %pad_maximum_fusion.1.sides, ...), custom_call_target="tpu_custom_call" | custom-call | tf_op jit(solution)/shard_map/join_columns/pallas_call | solution.py:83
  (90 shorter events, 11.6 us)
Async XLA Ops:
  0.0 8.0 %collective-permute-start = (s32[128]{0:T(128)}, s32[128]{0:T(128)S(1)}, u32[]{:S(2)}, u32[]{:S(2)}) collective-permute-start(s32[128]{0:T(128)} %bitcast.167), channel_id=1, source_target_pairs={{0,2},{1,3},{2,0},{3,1},{4,6},{5,7},{6,4},{7,5},{8,10},{9,11},{10,... | collective-permute-start | bytes 1544 | tf_op jit(solution)/shard_map/ppermute | solution.py:20
  3.4 15.2 %copy-start.10 = (s32[1,4]{1,0:T(1,128)S(1)}, s32[1,4]{1,0:T(1,128)}, u32[]{:S(2)}) copy-start(s32[1,4]{1,0:T(1,128)} %param.15) | copy-start | bytes 52
  3.4 15.2 %copy-start.11 = (s32[1,4]{1,0:T(1,128)S(1)}, s32[1,4]{1,0:T(1,128)}, u32[]{:S(2)}) copy-start(s32[1,4]{1,0:T(1,128)} %param.16) | copy-start | bytes 52
  3.4 18.8 %copy-start.8 = (s32[1,1,128]{2,1,0:T(1,128)S(1)}, s32[1,1,128]{2,1,0:T(1,128)}, u32[]{:S(2)}) copy-start(s32[1,1,128]{2,1,0:T(1,128)} %param.12) | copy-start | bytes 1540
  5.4 18.0 %collective-permute-start.4 = (f32[100,128]{1,0:T(8,128)S(1)}, f32[100,128]{1,0:T(8,128)S(1)}, u32[]{:S(2)}, u32[]{:S(2)}) collective-permute-start(f32[100,128]{1,0:T(8,128)S(1)} %get-tuple-element.86), channel_id=1, source_target_pairs={{0,2},{1,3},{2,0},{3,1},{4,6},{5,7},{6,4},{7,5},{8,10},{9,11},{10,... | collective-permute-start | bytes 153608 | tf_op jit(solution)/shard_map/ppermute | solution.py:20
  8.0 0.5 copy-start.9
  13.2 14.5 %copy-start.7 = (f32[1,1,64,64]{3,2,1,0:T(8,128)S(1)}, f32[1,1,64,64]{3,2,1,0:T(8,128)}, u32[]{:S(2)}) copy-start(f32[1,1,64,64]{3,2,1,0:T(8,128)} %param.14) | copy-start | bytes 49156
  13.2 14.1 %all-to-all-start = ((f32[4,129,128]{2,1,0:T(8,128)}), f32[4,129,128]{2,1,0:T(8,128)S(1)}, u32[]{:S(2)}, u32[]{:S(2)}) async-start(f32[4,129,128]{2,1,0:T(8,128)} %get-tuple-element.19), calls=%async_computation | async-start | bytes 557056 | tf_op jit(solution)/shard_map/all_to_all | solution.py:16
  18.6 27.2 %collective-permute-start.1 = (f32[34,32,128]{2,1,0:T(8,128)}, f32[34,32,128]{2,1,0:T(8,128)S(1)}, u32[]{:S(2)}, u32[]{:S(2)}) collective-permute-start(f32[34,32,128]{2,1,0:T(8,128)} %get-tuple-element.16), channel_id=1, source_target_pairs={{0,1},{1,0},{2,3},{3,2},{4,5},{5,4},{6,7},{7,6},{8,9},{9,8},{10,11... | collective-permute-start | bytes 1671176 | tf_op jit(solution)/shard_map/ppermute | solution.py:20
  18.7 43.3 %collective-permute-start.2 = (f32[34,32,128]{2,1,0:T(8,128)}, f32[34,32,128]{2,1,0:T(8,128)S(1)}, u32[]{:S(2)}, u32[]{:S(2)}) collective-permute-start(f32[34,32,128]{2,1,0:T(8,128)} %get-tuple-element.17), channel_id=1, source_target_pairs={{0,2},{1,3},{2,0},{3,1},{4,6},{5,7},{6,4},{7,5},{8,10},{9,11},{10,... | collective-permute-start | bytes 1671176 | tf_op jit(solution)/shard_map/ppermute | solution.py:20
  21.6 54.1 %collective-permute-start.3 = (f32[34,32,128]{2,1,0:T(8,128)}, f32[34,32,128]{2,1,0:T(8,128)S(1)}, u32[]{:S(2)}, u32[]{:S(2)}) collective-permute-start(f32[34,32,128]{2,1,0:T(8,128)} %get-tuple-element.18), channel_id=1, source_target_pairs={{0,3},{1,2},{2,1},{3,0},{4,7},{5,6},{6,5},{7,4},{8,11},{9,10},{10,... | collective-permute-start | bytes 1671176 | tf_op jit(solution)/shard_map/ppermute | solution.py:20
  39.8 36.3 %all-to-all-start.1 = ((f32[4,2,32,128]{3,2,1,0:T(8,128)}), f32[4,2,32,128]{3,2,1,0:T(8,128)S(1)}, u32[]{:S(2)}, u32[]{:S(2)}) async-start(f32[4,2,32,128]{3,2,1,0:T(8,128)} %pad_maximum_fusion), calls=%async_computation.1 | async-start | bytes 262144 | tf_op jit(solution)/shard_map/all_to_all | solution.py:16
  45.9 30.9 %copy-start = (f32[34,32,128]{2,1,0:T(8,128)}, f32[34,32,128]{2,1,0:T(8,128)S(1)}, u32[]{:S(2)}) copy-start(f32[34,32,128]{2,1,0:T(8,128)S(1)} %collective-permute-done.1.p1) | copy-start | bytes 1671172
  62.0 14.8 %copy-start.1 = (f32[34,32,128]{2,1,0:T(8,128)}, f32[34,32,128]{2,1,0:T(8,128)S(1)}, u32[]{:S(2)}) copy-start(f32[34,32,128]{2,1,0:T(8,128)S(1)} %collective-permute-done.2.p2) | copy-start | bytes 1671172
  75.7 1.1 copy-start.2
  76.1 0.7 copy-start.6
  86.2 12.5 %all-to-all-start.2 = ((f32[4,3,32,128]{3,2,1,0:T(8,128)}), f32[4,3,32,128]{3,2,1,0:T(8,128)S(1)}, u32[]{:S(2)}, u32[]{:S(2)}) async-start(f32[4,3,32,128]{3,2,1,0:T(8,128)} %get-tuple-element.24), calls=%async_computation.2 | async-start | bytes 393216 | tf_op jit(solution)/shard_map/all_to_all | solution.py:16
  91.5 23.7 %collective-permute-start.5 = (f32[32,32,128]{2,1,0:T(8,128)}, f32[32,32,128]{2,1,0:T(8,128)S(1)}, u32[]{:S(2)}, u32[]{:S(2)}) collective-permute-start(f32[32,32,128]{2,1,0:T(8,128)} %get-tuple-element.21), channel_id=1, source_target_pairs={{0,1},{1,0},{2,3},{3,2},{4,5},{5,4},{6,7},{7,6},{8,9},{9,8},{10,11... | collective-permute-start | bytes 1572872 | tf_op jit(solution)/shard_map/ppermute | solution.py:20
  91.6 38.0 %collective-permute-start.6 = (f32[32,32,128]{2,1,0:T(8,128)}, f32[32,32,128]{2,1,0:T(8,128)S(1)}, u32[]{:S(2)}, u32[]{:S(2)}) collective-permute-start(f32[32,32,128]{2,1,0:T(8,128)} %get-tuple-element.22), channel_id=1, source_target_pairs={{0,2},{1,3},{2,0},{3,1},{4,6},{5,7},{6,4},{7,5},{8,10},{9,11},{10,... | collective-permute-start | bytes 1572872 | tf_op jit(solution)/shard_map/ppermute | solution.py:20
  94.5 46.9 %collective-permute-start.7 = (f32[32,32,128]{2,1,0:T(8,128)}, f32[32,32,128]{2,1,0:T(8,128)S(1)}, u32[]{:S(2)}, u32[]{:S(2)}) collective-permute-start(f32[32,32,128]{2,1,0:T(8,128)} %get-tuple-element.23), channel_id=1, source_target_pairs={{0,3},{1,2},{2,1},{3,0},{4,7},{5,6},{6,5},{7,4},{8,11},{9,10},{10,... | collective-permute-start | bytes 1572872 | tf_op jit(solution)/shard_map/ppermute | solution.py:20
  115.2 26.2 %copy-start.3 = (f32[32,32,128]{2,1,0:T(8,128)}, f32[32,32,128]{2,1,0:T(8,128)S(1)}, u32[]{:S(2)}) copy-start(f32[32,32,128]{2,1,0:T(8,128)S(1)} %collective-permute-done.5.p1) | copy-start | bytes 1572868
  129.7 11.8 %copy-start.4 = (f32[32,32,128]{2,1,0:T(8,128)}, f32[32,32,128]{2,1,0:T(8,128)S(1)}, u32[]{:S(2)}) copy-start(f32[32,32,128]{2,1,0:T(8,128)S(1)} %collective-permute-done.6.p2) | copy-start | bytes 1572868
  141.4 0.8 copy-start.5

commit v3 on v2

--- a/solution.py
+++ b/solution.py
@@ -7,6 +7,8 @@
 
 Z = ("sect", "lev")
 PARTS = 4
+BLOCK = 8
+FIRST = 16
 HIGHEST = lax.Precision.HIGHEST
 SMEM = pl.BlockSpec(memory_space=pltpu.SMEM)
 VMEM = pl.BlockSpec(memory_space=pltpu.VMEM)
@@ -24,7 +26,41 @@
     return [blocks[0]] + [exchanged(blocks[bits], bits) for bits in range(1, PARTS)]
 
 
-def split_kernel(place, lent_rows, field, gain, p0, p1, p2, p3, borders, turned):
+def pack_kernel(place, mask, diffusion, inverse, remap, mine, sent):
+    rows, cols = mask.shape
+    levels = inverse.shape[0]
+    half, wide = levels // 2, cols // PARTS + 2
+    wet = mask[...].astype(jnp.float32)
+    nothing = jnp.zeros((1, rows), jnp.float32)
+    folded = jnp.concatenate([inverse[:half, :], inverse[half:, :]], axis=1)
+    for pack, part in ((mine, place[0]), (sent, place[0] ^ 2)):
+        for slot, plane in enumerate((wet.T, (wet * diffusion[...]).T)):
+            block = jnp.concatenate([nothing, plane, nothing], axis=0)
+            for at in range(PARTS):
+
+                @pl.when(part == at)
+                def _():
+                    first = at * (wide - 2)
+                    pack[slot * wide : (slot + 1) * wide, :] = block[first : first + wide]
+
+        pack[2 * wide : 2 * wide + half, :] = folded
+        pack[2 * wide + half :, :] = remap[...].astype(jnp.float32)
+
+
+def parameters(place, mask, diffusion, inverse, remap):
+    rows, cols = mask.shape
+    count = 2 * (cols // PARTS + 2) + inverse.shape[0] // 2 + 1
+    pack = jax.ShapeDtypeStruct((count, rows), jnp.float32)
+    return pl.pallas_call(
+        pack_kernel,
+        out_shape=[pack, pack],
+        in_specs=[SMEM] + [VMEM] * 4,
+        out_specs=[VMEM, VMEM],
+        name="parameters",
+    )(place, mask, diffusion, inverse, remap)
+
+
+def split_kernel(place, field, p0, p1, p2, p3, q2, ends, turned):
     levels, rows, cols = field.shape
     width = cols // PARTS
     turned[0] = jnp.zeros((levels, rows), jnp.float32)
@@ -32,31 +68,59 @@
     flat = turned.reshape((cols + 2) * levels, rows)
     for level in range(levels):
         flat[pl.ds(levels + level, cols, stride=levels), :] = field[level].T
-    for bits, part in enumerate((p0, p1, p2, p3)):
-        part[...] = turned[pl.ds((place[0] ^ bits) * width, width + 2)]
+    for bits, part in ((0, p0), (1, p1), (2, p2), (3, p3)):
+        part[...] = turned[pl.ds((place[0] ^ bits) * width, part.shape[0])]
+    q2[...] = turned[pl.ds((place[0] ^ 2) * width + p2.shape[0], q2.shape[0])]
+    ends[0] = turned[1]
+    ends[1] = turned[cols]
+
+
+def split_columns(place, field):
+    levels, rows, cols = field.shape
+    wide = cols // PARTS + 2
+    counts = [wide, wide, FIRST, wide, wide - FIRST, 2]
+    return pl.pallas_call(
+        split_kernel,
+        grid=(levels // BLOCK,),
+        out_shape=[jax.ShapeDtypeStruct((count, levels, rows), jnp.float32) for count in counts],
+        in_specs=[SMEM, pl.BlockSpec((BLOCK, rows, cols), lambda i: (i, 0, 0))],
+        out_specs=[pl.BlockSpec((count, BLOCK, rows), lambda i: (0, i, 0)) for count in counts],
+        scratch_shapes=[pltpu.VMEM((cols + 2, BLOCK, rows), jnp.float32)],
+        name="split_columns",
+    )(place, field)
+
+
+def border_kernel(place, lent_rows, field, ends, gain, borders, held, arrivals):
+    levels, rows, cols = field.shape
+    wanted = (0, rows - 1, lent_rows[0], lent_rows[rows - 1])
+    copies = [
+        pltpu.make_async_copy(field.at[:, pl.ds(row, 1), :], held.at[slot], arrivals.at[slot])
+        for slot, row in enumerate(wanted)
+    ]
+    for copy in copies:
+        copy.start()
+    for copy in copies:
+        copy.wait()
     component = place[0] // 2
     for at in range(PARTS):
-        lent = component != at // 2
-        for slot, fixed in enumerate((0, rows - 1)):
-            row = jnp.where(lent, lent_rows[fixed], fixed)
-            borders[at, slot * levels : (slot + 1) * levels, :] = field[:, pl.ds(row, 1), :].reshape(levels, cols)
-        borders[at, 2 * levels : 3 * levels, :] = turned[1]
-        borders[at, 3 * levels : 4 * levels, :] = turned[cols]
-        borders[at, 4 * levels :, :] = gain[...]
-
-
-def split_columns(place, lent_rows, field, gain):
+        lent = (component != at // 2).astype(jnp.int32)
+        for slot in range(2):
+            borders[at, slot * levels : (slot + 1) * levels, :] = held[2 * lent + slot].reshape(levels, cols)
+            borders[at, (2 + slot) * levels : (3 + slot) * levels, :] = ends[slot]
+        borders[at, 4 * levels :, :] = jnp.zeros((1, rows), jnp.float32)
+        borders[at, 4 * levels :, :levels] = gain[...]
+
+
+def side_borders(place, lent_rows, field, ends, gain):
     levels, rows, cols = field.shape
-    part = jax.ShapeDtypeStruct((cols // PARTS + 2, levels, rows), jnp.float32)
-    *parts, borders = pl.pallas_call(
-        split_kernel,
-        out_shape=[part] * PARTS + [jax.ShapeDtypeStruct((PARTS, 4 * levels + 1, rows), jnp.float32)],
-        in_specs=[SMEM, SMEM, VMEM, VMEM],
-        out_specs=[VMEM] * (PARTS + 1),
-        scratch_shapes=[pltpu.VMEM((cols + 2, levels, rows), jnp.float32)],
-        name="split_columns",
-    )(place, lent_rows, field, gain)
-    return parts, borders
+    return pl.pallas_call(
+        border_kernel,
+        out_shape=jax.ShapeDtypeStruct((PARTS, 4 * levels + 1, rows), jnp.float32),
+        in_specs=[SMEM, SMEM, pl.BlockSpec(memory_space=pl.ANY), VMEM, VMEM],
+        out_specs=VMEM,
+        scratch_shapes=[pltpu.VMEM((4, levels, 1, cols), jnp.float32), pltpu.SemaphoreType.DMA((4,))],
+        name="side_borders",
+    )(place, lent_rows, field, ends, gain)
 
 
 def join_kernel(place, p0, p1, p2, p3, sides, top_bottom, out, turned):
@@ -82,10 +146,16 @@
     cols = width * PARTS
     return pl.pallas_call(
         join_kernel,
+        grid=(levels // BLOCK,),
         out_shape=jax.ShapeDtypeStruct((levels, rows, cols), jnp.float32),
-        in_specs=[SMEM] + [VMEM] * 6,
-        out_specs=VMEM,
-        scratch_shapes=[pltpu.VMEM((cols, levels, rows), jnp.float32)],
+        in_specs=[SMEM]
+        + [pl.BlockSpec((width, BLOCK, rows), lambda i: (0, i, 0))] * PARTS
+        + [
+            pl.BlockSpec((PARTS, 2, BLOCK, rows), lambda i: (0, 0, i, 0)),
+            pl.BlockSpec((2, BLOCK, cols), lambda i: (0, i, 0)),
+        ],
+        out_specs=pl.BlockSpec((BLOCK, rows, cols), lambda i: (i, 0, 0)),
+        scratch_shapes=[pltpu.VMEM((cols, BLOCK, rows), jnp.float32)],
         name="join_columns",
     )(place, *parts, sides, top_bottom)
 
@@ -101,33 +171,36 @@
 
 
 def steps_kernel(
-    place, p0, p1, p2, p3, weights, gains, rows_from, wet, spread, halos,
+    place, p0, p1, p2, p3, q2, my_pack, other_pack, gains, halos,
     o0, o1, o2, o3, edges, column, state,
 ):
-    parts, outs = (p0, p1, p2, p3), (o0, o1, o2, o3)
+    outs = (o0, o1, o2, o3)
     wide, half, rows = p0.shape
-    spot = place[0]
-    component, swap = spot // 2, spot % 2
-    comps = [component, 1 - component]
-    width = wide - 2
+    spot, width = place[0], wide - 2
+    packs = (my_pack, other_pack)
+    at_once, few = 16, 8
     levels = 2 * half
-    at_once, few = 16, 8
     lane = lax.broadcasted_iota(jnp.int32, (levels, rows), 1)
     mixes, picks = [], []
-    for comp in range(2):
-        mix = weights[comps[comp]]
+    for pack in packs:
+        folded = pack[2 * wide : 2 * wide + half, :].T
+        mix = jnp.concatenate([folded[:levels], folded[levels:]], axis=1)
         turned = jnp.concatenate([mix[half:], mix[:half]], axis=0)
         turned = jnp.concatenate([turned[:, half:], turned[:, :half]], axis=1)
-        high, low = halves(jnp.where(swap == 0, mix, turned))
+        high, low = halves(jnp.where(spot % 2 == 0, mix, turned))
         mixes.append(jnp.concatenate([high, low, high], axis=1))
-        picks.append(jnp.broadcast_to(rows_from[pl.ds(comps[comp], 1), :], (levels, rows)))
+        pick = pack[2 * wide + half :, :].astype(jnp.int32)
+        picks.append(jnp.broadcast_to(pick, (levels, rows)))
 
     def joined(blocks, comp, *at):
         return jnp.concatenate(
             [blocks[(spot ^ (2 * comp + part),) + at] for part in range(2)], axis=0
         )
 
-    gain = [joined(gains, comp) for comp in range(2)]
+    gain = []
+    for comp in range(2):
+        parts_of = [jnp.broadcast_to(gains[spot ^ (2 * comp + part)], (rows, rows)).T for part in range(2)]
+        gain.append(jnp.concatenate([block[:half] for block in parts_of], axis=0))
 
     def solve(load, first, store, count):
         for comp in range(2):
@@ -144,7 +217,7 @@
                     column[comp, store + at + side] = solved[:, side * rows : (side + 1) * rows]
 
     def flux(comp, at):
-        return column[comp, at] * spread[comps[comp], pl.ds(at, 1), :]
+        return column[comp, at] * packs[comp][pl.ds(wide + at, 1), :]
 
     def lap(around, ends):
         mid = around[1]
@@ -153,16 +226,14 @@
         return above + below + around[0] + around[2] - 4.0 * mid
 
     def arrived(comp, at):
-        return jnp.concatenate([parts[2 * comp][at], parts[2 * comp + 1][at]], axis=0)
-
-    def first_solve(step, carry):
-        solve(arrived, step * at_once, step * at_once, at_once)
-        return carry
-
-    whole, rest = divmod(wide, at_once)
-    lax.fori_loop(0, whole, first_solve, 0)
-    if rest:
-        solve(arrived, whole * at_once, whole * at_once, rest)
+        if comp == 0:
+            blocks = [p0[at], p1[at]]
+        else:
+            blocks = [p2[at] if at < FIRST else q2[at - FIRST], p3[at]]
+        return jnp.concatenate(blocks, axis=0)
+
+    for first in range(0, wide, at_once):
+        solve(arrived, first, first, min(at_once, wide - first))
     tops = [joined(halos, comp, 1) for comp in range(2)]
     outer = []
     for comp in range(2):
@@ -185,7 +256,7 @@
                 j = first + at
                 ends = picked(tops[comp], jnp.where(lane == 0, j, j + width))
                 total = column[comp, j + 1] + lap(fluxes[at : at + 3], ends)
-                state[comp, j] = wet[comps[comp], pl.ds(j + 1, 1), :] * total
+                state[comp, j] = packs[comp][pl.ds(j + 1, 1), :] * total
 
     for first in range(0, width, few):
         spread_first(first, first == 0, first + few == width)
@@ -211,7 +282,7 @@
             for at in range(few):
                 j = first + at
                 total = column[comp, j + 1] + lap(fluxes[at : at + 3], 0.0)
-                done = wet[comps[comp], pl.ds(j + 1, 1), :] * total
+                done = packs[comp][pl.ds(j + 1, 1), :] * total
                 outs[2 * comp][j] = done[:half]
                 outs[2 * comp + 1][j] = done[half:]
                 ends = picked(fluxes[at + 1], jnp.where(lane == j, 0, rows - 1))
@@ -227,21 +298,21 @@
             edges[spot ^ (2 * comp + 1), slot] = value[half:]
 
 
-def two_steps(place, parts, weights, gains, rows_from, wet, spread, halos):
+def two_steps(place, parts, packs, gains, halos):
     wide, half, rows = parts[0].shape
     width = wide - 2
     part = jax.ShapeDtypeStruct((width, half, rows), jnp.float32)
     *results, edges = pl.pallas_call(
         steps_kernel,
         out_shape=[part] * PARTS + [jax.ShapeDtypeStruct((PARTS, 3, half, rows), jnp.float32)],
-        in_specs=[SMEM] + [VMEM] * 10,
+        in_specs=[SMEM] + [VMEM] * 9,
         out_specs=[VMEM] * (PARTS + 1),
         scratch_shapes=[
             pltpu.VMEM((2, wide, 2 * half, rows), jnp.float32),
             pltpu.VMEM((2, width, 2 * half, rows), jnp.float32),
         ],
         name="two_steps",
-    )(place, *parts, weights, gains, rows_from, wet, spread, halos)
+    )(place, *parts, *packs, gains, halos)
     return results, edges
 
 
@@ -261,39 +332,27 @@
     component, level_at = lax.axis_index("sect"), lax.axis_index("lev")
     spot = component * 2 + level_at
     place = spot[None].astype(jnp.int32)
-    wet = wet_mask[0, 0].astype(jnp.float32)
-    spread = wet * diffusion[0, 0]
     near = (nbr_tile[0], nbr_side[0], nbr_flip[0])
     inverse = vert_inverse[0, 0]
     my_rows = remap[0, 0]
 
-    def both(mine, other):
-        return jnp.where(component == 0, jnp.stack([mine, other]), jnp.stack([other, mine]))
-
-    other_rows = exchanged(my_rows, 2)
-
-    def padded(plane):
-        return jnp.pad(plane.T, ((1, 1), (0, 0)))
-
-    wet_cols, spread_cols = padded(wet), padded(spread)
-
-    def cut(plane, part):
-        return lax.dynamic_slice_in_dim(plane, part * width, width + 2, 0)
-
-    def packed(part):
-        return jnp.concatenate([cut(wet_cols, part), cut(spread_cols, part), inverse.reshape(-1, rows)])
-
-    packs = both(packed(spot), exchanged(packed(spot ^ 2), 2))
-    tall = width + 2
-    both_wet, both_spread = packs[:, :tall], packs[:, tall : 2 * tall]
-    weights = packs[:, 2 * tall :].reshape((2,) + inverse.shape).transpose(0, 2, 1)
-    rows_from = both(my_rows, other_rows)
-
-    gain = jnp.pad(coupling, ((0, 0), (0, rows - half)))
-    parts, borders = split_columns(place, other_rows, field, gain)
+    own_pack, sent = parameters(place, wet_mask[0, 0], diffusion[0, 0], inverse, remap[0])
+    packs = [own_pack, exchanged(sent, 2)]
+    other_rows = packs[1][-1].astype(jnp.int32)
+
+    mine, beside, ahead, far, rest, ends = split_columns(place, field)
+    ahead = exchanged(ahead, 2)
+    borders = side_borders(place, other_rows, field, ends, coupling)
+    beside, far, rest, borders, wet_mask, diffusion, inverse = lax.optimization_barrier(
+        (beside, far, rest, borders, wet_mask, diffusion, inverse)
+    )
     borders = traded(borders)
-    parts = all_exchanged(parts)
-
+    parts = [mine, exchanged(beside, 1), ahead, exchanged(far, 3), exchanged(rest, 2)]
+
+    wet = wet_mask[0, 0].astype(jnp.float32)
+    spread = wet * diffusion[0, 0]
+
+    gain_rows = borders[:, -1:]
     gains = borders[:, -1, :half].reshape(2, 2 * half)
     borders = borders[:, :-1].reshape(2, 2, 4, half, rows)
     borders = borders.transpose(0, 2, 1, 3, 4).reshape(2, 4, 2 * half, rows)
@@ -317,10 +376,7 @@
         blocks.append(jnp.stack([halo[2] if part == 0 else halo[3], ends]))
     halos = traded(jnp.stack(blocks))
 
-    gains = jnp.broadcast_to(gains.reshape(PARTS, half, 1), (PARTS, half, rows))
-    results, edges = two_steps(
-        place, parts, weights, gains, rows_from, both_wet, both_spread, halos
-    )
+    results, edges = two_steps(place, parts, packs, gain_rows, halos)
 
     edges = traded(edges)
     results = all_exchanged(results)

time: 147 us -> 139 us (0.946)
  waiting for transfers between devices: 68.3 us -> 60.3 us
  local copies, waits for them, and re-layouts: 9.45 us -> 4.27 us
  Pallas kernels: 18.3 us -> 21.8 us
  starting transfers between devices: 25.1 us -> 27.7 us
    ppermute x8, waiting for transfers between devices: 61.4 us -> 47.8 us  [exchanged(): return lax.ppermute(block, Z, [(at, at ^ bits) for at in range(PARTS)])]
    all_to_all x3, waiting for transfers between devices: 6.97 us -> 12.5 us  [traded(): return lax.all_to_all(blocks, Z, 0, 0)]
    pallas_call x2 -> x4, Pallas kernels: 8.9 us -> 12.7 us  [the longest x1 4.29 us: join_columns(): pl.pallas_call(join_kernel, grid=(levels // BLOCK,), out_shape=jax.ShapeD...]
    unnamed x26 -> x36, local copies, waits for them, and re-layouts: 3.24 us -> 1.49 us
    all_to_all x3, starting transfers between devices: 15 us -> 16.7 us  [traded(): return lax.all_to_all(blocks, Z, 0, 0)]
  transfers between devices with their start and end apart: 11 -> 11, of which waited for: 9 -> 7; matrix products, arithmetic and copies ran while one was open for 9% -> 5% of each run, Pallas kernels for 3% -> 5%
where the time goes in v3:
time: 139 us; the launch traced here: 138 us
  waiting for transfers between devices  60.3 us (43%)
  starting transfers between devices  27.7 us (20%)
  Pallas kernels  21.8 us (16%)
  blocking collectives  19.7 us (14%)
  local copies, waits for them, and re-layouts  4.27 us (3%)
  other arithmetic  3.34 us (2%)
    ppermute x8, waiting for transfers between devices, exchanged(): return lax.ppermute(block, Z, [(at, at ^ bits) for at in range(PARTS)])  47.8 us
    all_gather x2, blocking collectives, tile_halo(): every = lax.all_gather(edges, 'tile', axis=0)  19.7 us
    all_to_all x3, starting transfers between devices, traded(): return lax.all_to_all(blocks, Z, 0, 0)  16.7 us
    all_to_all x3, waiting for transfers between devices, traded(): return lax.all_to_all(blocks, Z, 0, 0)  12.5 us
    ppermute x8, starting transfers between devices, exchanged(): return lax.ppermute(block, Z, [(at, at ^ bits) for at in range(PARTS)])  10.9 us
    pallas_call x1, Pallas kernels, two_steps(): pl.pallas_call(steps_kernel, out_shape=[part] * PARTS + [jax.ShapeDtypeSt...  9.12 us
    pallas_call x1, Pallas kernels, join_columns(): pl.pallas_call(join_kernel, grid=(levels // BLOCK,), out_shape=jax.ShapeD...  4.29 us
    pallas_call x1, Pallas kernels, split_columns(): pl.pallas_call(split_kernel, grid=(levels // BLOCK,), out_shape=[jax.Shap...  4.21 us
  transfers between devices with their start and end apart: 11, of which 7 were waited for; matrix products, arithmetic and copies ran while one was open for 5% of the time, Pallas kernels for 5%

profile of v3, /device:TPU:8, one launch (start us, length us, event | category | flops | bytes accessed | tf_op | source)
XLA Modules:
  0.0 137.9 jit_solution(7393124470197399026)
XLA Ops:
  0.0 1.8 %parameters.1 = (f32[101,128]{1,0:T(8,128)}, f32[101,128]{1,0:T(8,128)}) custom-call(s32[1]{0:T(128)} %bitcast.place, s32[128,128]{1,0:T(8,128)} %bitcast.135, f32[128,128]{1,0:T(8,128)} %bitcast.137, f32[64,64]{1,0:T(8,128)} %bitcast.140, s32[1,128]{1,0:T(1,128)} %bitcast.142), custom_call_target="tpu_custom_call" | custom-call | tf_op jit(solution)/shard_map/parameters/pallas_call | solution.py:54
  1.8 2.6 %collective-permute-start = (f32[101,128]{1,0:T(8,128)}, f32[101,128]{1,0:T(8,128)S(1)}, u32[]{:S(2)}, u32[]{:S(2)}) collective-permute-start(f32[101,128]{1,0:T(8,128)} %get-tuple-element.29), channel_id=1, source_target_pairs={{0,2},{1,3},{2,0},{3,1},{4,6},{5,7},{6,4},{7,5},{8,10},{9,11},{10,... | collective-permute-start | bytes 155144 | tf_op jit(solution)/shard_map/ppermute | solution.py:22
  4.4 4.2 %split_columns.1 = (f32[34,32,128]{2,1,0:T(8,128)}, f32[34,32,128]{2,1,0:T(8,128)}, f32[16,32,128]{2,1,0:T(8,128)}, f32[34,32,128]{2,1,0:T(8,128)}, f32[18,32,128]{2,1,0:T(8,128)}, /*index=5*/f32[2,32,128]{2,1,0:T(8,128)}) custom-call(s32[1]{0:T(128)} %bitcast.place, f32[32,128,128]{2,1,0:T(8,128)} %bitcast.129), custom_call_target="tpu_custom_call" | custom-call | tf_op jit(solution)/shard_map/split_columns/pallas_call | solution.py:82
  9.7 2.4 %side_borders.1 = f32[4,129,128]{2,1,0:T(8,128)} custom-call(s32[1]{0:T(128)} %bitcast.place, s32[128]{0:T(128)} %fusion.29.lent_rows, f32[32,128,128]{2,1,0:T(8,128)} %bitcast.130, f32[2,32,128]{2,1,0:T(8,128)} %get-tuple-element.30.ends, f32[1,32]{1,0:T(1,128)} %gain.1), custom_call_target="tpu_custom_call" | custom-call | tf_op jit(solution)/shard_map/side_borders/pallas_call | solution.py:116
  12.1 5.3 %all-to-all-start = ((f32[4,129,128]{2,1,0:T(8,128)}), f32[4,129,128]{2,1,0:T(8,128)S(1)}, u32[]{:S(2)}, u32[]{:S(2)}) async-start(f32[4,129,128]{2,1,0:T(8,128)} %side_borders.1), calls=%async_computation | async-start | bytes 557056 | tf_op jit(solution)/shard_map/all_to_all | solution.py:18
  17.4 2.9 %collective-permute-start.3 = (f32[34,32,128]{2,1,0:T(8,128)S(1)}, f32[34,32,128]{2,1,0:T(8,128)S(1)}, u32[]{:S(2)}, u32[]{:S(2)}) collective-permute-start(f32[34,32,128]{2,1,0:T(8,128)S(1)} %copy-done.15), channel_id=1, source_target_pairs={{0,3},{1,2},{2,1},{3,0},{4,7},{5,6},{6,5},{7,4},{8,11},{9,10},{10,... | collective-permute-start | bytes 1671176 | tf_op jit(solution)/shard_map/ppermute | solution.py:22
  20.3 1.5 %collective-permute-start.4 = (f32[18,32,128]{2,1,0:T(8,128)S(1)}, f32[18,32,128]{2,1,0:T(8,128)S(1)}, u32[]{:S(2)}, u32[]{:S(2)}) collective-permute-start(f32[18,32,128]{2,1,0:T(8,128)S(1)} %copy-done.16), channel_id=1, source_target_pairs={{0,2},{1,3},{2,0},{3,1},{4,6},{5,7},{6,4},{7,5},{8,10},{9,11},{10,... | collective-permute-start | bytes 884744 | tf_op jit(solution)/shard_map/ppermute | solution.py:22
  22.0 5.9 %all-to-all-done = f32[4,129,128]{2,1,0:T(8,128)S(1)} async-done(((f32[4,129,128]{2,1,0:T(8,128)}), f32[4,129,128]{2,1,0:T(8,128)S(1)}, u32[]{:S(2)}, u32[]{:S(2)}) %all-to-all-start) | async-done | bytes 264224 | tf_op jit(solution)/shard_map/all_to_all | solution.py:18
  28.7 9.9 %all-gather = f32[32,32,128]{2,1,0:T(8,128)S(1)} all-gather(f32[4,32,128]{2,1,0:T(8,128)S(1)} %fusion), channel_id=2, replica_groups=mesh['tile'=8,'sect'=2,'lev'=2] {'tile'}, dimensions={0}, use_global_device_ids=true | all-gather | bytes 589824 | tf_op jit(solution)/shard_map/all_gather | solution.py:320
  39.8 0.7 pad_maximum_fusion
  40.4 6.2 %all-to-all-start.1 = ((f32[4,2,32,128]{3,2,1,0:T(8,128)}), f32[4,2,32,128]{3,2,1,0:T(8,128)S(1)}, u32[]{:S(2)}, u32[]{:S(2)}) async-start(f32[4,2,32,128]{3,2,1,0:T(8,128)} %pad_maximum_fusion), calls=%async_computation.1 | async-start | bytes 262144 | tf_op jit(solution)/shard_map/all_to_all | solution.py:18
  47.3 16.7 %collective-permute-done.4.q2 = f32[18,32,128]{2,1,0:T(8,128)S(1)} collective-permute-done((f32[18,32,128]{2,1,0:T(8,128)S(1)}, f32[18,32,128]{2,1,0:T(8,128)S(1)}, u32[]{:S(2)}, u32[]{:S(2)}) %collective-permute-start.4) | collective-permute-done | bytes 294944 | tf_op jit(solution)/shard_map/ppermute | solution.py:22
  64.0 3.2 %all-to-all-done.1.halos = f32[4,2,32,128]{3,2,1,0:T(8,128)S(1)} async-done(((f32[4,2,32,128]{3,2,1,0:T(8,128)}), f32[4,2,32,128]{3,2,1,0:T(8,128)S(1)}, u32[]{:S(2)}, u32[]{:S(2)}) %all-to-all-start.1) | async-done | bytes 131104 | tf_op jit(solution)/shard_map/all_to_all | solution.py:18
  67.8 9.1 %two_steps.1 = (f32[32,32,128]{2,1,0:T(8,128)}, f32[32,32,128]{2,1,0:T(8,128)}, f32[32,32,128]{2,1,0:T(8,128)}, f32[32,32,128]{2,1,0:T(8,128)}, f32[4,3,32,128]{3,2,1,0:T(8,128)}) custom-call(s32[1]{0:T(128)} %bitcast.place, f32[34,32,128]{2,1,0:T(8,128)} %get-tuple-element.25.p0, f32[34,32,128]{2,1,0:T(8,128)} %copy-done.1, f32[16,32,128]{2,1,0:T(8,128)} %copy-done.8, ...), custom_call_target="tpu_custom_call" | custom-call | tf_op jit(solution)/shard_map/two_steps/pallas_call | solution.py:305
  77.0 5.1 %all-to-all-start.2 = ((f32[4,3,32,128]{3,2,1,0:T(8,128)}), f32[4,3,32,128]{3,2,1,0:T(8,128)S(1)}, u32[]{:S(2)}, u32[]{:S(2)}) async-start(f32[4,3,32,128]{3,2,1,0:T(8,128)} %get-tuple-element.44), calls=%async_computation.2 | async-start | bytes 393216 | tf_op jit(solution)/shard_map/all_to_all | solution.py:18
  82.6 2.9 %collective-permute-start.6 = (f32[32,32,128]{2,1,0:T(8,128)}, f32[32,32,128]{2,1,0:T(8,128)S(1)}, u32[]{:S(2)}, u32[]{:S(2)}) collective-permute-start(f32[32,32,128]{2,1,0:T(8,128)} %get-tuple-element.42), channel_id=1, source_target_pairs={{0,2},{1,3},{2,0},{3,1},{4,6},{5,7},{6,4},{7,5},{8,10},{9,11},{10,... | collective-permute-start | bytes 1572872 | tf_op jit(solution)/shard_map/ppermute | solution.py:22
  86.0 3.4 %all-to-all-done.2 = f32[4,3,32,128]{3,2,1,0:T(8,128)S(1)} async-done(((f32[4,3,32,128]{3,2,1,0:T(8,128)}), f32[4,3,32,128]{3,2,1,0:T(8,128)S(1)}, u32[]{:S(2)}, u32[]{:S(2)}) %all-to-all-start.2) | async-done | bytes 196640 | tf_op jit(solution)/shard_map/all_to_all | solution.py:18
  89.7 9.8 %all-gather.1 = f32[32,32,128]{2,1,0:T(8,128)S(1)} all-gather(f32[4,32,128]{2,1,0:T(8,128)S(1)} %pad_maximum_fusion.2), channel_id=3, replica_groups=mesh['tile'=8,'sect'=2,'lev'=2] {'tile'}, dimensions={0}, use_global_device_ids=true | all-gather | bytes 589824 | tf_op jit(solution)/shard_map/all_gather | solution.py:320
  101.0 0.7 pad_maximum_fusion.1.sides
  101.7 4.7 %collective-permute-done.5.p1 = f32[32,32,128]{2,1,0:T(8,128)S(1)} collective-permute-done((f32[32,32,128]{2,1,0:T(8,128)}, f32[32,32,128]{2,1,0:T(8,128)S(1)}, u32[]{:S(2)}, u32[]{:S(2)}) %collective-permute-start.5) | collective-permute-done | bytes 524320 | tf_op jit(solution)/shard_map/ppermute | solution.py:22
  106.4 14.3 %collective-permute-done.6.p2 = f32[32,32,128]{2,1,0:T(8,128)S(1)} collective-permute-done((f32[32,32,128]{2,1,0:T(8,128)}, f32[32,32,128]{2,1,0:T(8,128)S(1)}, u32[]{:S(2)}, u32[]{:S(2)}) %collective-permute-start.6) | collective-permute-done | bytes 524320 | tf_op jit(solution)/shard_map/ppermute | solution.py:22
  120.7 12.1 %collective-permute-done.7.p3 = f32[32,32,128]{2,1,0:T(8,128)S(1)} collective-permute-done((f32[32,32,128]{2,1,0:T(8,128)}, f32[32,32,128]{2,1,0:T(8,128)S(1)}, u32[]{:S(2)}, u32[]{:S(2)}) %collective-permute-start.7) | collective-permute-done | bytes 524320 | tf_op jit(solution)/shard_map/ppermute | solution.py:22
  132.8 0.8 copy-done.5
  133.6 4.3 %join_columns.1 = f32[32,128,128]{2,1,0:T(8,128)} custom-call(s32[1]{0:T(128)} %bitcast.place, f32[32,32,128]{2,1,0:T(8,128)} %get-tuple-element.40.p0, f32[32,32,128]{2,1,0:T(8,128)} %copy-done.3, f32[32,32,128]{2,1,0:T(8,128)} %copy-done.4, f32[32,32,128]{2,1,0:T(8,128)} %copy-done.5, f32[4,2,32,128]{3,2,1,0:T(8,128)} %pad_maximum_fusion.1.sides, ...), custom_call_target="tpu_custom_call" | custom-call | tf_op jit(solution)/shard_map/join_columns/pallas_call | solution.py:147
  (89 shorter events, 7.1 us)
Async XLA Ops:
  0.0 9.0 %copy-start.14 = (s32[1,4]{1,0:T(1,128)S(1)}, s32[1,4]{1,0:T(1,128)}, u32[]{:S(2)}) copy-start(s32[1,4]{1,0:T(1,128)} %param.15) | copy-start | bytes 52
  0.0 9.0 %copy-start.13 = (s32[1,4]{1,0:T(1,128)S(1)}, s32[1,4]{1,0:T(1,128)}, u32[]{:S(2)}) copy-start(s32[1,4]{1,0:T(1,128)} %param.17) | copy-start | bytes 52
  0.0 9.0 %copy-start.17 = (s32[1,4]{1,0:T(1,128)S(1)}, s32[1,4]{1,0:T(1,128)}, u32[]{:S(2)}) copy-start(s32[1,4]{1,0:T(1,128)} %param.16) | copy-start | bytes 52
  1.8 7.3 %collective-permute-start = (f32[101,128]{1,0:T(8,128)}, f32[101,128]{1,0:T(8,128)S(1)}, u32[]{:S(2)}, u32[]{:S(2)}) collective-permute-start(f32[101,128]{1,0:T(8,128)} %get-tuple-element.29), channel_id=1, source_target_pairs={{0,2},{1,3},{2,0},{3,1},{4,6},{5,7},{6,4},{7,5},{8,10},{9,11},{10,... | collective-permute-start | bytes 155144 | tf_op jit(solution)/shard_map/ppermute | solution.py:22
  4.4 17.4 %copy-start = (s32[1,1,128,128]{3,2,1,0:T(8,128)S(1)}, s32[1,1,128,128]{3,2,1,0:T(8,128)}, u32[]{:S(2)}) copy-start(s32[1,1,128,128]{3,2,1,0:T(8,128)} %param.11) | copy-start | bytes 196612
  4.4 17.4 %copy-start.9 = (f32[1,1,128,128]{3,2,1,0:T(8,128)S(1)}, f32[1,1,128,128]{3,2,1,0:T(8,128)}, u32[]{:S(2)}) copy-start(f32[1,1,128,128]{3,2,1,0:T(8,128)} %param.10) | copy-start | bytes 196612
  8.6 8.8 %copy-start.15 = (f32[34,32,128]{2,1,0:T(8,128)S(1)}, f32[34,32,128]{2,1,0:T(8,128)}, u32[]{:S(2)}) copy-start(f32[34,32,128]{2,1,0:T(8,128)} %get-tuple-element.33) | copy-start | bytes 1671172
  8.6 11.7 %copy-start.16 = (f32[18,32,128]{2,1,0:T(8,128)S(1)}, f32[18,32,128]{2,1,0:T(8,128)}, u32[]{:S(2)}) copy-start(f32[18,32,128]{2,1,0:T(8,128)} %get-tuple-element.34) | copy-start | bytes 884740
  8.6 38.7 %collective-permute-start.2 = (f32[16,32,128]{2,1,0:T(8,128)}, f32[16,32,128]{2,1,0:T(8,128)S(1)}, u32[]{:S(2)}, u32[]{:S(2)}) collective-permute-start(f32[16,32,128]{2,1,0:T(8,128)} %get-tuple-element.32), channel_id=1, source_target_pairs={{0,2},{1,3},{2,0},{3,1},{4,6},{5,7},{6,4},{7,5},{8,10},{9,11},{10,... | collective-permute-start | bytes 786440 | tf_op jit(solution)/shard_map/ppermute | solution.py:22
  9.1 18.9 %copy-start.11 = (f32[101,128]{1,0:T(8,128)}, f32[101,128]{1,0:T(8,128)S(1)}, u32[]{:S(2)}) copy-start(f32[101,128]{1,0:T(8,128)S(1)} %collective-permute-done.other_pack) | copy-start | bytes 155140
  9.7 18.4 %copy-start.12 = (s32[1,1,128]{2,1,0:T(1,128)S(1)}, s32[1,1,128]{2,1,0:T(1,128)}, u32[]{:S(2)}) copy-start(s32[1,1,128]{2,1,0:T(1,128)} %param.12) | copy-start | bytes 1540
  9.7 18.6 %copy-start.10 = (f32[1,1,64,64]{3,2,1,0:T(8,128)S(1)}, f32[1,1,64,64]{3,2,1,0:T(8,128)}, u32[]{:S(2)}) copy-start(f32[1,1,64,64]{3,2,1,0:T(8,128)} %param.14) | copy-start | bytes 49156
  12.1 15.8 %all-to-all-start = ((f32[4,129,128]{2,1,0:T(8,128)}), f32[4,129,128]{2,1,0:T(8,128)S(1)}, u32[]{:S(2)}, u32[]{:S(2)}) async-start(f32[4,129,128]{2,1,0:T(8,128)} %side_borders.1), calls=%async_computation | async-start | bytes 557056 | tf_op jit(solution)/shard_map/all_to_all | solution.py:18
  17.4 46.6 %collective-permute-start.1 = (f32[34,32,128]{2,1,0:T(8,128)}, f32[34,32,128]{2,1,0:T(8,128)S(1)}, u32[]{:S(2)}, u32[]{:S(2)}) collective-permute-start(f32[34,32,128]{2,1,0:T(8,128)} %get-tuple-element.31), channel_id=1, source_target_pairs={{0,1},{1,0},{2,3},{3,2},{4,5},{5,4},{6,7},{7,6},{8,9},{9,8},{10,11... | collective-permute-start | bytes 1671176 | tf_op jit(solution)/shard_map/ppermute | solution.py:22
  17.4 46.6 %collective-permute-start.3 = (f32[34,32,128]{2,1,0:T(8,128)S(1)}, f32[34,32,128]{2,1,0:T(8,128)S(1)}, u32[]{:S(2)}, u32[]{:S(2)}) collective-permute-start(f32[34,32,128]{2,1,0:T(8,128)S(1)} %copy-done.15), channel_id=1, source_target_pairs={{0,3},{1,2},{2,1},{3,0},{4,7},{5,6},{6,5},{7,4},{8,11},{9,10},{10,... | collective-permute-start | bytes 1671176 | tf_op jit(solution)/shard_map/ppermute | solution.py:22
  20.3 43.7 %collective-permute-start.4 = (f32[18,32,128]{2,1,0:T(8,128)S(1)}, f32[18,32,128]{2,1,0:T(8,128)S(1)}, u32[]{:S(2)}, u32[]{:S(2)}) collective-permute-start(f32[18,32,128]{2,1,0:T(8,128)S(1)} %copy-done.16), channel_id=1, source_target_pairs={{0,2},{1,3},{2,0},{3,1},{4,6},{5,7},{6,4},{7,5},{8,10},{9,11},{10,... | collective-permute-start | bytes 884744 | tf_op jit(solution)/shard_map/ppermute | solution.py:22
  40.4 26.8 %all-to-all-start.1 = ((f32[4,2,32,128]{3,2,1,0:T(8,128)}), f32[4,2,32,128]{3,2,1,0:T(8,128)S(1)}, u32[]{:S(2)}, u32[]{:S(2)}) async-start(f32[4,2,32,128]{3,2,1,0:T(8,128)} %pad_maximum_fusion), calls=%async_computation.1 | async-start | bytes 262144 | tf_op jit(solution)/shard_map/all_to_all | solution.py:18
  47.3 19.9 %copy-start.8 = (f32[16,32,128]{2,1,0:T(8,128)}, f32[16,32,128]{2,1,0:T(8,128)S(1)}, u32[]{:S(2)}) copy-start(f32[16,32,128]{2,1,0:T(8,128)S(1)} %collective-permute-done.2.p2) | copy-start | bytes 786436
  77.0 12.5 %all-to-all-start.2 = ((f32[4,3,32,128]{3,2,1,0:T(8,128)}), f32[4,3,32,128]{3,2,1,0:T(8,128)S(1)}, u32[]{:S(2)}, u32[]{:S(2)}) async-start(f32[4,3,32,128]{3,2,1,0:T(8,128)} %get-tuple-element.44), calls=%async_computation.2 | async-start | bytes 393216 | tf_op jit(solution)/shard_map/all_to_all | solution.py:18
  82.5 23.9 %collective-permute-start.5 = (f32[32,32,128]{2,1,0:T(8,128)}, f32[32,32,128]{2,1,0:T(8,128)S(1)}, u32[]{:S(2)}, u32[]{:S(2)}) collective-permute-start(f32[32,32,128]{2,1,0:T(8,128)} %get-tuple-element.41), channel_id=1, source_target_pairs={{0,1},{1,0},{2,3},{3,2},{4,5},{5,4},{6,7},{7,6},{8,9},{9,8},{10,11... | collective-permute-start | bytes 1572872 | tf_op jit(solution)/shard_map/ppermute | solution.py:22
  82.6 38.1 %collective-permute-start.6 = (f32[32,32,128]{2,1,0:T(8,128)}, f32[32,32,128]{2,1,0:T(8,128)S(1)}, u32[]{:S(2)}, u32[]{:S(2)}) collective-permute-start(f32[32,32,128]{2,1,0:T(8,128)} %get-tuple-element.42), channel_id=1, source_target_pairs={{0,2},{1,3},{2,0},{3,1},{4,6},{5,7},{6,4},{7,5},{8,10},{9,11},{10,... | collective-permute-start | bytes 1572872 | tf_op jit(solution)/shard_map/ppermute | solution.py:22
  85.5 47.3 %collective-permute-start.7 = (f32[32,32,128]{2,1,0:T(8,128)}, f32[32,32,128]{2,1,0:T(8,128)S(1)}, u32[]{:S(2)}, u32[]{:S(2)}) collective-permute-start(f32[32,32,128]{2,1,0:T(8,128)} %get-tuple-element.43), channel_id=1, source_target_pairs={{0,3},{1,2},{2,1},{3,0},{4,7},{5,6},{6,5},{7,4},{8,11},{9,10},{10,... | collective-permute-start | bytes 1572872 | tf_op jit(solution)/shard_map/ppermute | solution.py:22
  106.4 26.4 %copy-start.3 = (f32[32,32,128]{2,1,0:T(8,128)}, f32[32,32,128]{2,1,0:T(8,128)S(1)}, u32[]{:S(2)}) copy-start(f32[32,32,128]{2,1,0:T(8,128)S(1)} %collective-permute-done.5.p1) | copy-start | bytes 1572868
  120.7 12.1 %copy-start.4 = (f32[32,32,128]{2,1,0:T(8,128)}, f32[32,32,128]{2,1,0:T(8,128)S(1)}, u32[]{:S(2)}) copy-start(f32[32,32,128]{2,1,0:T(8,128)S(1)} %collective-permute-done.6.p2) | copy-start | bytes 1572868
  (5 other events, 11.1 us)

commit v4 on v3

--- a/solution.py
+++ b/solution.py
@@ -7,7 +7,7 @@
 
 Z = ("sect", "lev")
 PARTS = 4
-BLOCK = 8
+BLOCK = 16
 FIRST = 16
 HIGHEST = lax.Precision.HIGHEST
 SMEM = pl.BlockSpec(memory_space=pltpu.SMEM)
@@ -234,10 +234,15 @@
 
     for first in range(0, wide, at_once):
         solve(arrived, first, first, min(at_once, wide - first))
-    tops = [joined(halos, comp, 1) for comp in range(2)]
+    tops = []
+    for comp in range(2):
+        folded = [halos[spot ^ (2 * comp + part), half:] for part in range(2)]
+        folded = [block[:, first : first + 2 * width] for block in folded for first in (0, 2 * width)]
+        ends = jnp.concatenate(folded, axis=0)
+        tops.append(jnp.concatenate([ends, ends], axis=1))
     outer = []
     for comp in range(2):
-        across = joined(halos, comp, 0)
+        across = joined(halos, comp, slice(0, half))
         outer.append(
             (
                 jnp.where(place[0] == 0, across, flux(comp, 0)),
@@ -293,9 +298,12 @@
     empty = jnp.zeros((levels, rows), jnp.float32)
     both = lax.fori_loop(0, width // few, second_spread, (empty, empty))
     for comp in range(2):
-        for slot, value in enumerate((flux(comp, 1), flux(comp, width), both[comp])):
-            edges[spot ^ (2 * comp), slot] = value[:half]
-            edges[spot ^ (2 * comp + 1), slot] = value[half:]
+        for part in range(2):
+            to, span = spot ^ (2 * comp + part), slice(part * half, (part + 1) * half)
+            edges[to, :half] = flux(comp, 1)[span]
+            edges[to, half : 2 * half] = flux(comp, width)[span]
+            ends = both[comp][span, : 2 * width]
+            edges[to, 2 * half :] = jnp.concatenate([ends[: half // 2], ends[half // 2 :]], axis=1)
 
 
 def two_steps(place, parts, packs, gains, halos):
@@ -304,7 +312,7 @@
     part = jax.ShapeDtypeStruct((width, half, rows), jnp.float32)
     *results, edges = pl.pallas_call(
         steps_kernel,
-        out_shape=[part] * PARTS + [jax.ShapeDtypeStruct((PARTS, 3, half, rows), jnp.float32)],
+        out_shape=[part] * PARTS + [jax.ShapeDtypeStruct((PARTS, 2 * half + half // 2, rows), jnp.float32)],
         in_specs=[SMEM] + [VMEM] * 9,
         out_specs=[VMEM] * (PARTS + 1),
         scratch_shapes=[
@@ -372,21 +380,21 @@
     for part in range(PARTS):
         span = slice(part * width, (part + 1) * width)
         ends = jnp.concatenate([halo[0][:, span], halo[1][:, span]], axis=1)
-        ends = jnp.pad(ends, ((0, 0), (0, rows - 2 * width)))
-        blocks.append(jnp.stack([halo[2] if part == 0 else halo[3], ends]))
+        ends = jnp.concatenate([ends[: half // 2], ends[half // 2 :]], axis=1)
+        blocks.append(jnp.concatenate([halo[2] if part == 0 else halo[3], ends]))
     halos = traded(jnp.stack(blocks))
 
     results, edges = two_steps(place, parts, packs, gain_rows, halos)
 
     edges = traded(edges)
     results = all_exchanged(results)
-    top = jnp.concatenate([edges[part, 2, :, :width] for part in range(PARTS)], axis=1)
-    bottom = jnp.concatenate([edges[part, 2, :, width : 2 * width] for part in range(PARTS)], axis=1)
-    halo = tile_halo(jnp.stack([top, bottom, edges[0, 0], edges[PARTS - 1, 1]]), *near)
+    starts, stops, folded = edges[:, :half], edges[:, half : 2 * half], edges[:, 2 * half :]
+    folded = folded.reshape(PARTS, half // 2, 2, 2, width).transpose(3, 2, 1, 0, 4).reshape(2, half, cols)
+    halo = tile_halo(jnp.concatenate([folded, starts[:1], stops[PARTS - 1 :]]), *near)
     sides = []
     for part in range(PARTS):
-        left = halo[2] if part == 0 else edges[part - 1, 1]
-        right = halo[3] if part == PARTS - 1 else edges[part + 1, 0]
+        left = halo[2] if part == 0 else stops[part - 1]
+        right = halo[3] if part == PARTS - 1 else starts[part + 1]
         sides.append(
             jnp.stack([left * wet[:, part * width], right * wet[:, (part + 1) * width - 1]])
         )

time: 139 us -> 136 us (0.978)
  Pallas kernels: 21.8 us -> 19.8 us
  transfers between devices with their start and end apart: 11 -> 11, of which waited for: 7 -> 7; matrix products, arithmetic and copies ran while one was open for 5% -> 5% of each run, Pallas kernels for 5% -> 4%
where the time goes in v4:
time: 136 us; the launch traced here: 135 us
  waiting for transfers between devices  59 us (43%)
  starting transfers between devices  27.5 us (20%)
  Pallas kernels  19.8 us (15%)
  blocking collectives  19.7 us (14%)
  local copies, waits for them, and re-layouts  4.92 us (4%)
  other arithmetic  3.21 us (2%)
    ppermute x8, waiting for transfers between devices, exchanged(): return lax.ppermute(block, Z, [(at, at ^ bits) for at in range(PARTS)])  47.2 us
    all_gather x2, blocking collectives, tile_halo(): every = lax.all_gather(edges, 'tile', axis=0)  19.7 us
    all_to_all x3, starting transfers between devices, traded(): return lax.all_to_all(blocks, Z, 0, 0)  16.6 us
    all_to_all x3, waiting for transfers between devices, traded(): return lax.all_to_all(blocks, Z, 0, 0)  11.8 us
    ppermute x8, starting transfers between devices, exchanged(): return lax.ppermute(block, Z, [(at, at ^ bits) for at in range(PARTS)])  10.9 us
    pallas_call x1, Pallas kernels, two_steps(): pl.pallas_call(steps_kernel, out_shape=[part] * PARTS + [jax.ShapeDtypeSt...  9.23 us
    pallas_call x1, Pallas kernels, split_columns(): pl.pallas_call(split_kernel, grid=(levels // BLOCK,), out_shape=[jax.Shap...  3.32 us
    pallas_call x1, Pallas kernels, join_columns(): pl.pallas_call(join_kernel, grid=(levels // BLOCK,), out_shape=jax.ShapeD...  3.12 us
  transfers between devices with their start and end apart: 11, of which 7 were waited for; matrix products, arithmetic and copies ran while one was open for 5% of the time, Pallas kernels for 4%

profile of v4, /device:TPU:8, one launch (start us, length us, event | category | flops | bytes accessed | tf_op | source)
XLA Modules:
  0.0 135.0 jit_solution(10396373284760458259)
XLA Ops:
  0.0 1.8 %parameters.1 = (f32[101,128]{1,0:T(8,128)}, f32[101,128]{1,0:T(8,128)}) custom-call(s32[1]{0:T(128)} %bitcast.place, s32[128,128]{1,0:T(8,128)} %bitcast.86, f32[128,128]{1,0:T(8,128)} %bitcast.89, f32[64,64]{1,0:T(8,128)} %bitcast.92, s32[1,128]{1,0:T(1,128)} %bitcast.94), custom_call_target="tpu_custom_call" | custom-call | tf_op jit(solution)/shard_map/parameters/pallas_call | solution.py:54
  1.8 2.6 %collective-permute-start = (f32[101,128]{1,0:T(8,128)}, f32[101,128]{1,0:T(8,128)S(1)}, u32[]{:S(2)}, u32[]{:S(2)}) collective-permute-start(f32[101,128]{1,0:T(8,128)} %get-tuple-element.29), channel_id=1, source_target_pairs={{0,2},{1,3},{2,0},{3,1},{4,6},{5,7},{6,4},{7,5},{8,10},{9,11},{10,... | collective-permute-start | bytes 155144 | tf_op jit(solution)/shard_map/ppermute | solution.py:22
  4.4 3.3 %split_columns.1 = (f32[34,32,128]{2,1,0:T(8,128)}, f32[34,32,128]{2,1,0:T(8,128)}, f32[16,32,128]{2,1,0:T(8,128)}, f32[34,32,128]{2,1,0:T(8,128)}, f32[18,32,128]{2,1,0:T(8,128)}, /*index=5*/f32[2,32,128]{2,1,0:T(8,128)}) custom-call(s32[1]{0:T(128)} %bitcast.place, f32[32,128,128]{2,1,0:T(8,128)} %bitcast.80), custom_call_target="tpu_custom_call" | custom-call | tf_op jit(solution)/shard_map/split_columns/pallas_call | solution.py:82
  8.7 2.4 %side_borders.1 = f32[4,129,128]{2,1,0:T(8,128)} custom-call(s32[1]{0:T(128)} %bitcast.place, s32[128]{0:T(128)} %fusion.30.lent_rows, f32[32,128,128]{2,1,0:T(8,128)} %bitcast.81, f32[2,32,128]{2,1,0:T(8,128)} %get-tuple-element.30.ends, f32[1,32]{1,0:T(1,128)} %gain.1), custom_call_target="tpu_custom_call" | custom-call | tf_op jit(solution)/shard_map/side_borders/pallas_call | solution.py:116
  11.1 5.3 %all-to-all-start = ((f32[4,129,128]{2,1,0:T(8,128)}), f32[4,129,128]{2,1,0:T(8,128)S(1)}, u32[]{:S(2)}, u32[]{:S(2)}) async-start(f32[4,129,128]{2,1,0:T(8,128)} %side_borders.1), calls=%async_computation | async-start | bytes 557056 | tf_op jit(solution)/shard_map/all_to_all | solution.py:18
  16.4 2.9 %collective-permute-start.3 = (f32[34,32,128]{2,1,0:T(8,128)S(1)}, f32[34,32,128]{2,1,0:T(8,128)S(1)}, u32[]{:S(2)}, u32[]{:S(2)}) collective-permute-start(f32[34,32,128]{2,1,0:T(8,128)S(1)} %copy-done.15), channel_id=1, source_target_pairs={{0,3},{1,2},{2,1},{3,0},{4,7},{5,6},{6,5},{7,4},{8,11},{9,10},{10,... | collective-permute-start | bytes 1671176 | tf_op jit(solution)/shard_map/ppermute | solution.py:22
  19.3 1.5 %collective-permute-start.4 = (f32[18,32,128]{2,1,0:T(8,128)S(1)}, f32[18,32,128]{2,1,0:T(8,128)S(1)}, u32[]{:S(2)}, u32[]{:S(2)}) collective-permute-start(f32[18,32,128]{2,1,0:T(8,128)S(1)} %copy-done.16), channel_id=1, source_target_pairs={{0,2},{1,3},{2,0},{3,1},{4,6},{5,7},{6,4},{7,5},{8,10},{9,11},{10,... | collective-permute-start | bytes 884744 | tf_op jit(solution)/shard_map/ppermute | solution.py:22
  21.0 6.0 %all-to-all-done = f32[4,129,128]{2,1,0:T(8,128)S(1)} async-done(((f32[4,129,128]{2,1,0:T(8,128)}), f32[4,129,128]{2,1,0:T(8,128)S(1)}, u32[]{:S(2)}, u32[]{:S(2)}) %all-to-all-start) | async-done | bytes 264224 | tf_op jit(solution)/shard_map/all_to_all | solution.py:18
  27.8 9.9 %all-gather = f32[32,32,128]{2,1,0:T(8,128)S(1)} all-gather(f32[4,32,128]{2,1,0:T(8,128)S(1)} %fusion), channel_id=2, replica_groups=mesh['tile'=8,'sect'=2,'lev'=2] {'tile'}, dimensions={0}, use_global_device_ids=true | all-gather | bytes 589824 | tf_op jit(solution)/shard_map/all_gather | solution.py:328
  39.0 0.7 pad_maximum_fusion.1
  39.7 6.2 %all-to-all-start.1 = ((f32[4,48,128]{2,1,0:T(8,128)}), f32[4,48,128]{2,1,0:T(8,128)S(1)}, u32[]{:S(2)}, u32[]{:S(2)}) async-start(f32[4,48,128]{2,1,0:T(8,128)} %pad_maximum_fusion.1), calls=%async_computation.1 | async-start | bytes 196608 | tf_op jit(solution)/shard_map/all_to_all | solution.py:18
  46.5 16.2 %collective-permute-done.4.q2 = f32[18,32,128]{2,1,0:T(8,128)S(1)} collective-permute-done((f32[18,32,128]{2,1,0:T(8,128)S(1)}, f32[18,32,128]{2,1,0:T(8,128)S(1)}, u32[]{:S(2)}, u32[]{:S(2)}) %collective-permute-start.4) | collective-permute-done | bytes 294944 | tf_op jit(solution)/shard_map/ppermute | solution.py:22
  62.8 2.9 %all-to-all-done.1.halos = f32[4,48,128]{2,1,0:T(8,128)S(1)} async-done(((f32[4,48,128]{2,1,0:T(8,128)}), f32[4,48,128]{2,1,0:T(8,128)S(1)}, u32[]{:S(2)}, u32[]{:S(2)}) %all-to-all-start.1) | async-done | bytes 98336 | tf_op jit(solution)/shard_map/all_to_all | solution.py:18
  66.7 9.2 %two_steps.1 = (f32[32,32,128]{2,1,0:T(8,128)}, f32[32,32,128]{2,1,0:T(8,128)}, f32[32,32,128]{2,1,0:T(8,128)}, f32[32,32,128]{2,1,0:T(8,128)}, f32[4,80,128]{2,1,0:T(8,128)}) custom-call(s32[1]{0:T(128)} %bitcast.place, f32[34,32,128]{2,1,0:T(8,128)} %get-tuple-element.25.p0, f32[34,32,128]{2,1,0:T(8,128)} %copy-done.1, f32[16,32,128]{2,1,0:T(8,128)} %copy-done.8, ...), custom_call_target="tpu_custom_call" | custom-call | tf_op jit(solution)/shard_map/two_steps/pallas_call | solution.py:313
  76.0 5.0 %all-to-all-start.2 = ((f32[4,80,128]{2,1,0:T(8,128)}), f32[4,80,128]{2,1,0:T(8,128)S(1)}, u32[]{:S(2)}, u32[]{:S(2)}) async-start(f32[4,80,128]{2,1,0:T(8,128)} %get-tuple-element.44), calls=%async_computation.2 | async-start | bytes 327680 | tf_op jit(solution)/shard_map/all_to_all | solution.py:18
  81.5 2.9 %collective-permute-start.6 = (f32[32,32,128]{2,1,0:T(8,128)}, f32[32,32,128]{2,1,0:T(8,128)S(1)}, u32[]{:S(2)}, u32[]{:S(2)}) collective-permute-start(f32[32,32,128]{2,1,0:T(8,128)} %get-tuple-element.42), channel_id=1, source_target_pairs={{0,2},{1,3},{2,0},{3,1},{4,6},{5,7},{6,4},{7,5},{8,10},{9,11},{10,... | collective-permute-start | bytes 1572872 | tf_op jit(solution)/shard_map/ppermute | solution.py:22
  84.9 2.9 %all-to-all-done.2 = f32[4,80,128]{2,1,0:T(8,128)S(1)} async-done(((f32[4,80,128]{2,1,0:T(8,128)}), f32[4,80,128]{2,1,0:T(8,128)S(1)}, u32[]{:S(2)}, u32[]{:S(2)}) %all-to-all-start.2) | async-done | bytes 163872 | tf_op jit(solution)/shard_map/all_to_all | solution.py:18
  88.2 9.9 %all-gather.1 = f32[32,32,128]{2,1,0:T(8,128)S(1)} all-gather(f32[4,32,128]{2,1,0:T(8,128)S(1)} %pad_maximum_fusion.2), channel_id=3, replica_groups=mesh['tile'=8,'sect'=2,'lev'=2] {'tile'}, dimensions={0}, use_global_device_ids=true | all-gather | bytes 589824 | tf_op jit(solution)/shard_map/all_gather | solution.py:328
  99.5 0.7 pad_maximum_fusion.sides
  100.1 4.7 %collective-permute-done.5.p1 = f32[32,32,128]{2,1,0:T(8,128)S(1)} collective-permute-done((f32[32,32,128]{2,1,0:T(8,128)}, f32[32,32,128]{2,1,0:T(8,128)S(1)}, u32[]{:S(2)}, u32[]{:S(2)}) %collective-permute-start.5) | collective-permute-done | bytes 524320 | tf_op jit(solution)/shard_map/ppermute | solution.py:22
  104.8 14.7 %collective-permute-done.6.p2 = f32[32,32,128]{2,1,0:T(8,128)S(1)} collective-permute-done((f32[32,32,128]{2,1,0:T(8,128)}, f32[32,32,128]{2,1,0:T(8,128)S(1)}, u32[]{:S(2)}, u32[]{:S(2)}) %collective-permute-start.6) | collective-permute-done | bytes 524320 | tf_op jit(solution)/shard_map/ppermute | solution.py:22
  119.5 11.6 %collective-permute-done.7.p3 = f32[32,32,128]{2,1,0:T(8,128)S(1)} collective-permute-done((f32[32,32,128]{2,1,0:T(8,128)}, f32[32,32,128]{2,1,0:T(8,128)S(1)}, u32[]{:S(2)}, u32[]{:S(2)}) %collective-permute-start.7) | collective-permute-done | bytes 524320 | tf_op jit(solution)/shard_map/ppermute | solution.py:22
  131.1 0.8 copy-done.5
  131.9 3.1 %join_columns.1 = f32[32,128,128]{2,1,0:T(8,128)} custom-call(s32[1]{0:T(128)} %bitcast.place, f32[32,32,128]{2,1,0:T(8,128)} %get-tuple-element.40.p0, f32[32,32,128]{2,1,0:T(8,128)} %copy-done.3, f32[32,32,128]{2,1,0:T(8,128)} %copy-done.4, f32[32,32,128]{2,1,0:T(8,128)} %copy-done.5, f32[4,2,32,128]{3,2,1,0:T(8,128)} %pad_maximum_fusion.sides, ...), custom_call_target="tpu_custom_call" | custom-call | tf_op jit(solution)/shard_map/join_columns/pallas_call | solution.py:147
  (89 shorter events, 7.6 us)
Async XLA Ops:
  0.0 8.1 %copy-start.14 = (s32[1,4]{1,0:T(1,128)S(1)}, s32[1,4]{1,0:T(1,128)}, u32[]{:S(2)}) copy-start(s32[1,4]{1,0:T(1,128)} %param.15) | copy-start | bytes 52
  0.0 8.1 %copy-start.13 = (s32[1,4]{1,0:T(1,128)S(1)}, s32[1,4]{1,0:T(1,128)}, u32[]{:S(2)}) copy-start(s32[1,4]{1,0:T(1,128)} %param.17) | copy-start | bytes 52
  0.0 8.1 %copy-start.17 = (s32[1,4]{1,0:T(1,128)S(1)}, s32[1,4]{1,0:T(1,128)}, u32[]{:S(2)}) copy-start(s32[1,4]{1,0:T(1,128)} %param.16) | copy-start | bytes 52
  1.8 6.4 %collective-permute-start = (f32[101,128]{1,0:T(8,128)}, f32[101,128]{1,0:T(8,128)S(1)}, u32[]{:S(2)}, u32[]{:S(2)}) collective-permute-start(f32[101,128]{1,0:T(8,128)} %get-tuple-element.29), channel_id=1, source_target_pairs={{0,2},{1,3},{2,0},{3,1},{4,6},{5,7},{6,4},{7,5},{8,10},{9,11},{10,... | collective-permute-start | bytes 155144 | tf_op jit(solution)/shard_map/ppermute | solution.py:22
  4.4 16.4 %copy-start = (s32[1,1,128,128]{3,2,1,0:T(8,128)S(1)}, s32[1,1,128,128]{3,2,1,0:T(8,128)}, u32[]{:S(2)}) copy-start(s32[1,1,128,128]{3,2,1,0:T(8,128)} %param.11) | copy-start | bytes 196612
  4.4 16.4 %copy-start.9 = (f32[1,1,128,128]{3,2,1,0:T(8,128)S(1)}, f32[1,1,128,128]{3,2,1,0:T(8,128)}, u32[]{:S(2)}) copy-start(f32[1,1,128,128]{3,2,1,0:T(8,128)} %param.10) | copy-start | bytes 196612
  7.7 8.7 %copy-start.15 = (f32[34,32,128]{2,1,0:T(8,128)S(1)}, f32[34,32,128]{2,1,0:T(8,128)}, u32[]{:S(2)}) copy-start(f32[34,32,128]{2,1,0:T(8,128)} %get-tuple-element.33) | copy-start | bytes 1671172
  7.7 11.6 %copy-start.16 = (f32[18,32,128]{2,1,0:T(8,128)S(1)}, f32[18,32,128]{2,1,0:T(8,128)}, u32[]{:S(2)}) copy-start(f32[18,32,128]{2,1,0:T(8,128)} %get-tuple-element.34) | copy-start | bytes 884740
  7.7 38.8 %collective-permute-start.2 = (f32[16,32,128]{2,1,0:T(8,128)}, f32[16,32,128]{2,1,0:T(8,128)S(1)}, u32[]{:S(2)}, u32[]{:S(2)}) collective-permute-start(f32[16,32,128]{2,1,0:T(8,128)} %get-tuple-element.32), channel_id=1, source_target_pairs={{0,2},{1,3},{2,0},{3,1},{4,6},{5,7},{6,4},{7,5},{8,10},{9,11},{10,... | collective-permute-start | bytes 786440 | tf_op jit(solution)/shard_map/ppermute | solution.py:22
  8.2 18.9 %copy-start.11 = (f32[101,128]{1,0:T(8,128)}, f32[101,128]{1,0:T(8,128)S(1)}, u32[]{:S(2)}) copy-start(f32[101,128]{1,0:T(8,128)S(1)} %collective-permute-done.other_pack) | copy-start | bytes 155140
  8.7 18.5 %copy-start.12 = (s32[1,1,128]{2,1,0:T(1,128)S(1)}, s32[1,1,128]{2,1,0:T(1,128)}, u32[]{:S(2)}) copy-start(s32[1,1,128]{2,1,0:T(1,128)} %param.12) | copy-start | bytes 1540
  8.7 18.7 %copy-start.10 = (f32[1,1,64,64]{3,2,1,0:T(8,128)S(1)}, f32[1,1,64,64]{3,2,1,0:T(8,128)}, u32[]{:S(2)}) copy-start(f32[1,1,64,64]{3,2,1,0:T(8,128)} %param.14) | copy-start | bytes 49156
  11.1 15.9 %all-to-all-start = ((f32[4,129,128]{2,1,0:T(8,128)}), f32[4,129,128]{2,1,0:T(8,128)S(1)}, u32[]{:S(2)}, u32[]{:S(2)}) async-start(f32[4,129,128]{2,1,0:T(8,128)} %side_borders.1), calls=%async_computation | async-start | bytes 557056 | tf_op jit(solution)/shard_map/all_to_all | solution.py:18
  16.4 49.3 %collective-permute-start.1 = (f32[34,32,128]{2,1,0:T(8,128)}, f32[34,32,128]{2,1,0:T(8,128)S(1)}, u32[]{:S(2)}, u32[]{:S(2)}) collective-permute-start(f32[34,32,128]{2,1,0:T(8,128)} %get-tuple-element.31), channel_id=1, source_target_pairs={{0,1},{1,0},{2,3},{3,2},{4,5},{5,4},{6,7},{7,6},{8,9},{9,8},{10,11... | collective-permute-start | bytes 1671176 | tf_op jit(solution)/shard_map/ppermute | solution.py:22
  16.4 49.3 %collective-permute-start.3 = (f32[34,32,128]{2,1,0:T(8,128)S(1)}, f32[34,32,128]{2,1,0:T(8,128)S(1)}, u32[]{:S(2)}, u32[]{:S(2)}) collective-permute-start(f32[34,32,128]{2,1,0:T(8,128)S(1)} %copy-done.15), channel_id=1, source_target_pairs={{0,3},{1,2},{2,1},{3,0},{4,7},{5,6},{6,5},{7,4},{8,11},{9,10},{10,... | collective-permute-start | bytes 1671176 | tf_op jit(solution)/shard_map/ppermute | solution.py:22
  19.3 43.4 %collective-permute-start.4 = (f32[18,32,128]{2,1,0:T(8,128)S(1)}, f32[18,32,128]{2,1,0:T(8,128)S(1)}, u32[]{:S(2)}, u32[]{:S(2)}) collective-permute-start(f32[18,32,128]{2,1,0:T(8,128)S(1)} %copy-done.16), channel_id=1, source_target_pairs={{0,2},{1,3},{2,0},{3,1},{4,6},{5,7},{6,4},{7,5},{8,10},{9,11},{10,... | collective-permute-start | bytes 884744 | tf_op jit(solution)/shard_map/ppermute | solution.py:22
  39.7 26.0 %all-to-all-start.1 = ((f32[4,48,128]{2,1,0:T(8,128)}), f32[4,48,128]{2,1,0:T(8,128)S(1)}, u32[]{:S(2)}, u32[]{:S(2)}) async-start(f32[4,48,128]{2,1,0:T(8,128)} %pad_maximum_fusion.1), calls=%async_computation.1 | async-start | bytes 196608 | tf_op jit(solution)/shard_map/all_to_all | solution.py:18
  46.5 19.2 %copy-start.8 = (f32[16,32,128]{2,1,0:T(8,128)}, f32[16,32,128]{2,1,0:T(8,128)S(1)}, u32[]{:S(2)}) copy-start(f32[16,32,128]{2,1,0:T(8,128)S(1)} %collective-permute-done.2.p2) | copy-start | bytes 786436
  76.0 11.8 %all-to-all-start.2 = ((f32[4,80,128]{2,1,0:T(8,128)}), f32[4,80,128]{2,1,0:T(8,128)S(1)}, u32[]{:S(2)}, u32[]{:S(2)}) async-start(f32[4,80,128]{2,1,0:T(8,128)} %get-tuple-element.44), calls=%async_computation.2 | async-start | bytes 327680 | tf_op jit(solution)/shard_map/all_to_all | solution.py:18
  81.4 23.5 %collective-permute-start.5 = (f32[32,32,128]{2,1,0:T(8,128)}, f32[32,32,128]{2,1,0:T(8,128)S(1)}, u32[]{:S(2)}, u32[]{:S(2)}) collective-permute-start(f32[32,32,128]{2,1,0:T(8,128)} %get-tuple-element.41), channel_id=1, source_target_pairs={{0,1},{1,0},{2,3},{3,2},{4,5},{5,4},{6,7},{7,6},{8,9},{9,8},{10,11... | collective-permute-start | bytes 1572872 | tf_op jit(solution)/shard_map/ppermute | solution.py:22
  81.5 38.1 %collective-permute-start.6 = (f32[32,32,128]{2,1,0:T(8,128)}, f32[32,32,128]{2,1,0:T(8,128)S(1)}, u32[]{:S(2)}, u32[]{:S(2)}) collective-permute-start(f32[32,32,128]{2,1,0:T(8,128)} %get-tuple-element.42), channel_id=1, source_target_pairs={{0,2},{1,3},{2,0},{3,1},{4,6},{5,7},{6,4},{7,5},{8,10},{9,11},{10,... | collective-permute-start | bytes 1572872 | tf_op jit(solution)/shard_map/ppermute | solution.py:22
  84.4 46.7 %collective-permute-start.7 = (f32[32,32,128]{2,1,0:T(8,128)}, f32[32,32,128]{2,1,0:T(8,128)S(1)}, u32[]{:S(2)}, u32[]{:S(2)}) collective-permute-start(f32[32,32,128]{2,1,0:T(8,128)} %get-tuple-element.43), channel_id=1, source_target_pairs={{0,3},{1,2},{2,1},{3,0},{4,7},{5,6},{6,5},{7,4},{8,11},{9,10},{10,... | collective-permute-start | bytes 1572872 | tf_op jit(solution)/shard_map/ppermute | solution.py:22
  104.8 26.3 %copy-start.3 = (f32[32,32,128]{2,1,0:T(8,128)}, f32[32,32,128]{2,1,0:T(8,128)S(1)}, u32[]{:S(2)}) copy-start(f32[32,32,128]{2,1,0:T(8,128)S(1)} %collective-permute-done.5.p1) | copy-start | bytes 1572868
  119.5 11.6 %copy-start.4 = (f32[32,32,128]{2,1,0:T(8,128)}, f32[32,32,128]{2,1,0:T(8,128)S(1)}, u32[]{:S(2)}) copy-start(f32[32,32,128]{2,1,0:T(8,128)S(1)} %collective-permute-done.6.p2) | copy-start | bytes 1572868
  (5 other events, 6.3 us)

commit v5 on v4

--- a/solution.py
+++ b/solution.py
@@ -12,6 +12,10 @@
 HIGHEST = lax.Precision.HIGHEST
 SMEM = pl.BlockSpec(memory_space=pltpu.SMEM)
 VMEM = pl.BlockSpec(memory_space=pltpu.VMEM)
+
+
+def in_vmem(block):
+    return pltpu.with_memory_space_constraint(block, pltpu.VMEM)
 
 
 def traded(blocks):
@@ -156,6 +160,7 @@
         ],
         out_specs=pl.BlockSpec((BLOCK, rows, cols), lambda i: (i, 0, 0)),
         scratch_shapes=[pltpu.VMEM((cols, BLOCK, rows), jnp.float32)],
+        compiler_params=pltpu.CompilerParams(vmem_limit_bytes=16 << 20),
         name="join_columns",
     )(place, *parts, sides, top_bottom)
 
@@ -269,11 +274,8 @@
     def held(comp, at):
         return state[comp, at]
 
-    def second_solve(step, carry):
-        solve(held, step * at_once, step * at_once + 1, at_once)
-        return carry
-
-    lax.fori_loop(0, width // at_once, second_solve, 0)
+    for first in range(0, width, at_once):
+        solve(held, first, first + 1, at_once)
     for comp in range(2):
         column[comp, 0] = jnp.zeros((levels, rows), jnp.float32)
         column[comp, width + 1] = jnp.zeros((levels, rows), jnp.float32)
@@ -296,7 +298,9 @@
         return tuple(kept)
 
     empty = jnp.zeros((levels, rows), jnp.float32)
-    both = lax.fori_loop(0, width // few, second_spread, (empty, empty))
+    both = (empty, empty)
+    for step in range(width // few):
+        both = second_spread(step, both)
     for comp in range(2):
         for part in range(2):
             to, span = spot ^ (2 * comp + part), slice(part * half, (part + 1) * half)
@@ -309,18 +313,19 @@
 def two_steps(place, parts, packs, gains, halos):
     wide, half, rows = parts[0].shape
     width = wide - 2
-    part = jax.ShapeDtypeStruct((width, half, rows), jnp.float32)
+    part = pltpu.HBM((width, half, rows), jnp.float32)
     *results, edges = pl.pallas_call(
         steps_kernel,
-        out_shape=[part] * PARTS + [jax.ShapeDtypeStruct((PARTS, 2 * half + half // 2, rows), jnp.float32)],
+        out_shape=[part] * PARTS + [pltpu.VMEM((PARTS, 2 * half + half // 2, rows), jnp.float32)],
         in_specs=[SMEM] + [VMEM] * 9,
         out_specs=[VMEM] * (PARTS + 1),
         scratch_shapes=[
             pltpu.VMEM((2, wide, 2 * half, rows), jnp.float32),
             pltpu.VMEM((2, width, 2 * half, rows), jnp.float32),
         ],
+        compiler_params=pltpu.CompilerParams(vmem_limit_bytes=24 << 20),
         name="two_steps",
-    )(place, *parts, *packs, gains, halos)
+    )(place, *map(in_vmem, parts), *packs, gains, halos)
     return results, edges
 
 

time: 136 us -> 130 us (0.956)
  Pallas kernels: 19.8 us -> 16.3 us
  local copies, waits for them, and re-layouts: 4.92 us -> 2.52 us
  waiting for transfers between devices: 59 us -> 60.7 us
    pallas_call x1, Pallas kernels: 9.23 us -> 6.81 us  [two_steps(): pl.pallas_call(steps_kernel, out_shape=[part] * PARTS + [pltpu.VMEM((PART...]
    ppermute x8, waiting for transfers between devices: 47.2 us -> 49.1 us  [exchanged(): return lax.ppermute(block, Z, [(at, at ^ bits) for at in range(PARTS)])]
    unnamed x36 -> x20, local copies, waits for them, and re-layouts: 1.87 us -> 0.04 us
  transfers between devices with their start and end apart: 11 -> 11, of which waited for: 7 -> 7; matrix products, arithmetic and copies ran while one was open for 5% -> 4% of each run, Pallas kernels for 4% -> 4%
where the time goes in v5:
time: 130 us
  waiting for transfers between devices  60.7 us (47%)
  starting transfers between devices  27.6 us (21%)
  blocking collectives  19.7 us (15%)
  Pallas kernels  16.3 us (13%)
  local copies, waits for them, and re-layouts  2.52 us (2%)
  other arithmetic  2.03 us (2%)
    ppermute x8, waiting for transfers between devices, exchanged(): return lax.ppermute(block, Z, [(at, at ^ bits) for at in range(PARTS)])  49.1 us
    all_gather x2, blocking collectives, tile_halo(): every = lax.all_gather(edges, 'tile', axis=0)  19.7 us
    all_to_all x3, starting transfers between devices, traded(): return lax.all_to_all(blocks, Z, 0, 0)  16.7 us
    all_to_all x3, waiting for transfers between devices, traded(): return lax.all_to_all(blocks, Z, 0, 0)  11.6 us
    ppermute x8, starting transfers between devices, exchanged(): return lax.ppermute(block, Z, [(at, at ^ bits) for at in range(PARTS)])  10.9 us
    pallas_call x1, Pallas kernels, two_steps(): pl.pallas_call(steps_kernel, out_shape=[part] * PARTS + [pltpu.VMEM((PART...  6.81 us
    pallas_call x1, Pallas kernels, split_columns(): pl.pallas_call(split_kernel, grid=(levels // BLOCK,), out_shape=[jax.Shap...  3.3 us
  transfers between devices with their start and end apart: 11, of which 7 were waited for; matrix products, arithmetic and copies ran while one was open for 4% of the time, Pallas kernels for 4%

profile of v5, /device:TPU:8, one launch (start us, length us, event | category | flops | bytes accessed | tf_op | source)
XLA Modules:
  0.0 129.8 jit_solution(2017023080177283796)
XLA Ops:
  0.0 1.8 %parameters.1 = (f32[101,128]{1,0:T(8,128)}, f32[101,128]{1,0:T(8,128)}) custom-call(s32[1]{0:T(128)} %bitcast.place, s32[128,128]{1,0:T(8,128)} %bitcast.86, f32[128,128]{1,0:T(8,128)} %bitcast.89, f32[64,64]{1,0:T(8,128)} %bitcast.92, s32[1,128]{1,0:T(1,128)} %bitcast.94), custom_call_target="tpu_custom_call" | custom-call | tf_op jit(solution)/shard_map/parameters/pallas_call | solution.py:58
  1.8 2.6 %collective-permute-start = (f32[101,128]{1,0:T(8,128)}, f32[101,128]{1,0:T(8,128)S(1)}, u32[]{:S(2)}, u32[]{:S(2)}) collective-permute-start(f32[101,128]{1,0:T(8,128)} %get-tuple-element.29), channel_id=1, source_target_pairs={{0,2},{1,3},{2,0},{3,1},{4,6},{5,7},{6,4},{7,5},{8,10},{9,11},{10,... | collective-permute-start | bytes 155144 | tf_op jit(solution)/shard_map/ppermute | solution.py:26
  4.4 3.3 %split_columns.1 = (f32[34,32,128]{2,1,0:T(8,128)}, f32[34,32,128]{2,1,0:T(8,128)}, f32[16,32,128]{2,1,0:T(8,128)}, f32[34,32,128]{2,1,0:T(8,128)}, f32[18,32,128]{2,1,0:T(8,128)}, /*index=5*/f32[2,32,128]{2,1,0:T(8,128)}) custom-call(s32[1]{0:T(128)} %bitcast.place, f32[32,128,128]{2,1,0:T(8,128)} %bitcast.80), custom_call_target="tpu_custom_call" | custom-call | tf_op jit(solution)/shard_map/split_columns/pallas_call | solution.py:86
  8.1 0.6 fusion.30.lent_rows
  8.7 2.4 %side_borders.1 = f32[4,129,128]{2,1,0:T(8,128)} custom-call(s32[1]{0:T(128)} %bitcast.place, s32[128]{0:T(128)} %fusion.30.lent_rows, f32[32,128,128]{2,1,0:T(8,128)} %bitcast.81, f32[2,32,128]{2,1,0:T(8,128)} %get-tuple-element.30.ends, f32[1,32]{1,0:T(1,128)} %gain.1), custom_call_target="tpu_custom_call" | custom-call | tf_op jit(solution)/shard_map/side_borders/pallas_call | solution.py:120
  11.0 5.3 %all-to-all-start = ((f32[4,129,128]{2,1,0:T(8,128)}), f32[4,129,128]{2,1,0:T(8,128)S(1)}, u32[]{:S(2)}, u32[]{:S(2)}) async-start(f32[4,129,128]{2,1,0:T(8,128)} %side_borders.1), calls=%async_computation | async-start | bytes 557056 | tf_op jit(solution)/shard_map/all_to_all | solution.py:22
  16.4 2.9 %collective-permute-start.3 = (f32[34,32,128]{2,1,0:T(8,128)}, f32[34,32,128]{2,1,0:T(8,128)S(1)}, u32[]{:S(2)}, u32[]{:S(2)}) collective-permute-start(f32[34,32,128]{2,1,0:T(8,128)} %get-tuple-element.33), channel_id=1, source_target_pairs={{0,3},{1,2},{2,1},{3,0},{4,7},{5,6},{6,5},{7,4},{8,11},{9,10},{10,... | collective-permute-start | bytes 1671176 | tf_op jit(solution)/shard_map/ppermute | solution.py:26
  19.3 1.5 %collective-permute-start.4 = (f32[18,32,128]{2,1,0:T(8,128)}, f32[18,32,128]{2,1,0:T(8,128)S(1)}, u32[]{:S(2)}, u32[]{:S(2)}) collective-permute-start(f32[18,32,128]{2,1,0:T(8,128)} %get-tuple-element.34), channel_id=1, source_target_pairs={{0,2},{1,3},{2,0},{3,1},{4,6},{5,7},{6,4},{7,5},{8,10},{9,11},{10,... | collective-permute-start | bytes 884744 | tf_op jit(solution)/shard_map/ppermute | solution.py:26
  21.0 5.9 %all-to-all-done = f32[4,129,128]{2,1,0:T(8,128)S(1)} async-done(((f32[4,129,128]{2,1,0:T(8,128)}), f32[4,129,128]{2,1,0:T(8,128)S(1)}, u32[]{:S(2)}, u32[]{:S(2)}) %all-to-all-start) | async-done | bytes 264224 | tf_op jit(solution)/shard_map/all_to_all | solution.py:22
  27.7 9.9 %all-gather = f32[32,32,128]{2,1,0:T(8,128)S(1)} all-gather(f32[4,32,128]{2,1,0:T(8,128)S(1)} %fusion), channel_id=2, replica_groups=mesh['tile'=8,'sect'=2,'lev'=2] {'tile'}, dimensions={0}, use_global_device_ids=true | all-gather | bytes 589824 | tf_op jit(solution)/shard_map/all_gather | solution.py:333
  38.9 0.6 pad_maximum_fusion.1
  39.6 6.2 %all-to-all-start.1 = ((f32[4,48,128]{2,1,0:T(8,128)}), f32[4,48,128]{2,1,0:T(8,128)S(1)}, u32[]{:S(2)}, u32[]{:S(2)}) async-start(f32[4,48,128]{2,1,0:T(8,128)} %pad_maximum_fusion.1), calls=%async_computation.1 | async-start | bytes 196608 | tf_op jit(solution)/shard_map/all_to_all | solution.py:22
  45.8 16.9 %collective-permute-done.4.q2 = f32[18,32,128]{2,1,0:T(8,128)S(1)} collective-permute-done((f32[18,32,128]{2,1,0:T(8,128)}, f32[18,32,128]{2,1,0:T(8,128)S(1)}, u32[]{:S(2)}, u32[]{:S(2)}) %collective-permute-start.4) | collective-permute-done | bytes 294944 | tf_op jit(solution)/shard_map/ppermute | solution.py:26
  62.8 2.8 %all-to-all-done.1.halos = f32[4,48,128]{2,1,0:T(8,128)S(1)} async-done(((f32[4,48,128]{2,1,0:T(8,128)}), f32[4,48,128]{2,1,0:T(8,128)S(1)}, u32[]{:S(2)}, u32[]{:S(2)}) %all-to-all-start.1) | async-done | bytes 98336 | tf_op jit(solution)/shard_map/all_to_all | solution.py:22
  65.6 6.8 %two_steps.1 = (f32[32,32,128]{2,1,0:T(8,128)}, f32[32,32,128]{2,1,0:T(8,128)}, f32[32,32,128]{2,1,0:T(8,128)}, f32[32,32,128]{2,1,0:T(8,128)}, f32[4,80,128]{2,1,0:T(8,128)}) custom-call(s32[1]{0:T(128)} %bitcast.place, f32[34,32,128]{2,1,0:T(8,128)S(1)} %copy-done, f32[34,32,128]{2,1,0:T(8,128)S(1)} %collective-permute-done.1.p1, ...), custom_call_target="tpu_custom_call" | custom-call | tf_op jit(solution)/shard_map/two_steps/pallas_call | solution.py:317
  72.4 5.2 %all-to-all-start.2 = ((f32[4,80,128]{2,1,0:T(8,128)}), f32[4,80,128]{2,1,0:T(8,128)S(1)}, u32[]{:S(2)}, u32[]{:S(2)}) async-start(f32[4,80,128]{2,1,0:T(8,128)} %get-tuple-element.44), calls=%async_computation.2 | async-start | bytes 327680 | tf_op jit(solution)/shard_map/all_to_all | solution.py:22
  78.1 2.9 %collective-permute-start.6 = (f32[32,32,128]{2,1,0:T(8,128)}, f32[32,32,128]{2,1,0:T(8,128)S(1)}, u32[]{:S(2)}, u32[]{:S(2)}) collective-permute-start(f32[32,32,128]{2,1,0:T(8,128)} %get-tuple-element.42), channel_id=1, source_target_pairs={{0,2},{1,3},{2,0},{3,1},{4,6},{5,7},{6,4},{7,5},{8,10},{9,11},{10,... | collective-permute-start | bytes 1572872 | tf_op jit(solution)/shard_map/ppermute | solution.py:26
  81.0 0.6 collective-permute-start.7
  81.5 2.9 %all-to-all-done.2 = f32[4,80,128]{2,1,0:T(8,128)S(1)} async-done(((f32[4,80,128]{2,1,0:T(8,128)}), f32[4,80,128]{2,1,0:T(8,128)S(1)}, u32[]{:S(2)}, u32[]{:S(2)}) %all-to-all-start.2) | async-done | bytes 163872 | tf_op jit(solution)/shard_map/all_to_all | solution.py:22
  84.8 9.9 %all-gather.1 = f32[32,32,128]{2,1,0:T(8,128)S(1)} all-gather(f32[4,32,128]{2,1,0:T(8,128)S(1)} %pad_maximum_fusion.2), channel_id=3, replica_groups=mesh['tile'=8,'sect'=2,'lev'=2] {'tile'}, dimensions={0}, use_global_device_ids=true | all-gather | bytes 589824 | tf_op jit(solution)/shard_map/all_gather | solution.py:333
  95.5 5.9 %collective-permute-done.5.p1 = f32[32,32,128]{2,1,0:T(8,128)S(1)} collective-permute-done((f32[32,32,128]{2,1,0:T(8,128)}, f32[32,32,128]{2,1,0:T(8,128)S(1)}, u32[]{:S(2)}, u32[]{:S(2)}) %collective-permute-start.5) | collective-permute-done | bytes 524320 | tf_op jit(solution)/shard_map/ppermute | solution.py:26
  101.4 14.7 %collective-permute-done.6.p2 = f32[32,32,128]{2,1,0:T(8,128)S(1)} collective-permute-done((f32[32,32,128]{2,1,0:T(8,128)}, f32[32,32,128]{2,1,0:T(8,128)S(1)}, u32[]{:S(2)}, u32[]{:S(2)}) %collective-permute-start.6) | collective-permute-done | bytes 524320 | tf_op jit(solution)/shard_map/ppermute | solution.py:26
  116.1 11.6 %collective-permute-done.7.p3 = f32[32,32,128]{2,1,0:T(8,128)S(1)} collective-permute-done((f32[32,32,128]{2,1,0:T(8,128)}, f32[32,32,128]{2,1,0:T(8,128)S(1)}, u32[]{:S(2)}, u32[]{:S(2)}) %collective-permute-start.7) | collective-permute-done | bytes 524320 | tf_op jit(solution)/shard_map/ppermute | solution.py:26
  127.7 2.1 %join_columns.1 = f32[32,128,128]{2,1,0:T(8,128)} custom-call(s32[1]{0:T(128)} %bitcast.place, f32[32,32,128]{2,1,0:T(8,128)S(1)} %copy-done.1, f32[32,32,128]{2,1,0:T(8,128)S(1)} %collective-permute-done.5.p1, f32[32,32,128]{2,1,0:T(8,128)S(1)} %collective-permute-done.6.p2, f32[32,32,128]{2,1,0:T(8,128)S(1)} %collective-permute-done.7.p3, ...), custom_call_target="tpu_custom_call" | custom-call | tf_op jit(solution)/shard_map/join_columns/pallas_call | solution.py:151
  (73 shorter events, 4.3 us)
Async XLA Ops:
  0.0 8.0 %copy-start.8 = (s32[1,4]{1,0:T(1,128)S(1)}, s32[1,4]{1,0:T(1,128)}, u32[]{:S(2)}) copy-start(s32[1,4]{1,0:T(1,128)} %param.15) | copy-start | bytes 52
  0.0 8.0 %copy-start.7 = (s32[1,4]{1,0:T(1,128)S(1)}, s32[1,4]{1,0:T(1,128)}, u32[]{:S(2)}) copy-start(s32[1,4]{1,0:T(1,128)} %param.17) | copy-start | bytes 52
  0.0 8.1 %copy-start.9 = (s32[1,4]{1,0:T(1,128)S(1)}, s32[1,4]{1,0:T(1,128)}, u32[]{:S(2)}) copy-start(s32[1,4]{1,0:T(1,128)} %param.16) | copy-start | bytes 52
  1.8 6.3 %collective-permute-start = (f32[101,128]{1,0:T(8,128)}, f32[101,128]{1,0:T(8,128)S(1)}, u32[]{:S(2)}, u32[]{:S(2)}) collective-permute-start(f32[101,128]{1,0:T(8,128)} %get-tuple-element.29), channel_id=1, source_target_pairs={{0,2},{1,3},{2,0},{3,1},{4,6},{5,7},{6,4},{7,5},{8,10},{9,11},{10,... | collective-permute-start | bytes 155144 | tf_op jit(solution)/shard_map/ppermute | solution.py:26
  4.4 16.4 %copy-start.3 = (s32[1,1,128,128]{3,2,1,0:T(8,128)S(1)}, s32[1,1,128,128]{3,2,1,0:T(8,128)}, u32[]{:S(2)}) copy-start(s32[1,1,128,128]{3,2,1,0:T(8,128)} %param.11) | copy-start | bytes 196612
  4.4 16.4 %copy-start.4 = (f32[1,1,128,128]{3,2,1,0:T(8,128)S(1)}, f32[1,1,128,128]{3,2,1,0:T(8,128)}, u32[]{:S(2)}) copy-start(f32[1,1,128,128]{3,2,1,0:T(8,128)} %param.10) | copy-start | bytes 196612
  7.7 38.1 %collective-permute-start.2 = (f32[16,32,128]{2,1,0:T(8,128)}, f32[16,32,128]{2,1,0:T(8,128)S(1)}, u32[]{:S(2)}, u32[]{:S(2)}) collective-permute-start(f32[16,32,128]{2,1,0:T(8,128)} %get-tuple-element.32), channel_id=1, source_target_pairs={{0,2},{1,3},{2,0},{3,1},{4,6},{5,7},{6,4},{7,5},{8,10},{9,11},{10,... | collective-permute-start | bytes 786440 | tf_op jit(solution)/shard_map/ppermute | solution.py:26
  8.7 18.5 %copy-start.6 = (s32[1,1,128]{2,1,0:T(1,128)S(1)}, s32[1,1,128]{2,1,0:T(1,128)}, u32[]{:S(2)}) copy-start(s32[1,1,128]{2,1,0:T(1,128)} %param.12) | copy-start | bytes 1540
  8.7 18.7 %copy-start.5 = (f32[1,1,64,64]{3,2,1,0:T(8,128)S(1)}, f32[1,1,64,64]{3,2,1,0:T(8,128)}, u32[]{:S(2)}) copy-start(f32[1,1,64,64]{3,2,1,0:T(8,128)} %param.14) | copy-start | bytes 49156
  11.0 15.9 %all-to-all-start = ((f32[4,129,128]{2,1,0:T(8,128)}), f32[4,129,128]{2,1,0:T(8,128)S(1)}, u32[]{:S(2)}, u32[]{:S(2)}) async-start(f32[4,129,128]{2,1,0:T(8,128)} %side_borders.1), calls=%async_computation | async-start | bytes 557056 | tf_op jit(solution)/shard_map/all_to_all | solution.py:22
  16.4 49.2 %collective-permute-start.1 = (f32[34,32,128]{2,1,0:T(8,128)}, f32[34,32,128]{2,1,0:T(8,128)S(1)}, u32[]{:S(2)}, u32[]{:S(2)}) collective-permute-start(f32[34,32,128]{2,1,0:T(8,128)} %get-tuple-element.31), channel_id=1, source_target_pairs={{0,1},{1,0},{2,3},{3,2},{4,5},{5,4},{6,7},{7,6},{8,9},{9,8},{10,11... | collective-permute-start | bytes 1671176 | tf_op jit(solution)/shard_map/ppermute | solution.py:26
  16.4 49.2 %collective-permute-start.3 = (f32[34,32,128]{2,1,0:T(8,128)}, f32[34,32,128]{2,1,0:T(8,128)S(1)}, u32[]{:S(2)}, u32[]{:S(2)}) collective-permute-start(f32[34,32,128]{2,1,0:T(8,128)} %get-tuple-element.33), channel_id=1, source_target_pairs={{0,3},{1,2},{2,1},{3,0},{4,7},{5,6},{6,5},{7,4},{8,11},{9,10},{10,... | collective-permute-start | bytes 1671176 | tf_op jit(solution)/shard_map/ppermute | solution.py:26
  19.3 43.5 %collective-permute-start.4 = (f32[18,32,128]{2,1,0:T(8,128)}, f32[18,32,128]{2,1,0:T(8,128)S(1)}, u32[]{:S(2)}, u32[]{:S(2)}) collective-permute-start(f32[18,32,128]{2,1,0:T(8,128)} %get-tuple-element.34), channel_id=1, source_target_pairs={{0,2},{1,3},{2,0},{3,1},{4,6},{5,7},{6,4},{7,5},{8,10},{9,11},{10,... | collective-permute-start | bytes 884744 | tf_op jit(solution)/shard_map/ppermute | solution.py:26
  26.9 38.7 %copy-start = (f32[34,32,128]{2,1,0:T(8,128)S(1)}, f32[34,32,128]{2,1,0:T(8,128)}, u32[]{:S(2)}) copy-start(f32[34,32,128]{2,1,0:T(8,128)} %get-tuple-element.25.p0) | copy-start | bytes 1671172
  26.9 38.7 %copy-start.2 = (f32[101,128]{1,0:T(8,128)S(1)}, f32[101,128]{1,0:T(8,128)}, u32[]{:S(2)}) copy-start(f32[101,128]{1,0:T(8,128)} %get-tuple-element.35.my_pack) | copy-start | bytes 155140
  39.6 26.0 %all-to-all-start.1 = ((f32[4,48,128]{2,1,0:T(8,128)}), f32[4,48,128]{2,1,0:T(8,128)S(1)}, u32[]{:S(2)}, u32[]{:S(2)}) async-start(f32[4,48,128]{2,1,0:T(8,128)} %pad_maximum_fusion.1), calls=%async_computation.1 | async-start | bytes 196608 | tf_op jit(solution)/shard_map/all_to_all | solution.py:22
  72.4 55.3 %copy-start.1 = (f32[32,32,128]{2,1,0:T(8,128)S(1)}, f32[32,32,128]{2,1,0:T(8,128)}, u32[]{:S(2)}) copy-start(f32[32,32,128]{2,1,0:T(8,128)} %get-tuple-element.40.p0) | copy-start | bytes 1572868
  72.4 12.0 %all-to-all-start.2 = ((f32[4,80,128]{2,1,0:T(8,128)}), f32[4,80,128]{2,1,0:T(8,128)S(1)}, u32[]{:S(2)}, u32[]{:S(2)}) async-start(f32[4,80,128]{2,1,0:T(8,128)} %get-tuple-element.44), calls=%async_computation.2 | async-start | bytes 327680 | tf_op jit(solution)/shard_map/all_to_all | solution.py:22
  78.0 23.5 %collective-permute-start.5 = (f32[32,32,128]{2,1,0:T(8,128)}, f32[32,32,128]{2,1,0:T(8,128)S(1)}, u32[]{:S(2)}, u32[]{:S(2)}) collective-permute-start(f32[32,32,128]{2,1,0:T(8,128)} %get-tuple-element.41), channel_id=1, source_target_pairs={{0,1},{1,0},{2,3},{3,2},{4,5},{5,4},{6,7},{7,6},{8,9},{9,8},{10,11... | collective-permute-start | bytes 1572872 | tf_op jit(solution)/shard_map/ppermute | solution.py:26
  78.1 38.1 %collective-permute-start.6 = (f32[32,32,128]{2,1,0:T(8,128)}, f32[32,32,128]{2,1,0:T(8,128)S(1)}, u32[]{:S(2)}, u32[]{:S(2)}) collective-permute-start(f32[32,32,128]{2,1,0:T(8,128)} %get-tuple-element.42), channel_id=1, source_target_pairs={{0,2},{1,3},{2,0},{3,1},{4,6},{5,7},{6,4},{7,5},{8,10},{9,11},{10,... | collective-permute-start | bytes 1572872 | tf_op jit(solution)/shard_map/ppermute | solution.py:26
  81.0 46.7 %collective-permute-start.7 = (f32[32,32,128]{2,1,0:T(8,128)}, f32[32,32,128]{2,1,0:T(8,128)S(1)}, u32[]{:S(2)}, u32[]{:S(2)}) collective-permute-start(f32[32,32,128]{2,1,0:T(8,128)} %get-tuple-element.43), channel_id=1, source_target_pairs={{0,3},{1,2},{2,1},{3,0},{4,7},{5,6},{6,5},{7,4},{8,11},{9,10},{10,... | collective-permute-start | bytes 1572872 | tf_op jit(solution)/shard_map/ppermute | solution.py:26

commit v6 on v5

--- a/solution.py
+++ b/solution.py
@@ -8,6 +8,7 @@
 Z = ("sect", "lev")
 PARTS = 4
 BLOCK = 16
+JOIN_BLOCK = 8
 FIRST = 16
 HIGHEST = lax.Precision.HIGHEST
 SMEM = pl.BlockSpec(memory_space=pltpu.SMEM)
@@ -150,16 +151,16 @@
     cols = width * PARTS
     return pl.pallas_call(
         join_kernel,
-        grid=(levels // BLOCK,),
+        grid=(levels // JOIN_BLOCK,),
         out_shape=jax.ShapeDtypeStruct((levels, rows, cols), jnp.float32),
         in_specs=[SMEM]
-        + [pl.BlockSpec((width, BLOCK, rows), lambda i: (0, i, 0))] * PARTS
+        + [pl.BlockSpec((width, JOIN_BLOCK, rows), lambda i: (0, i, 0))] * PARTS
         + [
-            pl.BlockSpec((PARTS, 2, BLOCK, rows), lambda i: (0, 0, i, 0)),
-            pl.BlockSpec((2, BLOCK, cols), lambda i: (0, i, 0)),
+            pl.BlockSpec((PARTS, 2, JOIN_BLOCK, rows), lambda i: (0, 0, i, 0)),
+            pl.BlockSpec((2, JOIN_BLOCK, cols), lambda i: (0, i, 0)),
         ],
-        out_specs=pl.BlockSpec((BLOCK, rows, cols), lambda i: (i, 0, 0)),
-        scratch_shapes=[pltpu.VMEM((cols, BLOCK, rows), jnp.float32)],
+        out_specs=pl.BlockSpec((JOIN_BLOCK, rows, cols), lambda i: (i, 0, 0)),
+        scratch_shapes=[pltpu.VMEM((cols, JOIN_BLOCK, rows), jnp.float32)],
         compiler_params=pltpu.CompilerParams(vmem_limit_bytes=16 << 20),
         name="join_columns",
     )(place, *parts, sides, top_bottom)
@@ -316,7 +317,7 @@
     part = pltpu.HBM((width, half, rows), jnp.float32)
     *results, edges = pl.pallas_call(
         steps_kernel,
-        out_shape=[part] * PARTS + [pltpu.VMEM((PARTS, 2 * half + half // 2, rows), jnp.float32)],
+        out_shape=[part] * 2 + [pltpu.VMEM((width, half, rows), jnp.float32)] * 2 + [pltpu.VMEM((PARTS, 2 * half + half // 2, rows), jnp.float32)],
         in_specs=[SMEM] + [VMEM] * 9,
         out_specs=[VMEM] * (PARTS + 1),
         scratch_shapes=[

time: 130 us -> 131 us (level)
  waiting for transfers between devices: 60.7 us -> 54.6 us
  local copies, waits for them, and re-layouts: 2.52 us -> 6.35 us
    ppermute x8, waiting for transfers between devices: 49.1 us -> 44.2 us  [exchanged(): return lax.ppermute(block, Z, [(at, at ^ bits) for at in range(PARTS)])]
    reshape x3, local copies, waits for them, and re-layouts: 0.36 us -> 1.91 us  [on_device(): folded.reshape(PARTS, half // 2, 2, 2, width).transpose(3, 2, 1, 0, 4)]
  transfers between devices with their start and end apart: 11 -> 11, of which waited for: 7 -> 7; matrix products, arithmetic and copies ran while one was open for 4% -> 8% of each run, Pallas kernels for 4% -> 4%
where the time goes in v6:
time: 131 us; the launch traced here: 130 us
  waiting for transfers between devices  54.6 us (42%)
  starting transfers between devices  27.6 us (21%)
  blocking collectives  20.8 us (16%)
  Pallas kernels  16.6 us (13%)
  local copies, waits for them, and re-layouts  6.35 us (5%)
  other arithmetic  3.29 us (3%)
    ppermute x8, waiting for transfers between devices, exchanged(): return lax.ppermute(block, Z, [(at, at ^ bits) for at in range(PARTS)])  44.2 us
    all_gather x2, blocking collectives, tile_halo(): every = lax.all_gather(edges, 'tile', axis=0)  20.8 us
    all_to_all x3, starting transfers between devices, traded(): return lax.all_to_all(blocks, Z, 0, 0)  16.8 us
    ppermute x8, starting transfers between devices, exchanged(): return lax.ppermute(block, Z, [(at, at ^ bits) for at in range(PARTS)])  10.8 us
    all_to_all x3, waiting for transfers between devices, traded(): return lax.all_to_all(blocks, Z, 0, 0)  10.4 us
    pallas_call x1, Pallas kernels, two_steps(): pl.pallas_call(steps_kernel, out_shape=[part] * 2 + [pltpu.VMEM((width, h...  6.48 us
    pallas_call x1, Pallas kernels, split_columns(): pl.pallas_call(split_kernel, grid=(levels // BLOCK,), out_shape=[jax.Shap...  3.32 us
  transfers between devices with their start and end apart: 11, of which 7 were waited for; matrix products, arithmetic and copies ran while one was open for 8% of the time, Pallas kernels for 4%

profile of v6, /device:TPU:8, one launch (start us, length us, event | category | flops | bytes accessed | tf_op | source)
XLA Modules:
  0.0 130.1 jit_solution(11153169653472756541)
XLA Ops:
  0.0 1.8 %parameters.1 = (f32[101,128]{1,0:T(8,128)}, f32[101,128]{1,0:T(8,128)}) custom-call(s32[1]{0:T(128)} %bitcast.place, s32[128,128]{1,0:T(8,128)} %bitcast.86, f32[128,128]{1,0:T(8,128)} %bitcast.89, f32[64,64]{1,0:T(8,128)} %bitcast.92, s32[1,128]{1,0:T(1,128)} %bitcast.94), custom_call_target="tpu_custom_call" | custom-call | tf_op jit(solution)/shard_map/parameters/pallas_call | solution.py:59
  1.8 2.6 %collective-permute-start = (f32[101,128]{1,0:T(8,128)}, f32[101,128]{1,0:T(8,128)S(1)}, u32[]{:S(2)}, u32[]{:S(2)}) collective-permute-start(f32[101,128]{1,0:T(8,128)} %get-tuple-element.29), channel_id=1, source_target_pairs={{0,2},{1,3},{2,0},{3,1},{4,6},{5,7},{6,4},{7,5},{8,10},{9,11},{10,... | collective-permute-start | bytes 155144 | tf_op jit(solution)/shard_map/ppermute | solution.py:27
  4.4 3.3 %split_columns.1 = (f32[34,32,128]{2,1,0:T(8,128)}, f32[34,32,128]{2,1,0:T(8,128)}, f32[16,32,128]{2,1,0:T(8,128)}, f32[34,32,128]{2,1,0:T(8,128)}, f32[18,32,128]{2,1,0:T(8,128)}, /*index=5*/f32[2,32,128]{2,1,0:T(8,128)}) custom-call(s32[1]{0:T(128)} %bitcast.place, f32[32,128,128]{2,1,0:T(8,128)} %bitcast.80), custom_call_target="tpu_custom_call" | custom-call | tf_op jit(solution)/shard_map/split_columns/pallas_call | solution.py:87
  8.7 2.4 %side_borders.1 = f32[4,129,128]{2,1,0:T(8,128)} custom-call(s32[1]{0:T(128)} %bitcast.place, s32[128]{0:T(128)} %fusion.30.lent_rows, f32[32,128,128]{2,1,0:T(8,128)} %bitcast.81, f32[2,32,128]{2,1,0:T(8,128)} %get-tuple-element.30.ends, f32[1,32]{1,0:T(1,128)} %gain.1), custom_call_target="tpu_custom_call" | custom-call | tf_op jit(solution)/shard_map/side_borders/pallas_call | solution.py:121
  11.1 5.4 %all-to-all-start = ((f32[4,129,128]{2,1,0:T(8,128)}), f32[4,129,128]{2,1,0:T(8,128)S(1)}, u32[]{:S(2)}, u32[]{:S(2)}) async-start(f32[4,129,128]{2,1,0:T(8,128)} %side_borders.1), calls=%async_computation | async-start | bytes 557056 | tf_op jit(solution)/shard_map/all_to_all | solution.py:23
  16.5 2.9 %collective-permute-start.3 = (f32[34,32,128]{2,1,0:T(8,128)}, f32[34,32,128]{2,1,0:T(8,128)S(1)}, u32[]{:S(2)}, u32[]{:S(2)}) collective-permute-start(f32[34,32,128]{2,1,0:T(8,128)} %get-tuple-element.33), channel_id=1, source_target_pairs={{0,3},{1,2},{2,1},{3,0},{4,7},{5,6},{6,5},{7,4},{8,11},{9,10},{10,... | collective-permute-start | bytes 1671176 | tf_op jit(solution)/shard_map/ppermute | solution.py:27
  19.4 1.5 %collective-permute-start.4 = (f32[18,32,128]{2,1,0:T(8,128)}, f32[18,32,128]{2,1,0:T(8,128)S(1)}, u32[]{:S(2)}, u32[]{:S(2)}) collective-permute-start(f32[18,32,128]{2,1,0:T(8,128)} %get-tuple-element.34), channel_id=1, source_target_pairs={{0,2},{1,3},{2,0},{3,1},{4,6},{5,7},{6,4},{7,5},{8,10},{9,11},{10,... | collective-permute-start | bytes 884744 | tf_op jit(solution)/shard_map/ppermute | solution.py:27
  21.0 5.9 %all-to-all-done = f32[4,129,128]{2,1,0:T(8,128)S(1)} async-done(((f32[4,129,128]{2,1,0:T(8,128)}), f32[4,129,128]{2,1,0:T(8,128)S(1)}, u32[]{:S(2)}, u32[]{:S(2)}) %all-to-all-start) | async-done | bytes 264224 | tf_op jit(solution)/shard_map/all_to_all | solution.py:23
  27.7 9.9 %all-gather = f32[32,32,128]{2,1,0:T(8,128)S(1)} all-gather(f32[4,32,128]{2,1,0:T(8,128)S(1)} %fusion), channel_id=2, replica_groups=mesh['tile'=8,'sect'=2,'lev'=2] {'tile'}, dimensions={0}, use_global_device_ids=true | all-gather | bytes 589824 | tf_op jit(solution)/shard_map/all_gather | solution.py:334
  39.6 6.2 %all-to-all-start.1 = ((f32[4,48,128]{2,1,0:T(8,128)}), f32[4,48,128]{2,1,0:T(8,128)S(1)}, u32[]{:S(2)}, u32[]{:S(2)}) async-start(f32[4,48,128]{2,1,0:T(8,128)} %pad_maximum_fusion.1), calls=%async_computation.1 | async-start | bytes 196608 | tf_op jit(solution)/shard_map/all_to_all | solution.py:23
  46.5 16.3 %collective-permute-done.4.q2 = f32[18,32,128]{2,1,0:T(8,128)S(1)} collective-permute-done((f32[18,32,128]{2,1,0:T(8,128)}, f32[18,32,128]{2,1,0:T(8,128)S(1)}, u32[]{:S(2)}, u32[]{:S(2)}) %collective-permute-start.4) | collective-permute-done | bytes 294944 | tf_op jit(solution)/shard_map/ppermute | solution.py:27
  62.8 2.8 %all-to-all-done.1.halos = f32[4,48,128]{2,1,0:T(8,128)S(1)} async-done(((f32[4,48,128]{2,1,0:T(8,128)}), f32[4,48,128]{2,1,0:T(8,128)S(1)}, u32[]{:S(2)}, u32[]{:S(2)}) %all-to-all-start.1) | async-done | bytes 98336 | tf_op jit(solution)/shard_map/all_to_all | solution.py:23
  65.6 6.5 %two_steps.1 = (f32[32,32,128]{2,1,0:T(8,128)}, f32[32,32,128]{2,1,0:T(8,128)}, f32[32,32,128]{2,1,0:T(8,128)S(1)}, f32[32,32,128]{2,1,0:T(8,128)S(1)}, f32[4,80,128]{2,1,0:T(8,128)}) custom-call(s32[1]{0:T(128)} %bitcast.place, f32[34,32,128]{2,1,0:T(8,128)S(1)} %copy-done, f32[34,32,128]{2,1,0:T(8,128)S(1)} %collective-permute-done.1.p1, ...), custom_call_target="tpu_custom_call" | custom-call | tf_op jit(solution)/shard_map/two_steps/pallas_call | solution.py:318
  72.1 5.2 %all-to-all-start.2 = ((f32[4,80,128]{2,1,0:T(8,128)}), f32[4,80,128]{2,1,0:T(8,128)S(1)}, u32[]{:S(2)}, u32[]{:S(2)}) async-start(f32[4,80,128]{2,1,0:T(8,128)} %get-tuple-element.44), calls=%async_computation.2 | async-start | bytes 327680 | tf_op jit(solution)/shard_map/all_to_all | solution.py:23
  77.3 0.9 slice_reduce_fusion.7
  78.9 2.9 %collective-permute-start.6 = (f32[32,32,128]{2,1,0:T(8,128)S(1)}, f32[32,32,128]{2,1,0:T(8,128)S(1)}, u32[]{:S(2)}, u32[]{:S(2)}) collective-permute-start(f32[32,32,128]{2,1,0:T(8,128)S(1)} %get-tuple-element.42), channel_id=1, source_target_pairs={{0,2},{1,3},{2,0},{3,1},{4,6},{5,7},{6,4},{7,5},{8,10},{9,11},{10,... | collective-permute-start | bytes 1572872 | tf_op jit(solution)/shard_map/ppermute | solution.py:27
  82.4 1.7 %all-to-all-done.2 = f32[4,80,128]{2,1,0:T(8,128)S(1)} async-done(((f32[4,80,128]{2,1,0:T(8,128)}), f32[4,80,128]{2,1,0:T(8,128)S(1)}, u32[]{:S(2)}, u32[]{:S(2)}) %all-to-all-start.2) | async-done | bytes 163872 | tf_op jit(solution)/shard_map/all_to_all | solution.py:23
  84.9 1.0 reshape.167
  86.7 10.9 %all-gather.1 = f32[32,32,128]{2,1,0:T(8,128)} all-gather(f32[4,32,128]{2,1,0:T(8,128)S(1)} %pad_maximum_fusion.2), channel_id=3, replica_groups=mesh['tile'=8,'sect'=2,'lev'=2] {'tile'}, dimensions={0}, use_global_device_ids=true | all-gather | bytes 589824 | tf_op jit(solution)/shard_map/all_gather | solution.py:334
  97.6 1.6 %gather_fusion.1 = f32[4,32,128]{2,1,0:T(8,128)S(1)} fusion(f32[8,4,32,128]{3,2,1,0:T(8,128)} %bitcast.84, s32[4]{0:T(128)S(1)} %fusion.31), kind=kCustom, calls=%fused_computation.1 | custom fusion | bytes 131104 | tf_op jit(solution)/shard_map/gather | solution.py:335
  99.5 2.5 %collective-permute-done.5.p1 = f32[32,32,128]{2,1,0:T(8,128)S(1)} collective-permute-done((f32[32,32,128]{2,1,0:T(8,128)}, f32[32,32,128]{2,1,0:T(8,128)S(1)}, u32[]{:S(2)}, u32[]{:S(2)}) %collective-permute-start.5) | collective-permute-done | bytes 524320 | tf_op jit(solution)/shard_map/ppermute | solution.py:27
  102.0 14.7 %collective-permute-done.6.p2 = f32[32,32,128]{2,1,0:T(8,128)S(1)} collective-permute-done((f32[32,32,128]{2,1,0:T(8,128)S(1)}, f32[32,32,128]{2,1,0:T(8,128)S(1)}, u32[]{:S(2)}, u32[]{:S(2)}) %collective-permute-start.6) | collective-permute-done | bytes 524320 | tf_op jit(solution)/shard_map/ppermute | solution.py:27
  116.7 10.8 %collective-permute-done.7.p3 = f32[32,32,128]{2,1,0:T(8,128)S(1)} collective-permute-done((f32[32,32,128]{2,1,0:T(8,128)S(1)}, f32[32,32,128]{2,1,0:T(8,128)S(1)}, u32[]{:S(2)}, u32[]{:S(2)}) %collective-permute-start.7) | collective-permute-done | bytes 524320 | tf_op jit(solution)/shard_map/ppermute | solution.py:27
  127.4 2.6 %join_columns.1 = f32[32,128,128]{2,1,0:T(8,128)} custom-call(s32[1]{0:T(128)} %bitcast.place, f32[32,32,128]{2,1,0:T(8,128)S(1)} %copy-done.1, f32[32,32,128]{2,1,0:T(8,128)S(1)} %collective-permute-done.5.p1, f32[32,32,128]{2,1,0:T(8,128)S(1)} %collective-permute-done.6.p2, f32[32,32,128]{2,1,0:T(8,128)S(1)} %collective-permute-done.7.p3, ...), custom_call_target="tpu_custom_call" | custom-call | tf_op jit(solution)/shard_map/join_columns/pallas_call | solution.py:152
  (85 shorter events, 7.6 us)
Async XLA Ops:
  1.8 6.3 %collective-permute-start = (f32[101,128]{1,0:T(8,128)}, f32[101,128]{1,0:T(8,128)S(1)}, u32[]{:S(2)}, u32[]{:S(2)}) collective-permute-start(f32[101,128]{1,0:T(8,128)} %get-tuple-element.29), channel_id=1, source_target_pairs={{0,2},{1,3},{2,0},{3,1},{4,6},{5,7},{6,4},{7,5},{8,10},{9,11},{10,... | collective-permute-start | bytes 155144 | tf_op jit(solution)/shard_map/ppermute | solution.py:27
  4.4 16.4 %copy-start.3 = (s32[1,1,128,128]{3,2,1,0:T(8,128)S(1)}, s32[1,1,128,128]{3,2,1,0:T(8,128)}, u32[]{:S(2)}) copy-start(s32[1,1,128,128]{3,2,1,0:T(8,128)} %param.11) | copy-start | bytes 196612
  4.4 16.4 %copy-start.4 = (f32[1,1,128,128]{3,2,1,0:T(8,128)S(1)}, f32[1,1,128,128]{3,2,1,0:T(8,128)}, u32[]{:S(2)}) copy-start(f32[1,1,128,128]{3,2,1,0:T(8,128)} %param.10) | copy-start | bytes 196612
  7.7 38.8 %collective-permute-start.2 = (f32[16,32,128]{2,1,0:T(8,128)}, f32[16,32,128]{2,1,0:T(8,128)S(1)}, u32[]{:S(2)}, u32[]{:S(2)}) collective-permute-start(f32[16,32,128]{2,1,0:T(8,128)} %get-tuple-element.32), channel_id=1, source_target_pairs={{0,2},{1,3},{2,0},{3,1},{4,6},{5,7},{6,4},{7,5},{8,10},{9,11},{10,... | collective-permute-start | bytes 786440 | tf_op jit(solution)/shard_map/ppermute | solution.py:27
  8.1 30.1 %copy-start.6 = (pred[4]{0:T(512)(128)(4,1)}, pred[4]{0:T(512)(128)(4,1)S(1)}, u32[]{:S(2)}) copy-start(pred[4]{0:T(512)(128)(4,1)S(1)} %get-tuple-element.92) | copy-start | bytes 16
  8.1 30.1 %copy-start.8 = (pred[4]{0:T(512)(128)(4,1)}, pred[4]{0:T(512)(128)(4,1)S(1)}, u32[]{:S(2)}) copy-start(pred[4]{0:T(512)(128)(4,1)S(1)} %get-tuple-element.93) | copy-start | bytes 16
  8.7 18.5 %copy-start.10 = (s32[1,1,128]{2,1,0:T(1,128)S(1)}, s32[1,1,128]{2,1,0:T(1,128)}, u32[]{:S(2)}) copy-start(s32[1,1,128]{2,1,0:T(1,128)} %param.12) | copy-start | bytes 1540
  8.7 18.7 %copy-start.5 = (f32[1,1,64,64]{3,2,1,0:T(8,128)S(1)}, f32[1,1,64,64]{3,2,1,0:T(8,128)}, u32[]{:S(2)}) copy-start(f32[1,1,64,64]{3,2,1,0:T(8,128)} %param.14) | copy-start | bytes 49156
  11.1 15.9 %all-to-all-start = ((f32[4,129,128]{2,1,0:T(8,128)}), f32[4,129,128]{2,1,0:T(8,128)S(1)}, u32[]{:S(2)}, u32[]{:S(2)}) async-start(f32[4,129,128]{2,1,0:T(8,128)} %side_borders.1), calls=%async_computation | async-start | bytes 557056 | tf_op jit(solution)/shard_map/all_to_all | solution.py:23
  16.4 49.2 %collective-permute-start.1 = (f32[34,32,128]{2,1,0:T(8,128)}, f32[34,32,128]{2,1,0:T(8,128)S(1)}, u32[]{:S(2)}, u32[]{:S(2)}) collective-permute-start(f32[34,32,128]{2,1,0:T(8,128)} %get-tuple-element.31), channel_id=1, source_target_pairs={{0,1},{1,0},{2,3},{3,2},{4,5},{5,4},{6,7},{7,6},{8,9},{9,8},{10,11... | collective-permute-start | bytes 1671176 | tf_op jit(solution)/shard_map/ppermute | solution.py:27
  16.5 49.2 %collective-permute-start.3 = (f32[34,32,128]{2,1,0:T(8,128)}, f32[34,32,128]{2,1,0:T(8,128)S(1)}, u32[]{:S(2)}, u32[]{:S(2)}) collective-permute-start(f32[34,32,128]{2,1,0:T(8,128)} %get-tuple-element.33), channel_id=1, source_target_pairs={{0,3},{1,2},{2,1},{3,0},{4,7},{5,6},{6,5},{7,4},{8,11},{9,10},{10,... | collective-permute-start | bytes 1671176 | tf_op jit(solution)/shard_map/ppermute | solution.py:27
  19.4 43.4 %collective-permute-start.4 = (f32[18,32,128]{2,1,0:T(8,128)}, f32[18,32,128]{2,1,0:T(8,128)S(1)}, u32[]{:S(2)}, u32[]{:S(2)}) collective-permute-start(f32[18,32,128]{2,1,0:T(8,128)} %get-tuple-element.34), channel_id=1, source_target_pairs={{0,2},{1,3},{2,0},{3,1},{4,6},{5,7},{6,4},{7,5},{8,10},{9,11},{10,... | collective-permute-start | bytes 884744 | tf_op jit(solution)/shard_map/ppermute | solution.py:27
  27.0 38.7 %copy-start = (f32[34,32,128]{2,1,0:T(8,128)S(1)}, f32[34,32,128]{2,1,0:T(8,128)}, u32[]{:S(2)}) copy-start(f32[34,32,128]{2,1,0:T(8,128)} %get-tuple-element.25.p0) | copy-start | bytes 1671172
  27.0 38.7 %copy-start.2 = (f32[101,128]{1,0:T(8,128)S(1)}, f32[101,128]{1,0:T(8,128)}, u32[]{:S(2)}) copy-start(f32[101,128]{1,0:T(8,128)} %get-tuple-element.35.my_pack) | copy-start | bytes 155140
  39.6 26.0 %all-to-all-start.1 = ((f32[4,48,128]{2,1,0:T(8,128)}), f32[4,48,128]{2,1,0:T(8,128)S(1)}, u32[]{:S(2)}, u32[]{:S(2)}) async-start(f32[4,48,128]{2,1,0:T(8,128)} %pad_maximum_fusion.1), calls=%async_computation.1 | async-start | bytes 196608 | tf_op jit(solution)/shard_map/all_to_all | solution.py:23
  72.1 27.2 %copy-start.7 = (pred[4]{0:T(512)(128)(4,1)S(1)}, pred[4]{0:T(512)(128)(4,1)}, u32[]{:S(2)}) copy-start(pred[4]{0:T(512)(128)(4,1)} %copy-done.6) | copy-start | bytes 16
  72.1 27.2 %copy-start.9 = (pred[4]{0:T(512)(128)(4,1)S(1)}, pred[4]{0:T(512)(128)(4,1)}, u32[]{:S(2)}) copy-start(pred[4]{0:T(512)(128)(4,1)} %copy-done.8) | copy-start | bytes 16
  72.1 55.3 %copy-start.1 = (f32[32,32,128]{2,1,0:T(8,128)S(1)}, f32[32,32,128]{2,1,0:T(8,128)}, u32[]{:S(2)}) copy-start(f32[32,32,128]{2,1,0:T(8,128)} %get-tuple-element.40.p0) | copy-start | bytes 1572868
  72.1 11.9 %all-to-all-start.2 = ((f32[4,80,128]{2,1,0:T(8,128)}), f32[4,80,128]{2,1,0:T(8,128)S(1)}, u32[]{:S(2)}, u32[]{:S(2)}) async-start(f32[4,80,128]{2,1,0:T(8,128)} %get-tuple-element.44), calls=%async_computation.2 | async-start | bytes 327680 | tf_op jit(solution)/shard_map/all_to_all | solution.py:23
  78.2 21.2 %copy-start.11 = (f32[128]{0:T(128)S(1)}, f32[128]{0:T(128)}, u32[]{:S(2)}) copy-start(f32[128]{0:T(128)} %get-tuple-element.45) | copy-start | bytes 1540
  78.2 21.2 %copy-start.12 = (f32[128]{0:T(128)S(1)}, f32[128]{0:T(128)}, u32[]{:S(2)}) copy-start(f32[128]{0:T(128)} %get-tuple-element.52) | copy-start | bytes 1540
  78.9 23.1 %collective-permute-start.5 = (f32[32,32,128]{2,1,0:T(8,128)}, f32[32,32,128]{2,1,0:T(8,128)S(1)}, u32[]{:S(2)}, u32[]{:S(2)}) collective-permute-start(f32[32,32,128]{2,1,0:T(8,128)} %get-tuple-element.41), channel_id=1, source_target_pairs={{0,1},{1,0},{2,3},{3,2},{4,5},{5,4},{6,7},{7,6},{8,9},{9,8},{10,11... | collective-permute-start | bytes 1572872 | tf_op jit(solution)/shard_map/ppermute | solution.py:27
  78.9 37.7 %collective-permute-start.6 = (f32[32,32,128]{2,1,0:T(8,128)S(1)}, f32[32,32,128]{2,1,0:T(8,128)S(1)}, u32[]{:S(2)}, u32[]{:S(2)}) collective-permute-start(f32[32,32,128]{2,1,0:T(8,128)S(1)} %get-tuple-element.42), channel_id=1, source_target_pairs={{0,2},{1,3},{2,0},{3,1},{4,6},{5,7},{6,4},{7,5},{8,10},{9,11},{10,... | collective-permute-start | bytes 1572872 | tf_op jit(solution)/shard_map/ppermute | solution.py:27
  81.8 45.6 %collective-permute-start.7 = (f32[32,32,128]{2,1,0:T(8,128)S(1)}, f32[32,32,128]{2,1,0:T(8,128)S(1)}, u32[]{:S(2)}, u32[]{:S(2)}) collective-permute-start(f32[32,32,128]{2,1,0:T(8,128)S(1)} %get-tuple-element.43), channel_id=1, source_target_pairs={{0,3},{1,2},{2,1},{3,0},{4,7},{5,6},{6,5},{7,4},{8,11},{9,10},{10,... | collective-permute-start | bytes 1572872 | tf_op jit(solution)/shard_map/ppermute | solution.py:27
  (3 other events, 24.2 us)

commit v7 on v6

--- a/solution.py
+++ b/solution.py
@@ -317,7 +317,7 @@
     part = pltpu.HBM((width, half, rows), jnp.float32)
     *results, edges = pl.pallas_call(
         steps_kernel,
-        out_shape=[part] * 2 + [pltpu.VMEM((width, half, rows), jnp.float32)] * 2 + [pltpu.VMEM((PARTS, 2 * half + half // 2, rows), jnp.float32)],
+        out_shape=[part] * PARTS + [pltpu.VMEM((PARTS, 2 * half + half // 2, rows), jnp.float32)],
         in_specs=[SMEM] + [VMEM] * 9,
         out_specs=[VMEM] * (PARTS + 1),
         scratch_shapes=[

time: 131 us -> 131 us (level)
  waiting for transfers between devices: 54.6 us -> 60.7 us
  local copies, waits for them, and re-layouts: 6.35 us -> 2.52 us
    ppermute x8, waiting for transfers between devices: 44.2 us -> 49.1 us  [exchanged(): return lax.ppermute(block, Z, [(at, at ^ bits) for at in range(PARTS)])]
    reshape x3, local copies, waits for them, and re-layouts: 1.91 us -> 0.36 us  [on_device(): folded.reshape(PARTS, half // 2, 2, 2, width).transpose(3, 2, 1, 0, 4)]
  transfers between devices with their start and end apart: 11 -> 11, of which waited for: 7 -> 7; matrix products, arithmetic and copies ran while one was open for 8% -> 4% of each run, Pallas kernels for 4% -> 4%
where the time goes in v7:
time: 131 us; the launch traced here: 130 us
  waiting for transfers between devices  60.7 us (46%)
  starting transfers between devices  27.6 us (21%)
  blocking collectives  19.7 us (15%)
  Pallas kernels  16.9 us (13%)
  local copies, waits for them, and re-layouts  2.52 us (2%)
  other arithmetic  2.03 us (2%)
    ppermute x8, waiting for transfers between devices, exchanged(): return lax.ppermute(block, Z, [(at, at ^ bits) for at in range(PARTS)])  49.1 us
    all_gather x2, blocking collectives, tile_halo(): every = lax.all_gather(edges, 'tile', axis=0)  19.7 us
    all_to_all x3, starting transfers between devices, traded(): return lax.all_to_all(blocks, Z, 0, 0)  16.7 us
    all_to_all x3, waiting for transfers between devices, traded(): return lax.all_to_all(blocks, Z, 0, 0)  11.6 us
    ppermute x8, starting transfers between devices, exchanged(): return lax.ppermute(block, Z, [(at, at ^ bits) for at in range(PARTS)])  10.9 us
    pallas_call x1, Pallas kernels, two_steps(): pl.pallas_call(steps_kernel, out_shape=[part] * PARTS + [pltpu.VMEM((PART...  6.81 us
    pallas_call x1, Pallas kernels, split_columns(): pl.pallas_call(split_kernel, grid=(levels // BLOCK,), out_shape=[jax.Shap...  3.3 us
  transfers between devices with their start and end apart: 11, of which 7 were waited for; matrix products, arithmetic and copies ran while one was open for 4% of the time, Pallas kernels for 4%

profile of v7, /device:TPU:8, one launch (start us, length us, event | category | flops | bytes accessed | tf_op | source)
XLA Modules:
  0.0 130.3 jit_solution(6607351527599634277)
XLA Ops:
  0.0 1.8 %parameters.1 = (f32[101,128]{1,0:T(8,128)}, f32[101,128]{1,0:T(8,128)}) custom-call(s32[1]{0:T(128)} %bitcast.place, s32[128,128]{1,0:T(8,128)} %bitcast.86, f32[128,128]{1,0:T(8,128)} %bitcast.89, f32[64,64]{1,0:T(8,128)} %bitcast.92, s32[1,128]{1,0:T(1,128)} %bitcast.94), custom_call_target="tpu_custom_call" | custom-call | tf_op jit(solution)/shard_map/parameters/pallas_call | solution.py:59
  1.8 2.6 %collective-permute-start = (f32[101,128]{1,0:T(8,128)}, f32[101,128]{1,0:T(8,128)S(1)}, u32[]{:S(2)}, u32[]{:S(2)}) collective-permute-start(f32[101,128]{1,0:T(8,128)} %get-tuple-element.29), channel_id=1, source_target_pairs={{0,2},{1,3},{2,0},{3,1},{4,6},{5,7},{6,4},{7,5},{8,10},{9,11},{10,... | collective-permute-start | bytes 155144 | tf_op jit(solution)/shard_map/ppermute | solution.py:27
  4.4 3.3 %split_columns.1 = (f32[34,32,128]{2,1,0:T(8,128)}, f32[34,32,128]{2,1,0:T(8,128)}, f32[16,32,128]{2,1,0:T(8,128)}, f32[34,32,128]{2,1,0:T(8,128)}, f32[18,32,128]{2,1,0:T(8,128)}, /*index=5*/f32[2,32,128]{2,1,0:T(8,128)}) custom-call(s32[1]{0:T(128)} %bitcast.place, f32[32,128,128]{2,1,0:T(8,128)} %bitcast.80), custom_call_target="tpu_custom_call" | custom-call | tf_op jit(solution)/shard_map/split_columns/pallas_call | solution.py:87
  8.1 0.6 fusion.30.lent_rows
  8.7 2.4 %side_borders.1 = f32[4,129,128]{2,1,0:T(8,128)} custom-call(s32[1]{0:T(128)} %bitcast.place, s32[128]{0:T(128)} %fusion.30.lent_rows, f32[32,128,128]{2,1,0:T(8,128)} %bitcast.81, f32[2,32,128]{2,1,0:T(8,128)} %get-tuple-element.30.ends, f32[1,32]{1,0:T(1,128)} %gain.1), custom_call_target="tpu_custom_call" | custom-call | tf_op jit(solution)/shard_map/side_borders/pallas_call | solution.py:121
  11.0 5.3 %all-to-all-start = ((f32[4,129,128]{2,1,0:T(8,128)}), f32[4,129,128]{2,1,0:T(8,128)S(1)}, u32[]{:S(2)}, u32[]{:S(2)}) async-start(f32[4,129,128]{2,1,0:T(8,128)} %side_borders.1), calls=%async_computation | async-start | bytes 557056 | tf_op jit(solution)/shard_map/all_to_all | solution.py:23
  16.4 2.9 %collective-permute-start.3 = (f32[34,32,128]{2,1,0:T(8,128)}, f32[34,32,128]{2,1,0:T(8,128)S(1)}, u32[]{:S(2)}, u32[]{:S(2)}) collective-permute-start(f32[34,32,128]{2,1,0:T(8,128)} %get-tuple-element.33), channel_id=1, source_target_pairs={{0,3},{1,2},{2,1},{3,0},{4,7},{5,6},{6,5},{7,4},{8,11},{9,10},{10,... | collective-permute-start | bytes 1671176 | tf_op jit(solution)/shard_map/ppermute | solution.py:27
  19.3 1.5 %collective-permute-start.4 = (f32[18,32,128]{2,1,0:T(8,128)}, f32[18,32,128]{2,1,0:T(8,128)S(1)}, u32[]{:S(2)}, u32[]{:S(2)}) collective-permute-start(f32[18,32,128]{2,1,0:T(8,128)} %get-tuple-element.34), channel_id=1, source_target_pairs={{0,2},{1,3},{2,0},{3,1},{4,6},{5,7},{6,4},{7,5},{8,10},{9,11},{10,... | collective-permute-start | bytes 884744 | tf_op jit(solution)/shard_map/ppermute | solution.py:27
  21.0 5.9 %all-to-all-done = f32[4,129,128]{2,1,0:T(8,128)S(1)} async-done(((f32[4,129,128]{2,1,0:T(8,128)}), f32[4,129,128]{2,1,0:T(8,128)S(1)}, u32[]{:S(2)}, u32[]{:S(2)}) %all-to-all-start) | async-done | bytes 264224 | tf_op jit(solution)/shard_map/all_to_all | solution.py:23
  27.7 9.9 %all-gather = f32[32,32,128]{2,1,0:T(8,128)S(1)} all-gather(f32[4,32,128]{2,1,0:T(8,128)S(1)} %fusion), channel_id=2, replica_groups=mesh['tile'=8,'sect'=2,'lev'=2] {'tile'}, dimensions={0}, use_global_device_ids=true | all-gather | bytes 589824 | tf_op jit(solution)/shard_map/all_gather | solution.py:334
  38.9 0.6 pad_maximum_fusion.1
  39.6 6.2 %all-to-all-start.1 = ((f32[4,48,128]{2,1,0:T(8,128)}), f32[4,48,128]{2,1,0:T(8,128)S(1)}, u32[]{:S(2)}, u32[]{:S(2)}) async-start(f32[4,48,128]{2,1,0:T(8,128)} %pad_maximum_fusion.1), calls=%async_computation.1 | async-start | bytes 196608 | tf_op jit(solution)/shard_map/all_to_all | solution.py:23
  45.8 16.9 %collective-permute-done.4.q2 = f32[18,32,128]{2,1,0:T(8,128)S(1)} collective-permute-done((f32[18,32,128]{2,1,0:T(8,128)}, f32[18,32,128]{2,1,0:T(8,128)S(1)}, u32[]{:S(2)}, u32[]{:S(2)}) %collective-permute-start.4) | collective-permute-done | bytes 294944 | tf_op jit(solution)/shard_map/ppermute | solution.py:27
  62.8 2.8 %all-to-all-done.1.halos = f32[4,48,128]{2,1,0:T(8,128)S(1)} async-done(((f32[4,48,128]{2,1,0:T(8,128)}), f32[4,48,128]{2,1,0:T(8,128)S(1)}, u32[]{:S(2)}, u32[]{:S(2)}) %all-to-all-start.1) | async-done | bytes 98336 | tf_op jit(solution)/shard_map/all_to_all | solution.py:23
  65.6 6.8 %two_steps.1 = (f32[32,32,128]{2,1,0:T(8,128)}, f32[32,32,128]{2,1,0:T(8,128)}, f32[32,32,128]{2,1,0:T(8,128)}, f32[32,32,128]{2,1,0:T(8,128)}, f32[4,80,128]{2,1,0:T(8,128)}) custom-call(s32[1]{0:T(128)} %bitcast.place, f32[34,32,128]{2,1,0:T(8,128)S(1)} %copy-done, f32[34,32,128]{2,1,0:T(8,128)S(1)} %collective-permute-done.1.p1, ...), custom_call_target="tpu_custom_call" | custom-call | tf_op jit(solution)/shard_map/two_steps/pallas_call | solution.py:318
  72.4 5.2 %all-to-all-start.2 = ((f32[4,80,128]{2,1,0:T(8,128)}), f32[4,80,128]{2,1,0:T(8,128)S(1)}, u32[]{:S(2)}, u32[]{:S(2)}) async-start(f32[4,80,128]{2,1,0:T(8,128)} %get-tuple-element.44), calls=%async_computation.2 | async-start | bytes 327680 | tf_op jit(solution)/shard_map/all_to_all | solution.py:23
  78.1 2.9 %collective-permute-start.6 = (f32[32,32,128]{2,1,0:T(8,128)}, f32[32,32,128]{2,1,0:T(8,128)S(1)}, u32[]{:S(2)}, u32[]{:S(2)}) collective-permute-start(f32[32,32,128]{2,1,0:T(8,128)} %get-tuple-element.42), channel_id=1, source_target_pairs={{0,2},{1,3},{2,0},{3,1},{4,6},{5,7},{6,4},{7,5},{8,10},{9,11},{10,... | collective-permute-start | bytes 1572872 | tf_op jit(solution)/shard_map/ppermute | solution.py:27
  81.0 0.6 collective-permute-start.7
  81.5 2.9 %all-to-all-done.2 = f32[4,80,128]{2,1,0:T(8,128)S(1)} async-done(((f32[4,80,128]{2,1,0:T(8,128)}), f32[4,80,128]{2,1,0:T(8,128)S(1)}, u32[]{:S(2)}, u32[]{:S(2)}) %all-to-all-start.2) | async-done | bytes 163872 | tf_op jit(solution)/shard_map/all_to_all | solution.py:23
  84.8 9.9 %all-gather.1 = f32[32,32,128]{2,1,0:T(8,128)S(1)} all-gather(f32[4,32,128]{2,1,0:T(8,128)S(1)} %pad_maximum_fusion.2), channel_id=3, replica_groups=mesh['tile'=8,'sect'=2,'lev'=2] {'tile'}, dimensions={0}, use_global_device_ids=true | all-gather | bytes 589824 | tf_op jit(solution)/shard_map/all_gather | solution.py:334
  95.5 5.9 %collective-permute-done.5.p1 = f32[32,32,128]{2,1,0:T(8,128)S(1)} collective-permute-done((f32[32,32,128]{2,1,0:T(8,128)}, f32[32,32,128]{2,1,0:T(8,128)S(1)}, u32[]{:S(2)}, u32[]{:S(2)}) %collective-permute-start.5) | collective-permute-done | bytes 524320 | tf_op jit(solution)/shard_map/ppermute | solution.py:27
  101.4 14.7 %collective-permute-done.6.p2 = f32[32,32,128]{2,1,0:T(8,128)S(1)} collective-permute-done((f32[32,32,128]{2,1,0:T(8,128)}, f32[32,32,128]{2,1,0:T(8,128)S(1)}, u32[]{:S(2)}, u32[]{:S(2)}) %collective-permute-start.6) | collective-permute-done | bytes 524320 | tf_op jit(solution)/shard_map/ppermute | solution.py:27
  116.1 11.6 %collective-permute-done.7.p3 = f32[32,32,128]{2,1,0:T(8,128)S(1)} collective-permute-done((f32[32,32,128]{2,1,0:T(8,128)}, f32[32,32,128]{2,1,0:T(8,128)S(1)}, u32[]{:S(2)}, u32[]{:S(2)}) %collective-permute-start.7) | collective-permute-done | bytes 524320 | tf_op jit(solution)/shard_map/ppermute | solution.py:27
  127.7 2.6 %join_columns.1 = f32[32,128,128]{2,1,0:T(8,128)} custom-call(s32[1]{0:T(128)} %bitcast.place, f32[32,32,128]{2,1,0:T(8,128)S(1)} %copy-done.1, f32[32,32,128]{2,1,0:T(8,128)S(1)} %collective-permute-done.5.p1, f32[32,32,128]{2,1,0:T(8,128)S(1)} %collective-permute-done.6.p2, f32[32,32,128]{2,1,0:T(8,128)S(1)} %collective-permute-done.7.p3, ...), custom_call_target="tpu_custom_call" | custom-call | tf_op jit(solution)/shard_map/join_columns/pallas_call | solution.py:152
  (73 shorter events, 4.3 us)
Async XLA Ops:
  0.0 8.0 %copy-start.8 = (s32[1,4]{1,0:T(1,128)S(1)}, s32[1,4]{1,0:T(1,128)}, u32[]{:S(2)}) copy-start(s32[1,4]{1,0:T(1,128)} %param.15) | copy-start | bytes 52
  0.0 8.0 %copy-start.7 = (s32[1,4]{1,0:T(1,128)S(1)}, s32[1,4]{1,0:T(1,128)}, u32[]{:S(2)}) copy-start(s32[1,4]{1,0:T(1,128)} %param.17) | copy-start | bytes 52
  0.0 8.1 %copy-start.9 = (s32[1,4]{1,0:T(1,128)S(1)}, s32[1,4]{1,0:T(1,128)}, u32[]{:S(2)}) copy-start(s32[1,4]{1,0:T(1,128)} %param.16) | copy-start | bytes 52
  1.8 6.3 %collective-permute-start = (f32[101,128]{1,0:T(8,128)}, f32[101,128]{1,0:T(8,128)S(1)}, u32[]{:S(2)}, u32[]{:S(2)}) collective-permute-start(f32[101,128]{1,0:T(8,128)} %get-tuple-element.29), channel_id=1, source_target_pairs={{0,2},{1,3},{2,0},{3,1},{4,6},{5,7},{6,4},{7,5},{8,10},{9,11},{10,... | collective-permute-start | bytes 155144 | tf_op jit(solution)/shard_map/ppermute | solution.py:27
  4.4 16.4 %copy-start.3 = (s32[1,1,128,128]{3,2,1,0:T(8,128)S(1)}, s32[1,1,128,128]{3,2,1,0:T(8,128)}, u32[]{:S(2)}) copy-start(s32[1,1,128,128]{3,2,1,0:T(8,128)} %param.11) | copy-start | bytes 196612
  4.4 16.4 %copy-start.4 = (f32[1,1,128,128]{3,2,1,0:T(8,128)S(1)}, f32[1,1,128,128]{3,2,1,0:T(8,128)}, u32[]{:S(2)}) copy-start(f32[1,1,128,128]{3,2,1,0:T(8,128)} %param.10) | copy-start | bytes 196612
  7.7 38.1 %collective-permute-start.2 = (f32[16,32,128]{2,1,0:T(8,128)}, f32[16,32,128]{2,1,0:T(8,128)S(1)}, u32[]{:S(2)}, u32[]{:S(2)}) collective-permute-start(f32[16,32,128]{2,1,0:T(8,128)} %get-tuple-element.32), channel_id=1, source_target_pairs={{0,2},{1,3},{2,0},{3,1},{4,6},{5,7},{6,4},{7,5},{8,10},{9,11},{10,... | collective-permute-start | bytes 786440 | tf_op jit(solution)/shard_map/ppermute | solution.py:27
  8.7 18.5 %copy-start.6 = (s32[1,1,128]{2,1,0:T(1,128)S(1)}, s32[1,1,128]{2,1,0:T(1,128)}, u32[]{:S(2)}) copy-start(s32[1,1,128]{2,1,0:T(1,128)} %param.12) | copy-start | bytes 1540
  8.7 18.7 %copy-start.5 = (f32[1,1,64,64]{3,2,1,0:T(8,128)S(1)}, f32[1,1,64,64]{3,2,1,0:T(8,128)}, u32[]{:S(2)}) copy-start(f32[1,1,64,64]{3,2,1,0:T(8,128)} %param.14) | copy-start | bytes 49156
  11.0 15.9 %all-to-all-start = ((f32[4,129,128]{2,1,0:T(8,128)}), f32[4,129,128]{2,1,0:T(8,128)S(1)}, u32[]{:S(2)}, u32[]{:S(2)}) async-start(f32[4,129,128]{2,1,0:T(8,128)} %side_borders.1), calls=%async_computation | async-start | bytes 557056 | tf_op jit(solution)/shard_map/all_to_all | solution.py:23
  16.4 49.2 %collective-permute-start.1 = (f32[34,32,128]{2,1,0:T(8,128)}, f32[34,32,128]{2,1,0:T(8,128)S(1)}, u32[]{:S(2)}, u32[]{:S(2)}) collective-permute-start(f32[34,32,128]{2,1,0:T(8,128)} %get-tuple-element.31), channel_id=1, source_target_pairs={{0,1},{1,0},{2,3},{3,2},{4,5},{5,4},{6,7},{7,6},{8,9},{9,8},{10,11... | collective-permute-start | bytes 1671176 | tf_op jit(solution)/shard_map/ppermute | solution.py:27
  16.4 49.2 %collective-permute-start.3 = (f32[34,32,128]{2,1,0:T(8,128)}, f32[34,32,128]{2,1,0:T(8,128)S(1)}, u32[]{:S(2)}, u32[]{:S(2)}) collective-permute-start(f32[34,32,128]{2,1,0:T(8,128)} %get-tuple-element.33), channel_id=1, source_target_pairs={{0,3},{1,2},{2,1},{3,0},{4,7},{5,6},{6,5},{7,4},{8,11},{9,10},{10,... | collective-permute-start | bytes 1671176 | tf_op jit(solution)/shard_map/ppermute | solution.py:27
  19.3 43.5 %collective-permute-start.4 = (f32[18,32,128]{2,1,0:T(8,128)}, f32[18,32,128]{2,1,0:T(8,128)S(1)}, u32[]{:S(2)}, u32[]{:S(2)}) collective-permute-start(f32[18,32,128]{2,1,0:T(8,128)} %get-tuple-element.34), channel_id=1, source_target_pairs={{0,2},{1,3},{2,0},{3,1},{4,6},{5,7},{6,4},{7,5},{8,10},{9,11},{10,... | collective-permute-start | bytes 884744 | tf_op jit(solution)/shard_map/ppermute | solution.py:27
  26.9 38.7 %copy-start = (f32[34,32,128]{2,1,0:T(8,128)S(1)}, f32[34,32,128]{2,1,0:T(8,128)}, u32[]{:S(2)}) copy-start(f32[34,32,128]{2,1,0:T(8,128)} %get-tuple-element.25.p0) | copy-start | bytes 1671172
  26.9 38.7 %copy-start.2 = (f32[101,128]{1,0:T(8,128)S(1)}, f32[101,128]{1,0:T(8,128)}, u32[]{:S(2)}) copy-start(f32[101,128]{1,0:T(8,128)} %get-tuple-element.35.my_pack) | copy-start | bytes 155140
  39.6 26.0 %all-to-all-start.1 = ((f32[4,48,128]{2,1,0:T(8,128)}), f32[4,48,128]{2,1,0:T(8,128)S(1)}, u32[]{:S(2)}, u32[]{:S(2)}) async-start(f32[4,48,128]{2,1,0:T(8,128)} %pad_maximum_fusion.1), calls=%async_computation.1 | async-start | bytes 196608 | tf_op jit(solution)/shard_map/all_to_all | solution.py:23
  72.4 55.3 %copy-start.1 = (f32[32,32,128]{2,1,0:T(8,128)S(1)}, f32[32,32,128]{2,1,0:T(8,128)}, u32[]{:S(2)}) copy-start(f32[32,32,128]{2,1,0:T(8,128)} %get-tuple-element.40.p0) | copy-start | bytes 1572868
  72.4 12.0 %all-to-all-start.2 = ((f32[4,80,128]{2,1,0:T(8,128)}), f32[4,80,128]{2,1,0:T(8,128)S(1)}, u32[]{:S(2)}, u32[]{:S(2)}) async-start(f32[4,80,128]{2,1,0:T(8,128)} %get-tuple-element.44), calls=%async_computation.2 | async-start | bytes 327680 | tf_op jit(solution)/shard_map/all_to_all | solution.py:23
  78.0 23.5 %collective-permute-start.5 = (f32[32,32,128]{2,1,0:T(8,128)}, f32[32,32,128]{2,1,0:T(8,128)S(1)}, u32[]{:S(2)}, u32[]{:S(2)}) collective-permute-start(f32[32,32,128]{2,1,0:T(8,128)} %get-tuple-element.41), channel_id=1, source_target_pairs={{0,1},{1,0},{2,3},{3,2},{4,5},{5,4},{6,7},{7,6},{8,9},{9,8},{10,11... | collective-permute-start | bytes 1572872 | tf_op jit(solution)/shard_map/ppermute | solution.py:27
  78.1 38.1 %collective-permute-start.6 = (f32[32,32,128]{2,1,0:T(8,128)}, f32[32,32,128]{2,1,0:T(8,128)S(1)}, u32[]{:S(2)}, u32[]{:S(2)}) collective-permute-start(f32[32,32,128]{2,1,0:T(8,128)} %get-tuple-element.42), channel_id=1, source_target_pairs={{0,2},{1,3},{2,0},{3,1},{4,6},{5,7},{6,4},{7,5},{8,10},{9,11},{10,... | collective-permute-start | bytes 1572872 | tf_op jit(solution)/shard_map/ppermute | solution.py:27
  81.0 46.7 %collective-permute-start.7 = (f32[32,32,128]{2,1,0:T(8,128)}, f32[32,32,128]{2,1,0:T(8,128)S(1)}, u32[]{:S(2)}, u32[]{:S(2)}) collective-permute-start(f32[32,32,128]{2,1,0:T(8,128)} %get-tuple-element.43), channel_id=1, source_target_pairs={{0,3},{1,2},{2,1},{3,0},{4,7},{5,6},{6,5},{7,4},{8,11},{9,10},{10,... | collective-permute-start | bytes 1572872 | tf_op jit(solution)/shard_map/ppermute | solution.py:27

commit v8 on v5

--- a/solution.py
+++ b/solution.py
@@ -316,7 +316,7 @@
     part = pltpu.HBM((width, half, rows), jnp.float32)
     *results, edges = pl.pallas_call(
         steps_kernel,
-        out_shape=[part] * PARTS + [pltpu.VMEM((PARTS, 2 * half + half // 2, rows), jnp.float32)],
+        out_shape=[part] * 2 + [pltpu.VMEM((width, half, rows), jnp.float32)] * 2 + [pltpu.VMEM((PARTS, 2 * half + half // 2, rows), jnp.float32)],
         in_specs=[SMEM] + [VMEM] * 9,
         out_specs=[VMEM] * (PARTS + 1),
         scratch_shapes=[

time: 130 us -> 130 us (level)
  waiting for transfers between devices: 60.7 us -> 54.7 us
  local copies, waits for them, and re-layouts: 2.52 us -> 6.35 us
    ppermute x8, waiting for transfers between devices: 49.1 us -> 44.2 us  [exchanged(): return lax.ppermute(block, Z, [(at, at ^ bits) for at in range(PARTS)])]
    reshape x3, local copies, waits for them, and re-layouts: 0.36 us -> 1.91 us  [on_device(): folded.reshape(PARTS, half // 2, 2, 2, width).transpose(3, 2, 1, 0, 4)]
  transfers between devices with their start and end apart: 11 -> 11, of which waited for: 7 -> 7; matrix products, arithmetic and copies ran while one was open for 4% -> 8% of each run, Pallas kernels for 4% -> 4%
where the time goes in v8:
time: 130 us
  waiting for transfers between devices  54.7 us (42%)
  starting transfers between devices  27.5 us (21%)
  blocking collectives  20.8 us (16%)
  Pallas kernels  16 us (12%)
  local copies, waits for them, and re-layouts  6.35 us (5%)
  other arithmetic  3.29 us (3%)
    ppermute x8, waiting for transfers between devices, exchanged(): return lax.ppermute(block, Z, [(at, at ^ bits) for at in range(PARTS)])  44.2 us
    all_gather x2, blocking collectives, tile_halo(): every = lax.all_gather(edges, 'tile', axis=0)  20.8 us
    all_to_all x3, starting transfers between devices, traded(): return lax.all_to_all(blocks, Z, 0, 0)  16.7 us
    ppermute x8, starting transfers between devices, exchanged(): return lax.ppermute(block, Z, [(at, at ^ bits) for at in range(PARTS)])  10.8 us
    all_to_all x3, waiting for transfers between devices, traded(): return lax.all_to_all(blocks, Z, 0, 0)  10.4 us
    pallas_call x1, Pallas kernels, two_steps(): pl.pallas_call(steps_kernel, out_shape=[part] * 2 + [pltpu.VMEM((width, h...  6.48 us
    pallas_call x1, Pallas kernels, split_columns(): pl.pallas_call(split_kernel, grid=(levels // BLOCK,), out_shape=[jax.Shap...  3.32 us
  transfers between devices with their start and end apart: 11, of which 7 were waited for; matrix products, arithmetic and copies ran while one was open for 8% of the time, Pallas kernels for 4%

profile of v8, /device:TPU:8, one launch (start us, length us, event | category | flops | bytes accessed | tf_op | source)
XLA Modules:
  0.0 129.5 jit_solution(12183471641062951361)
XLA Ops:
  0.0 1.8 %parameters.1 = (f32[101,128]{1,0:T(8,128)}, f32[101,128]{1,0:T(8,128)}) custom-call(s32[1]{0:T(128)} %bitcast.place, s32[128,128]{1,0:T(8,128)} %bitcast.86, f32[128,128]{1,0:T(8,128)} %bitcast.89, f32[64,64]{1,0:T(8,128)} %bitcast.92, s32[1,128]{1,0:T(1,128)} %bitcast.94), custom_call_target="tpu_custom_call" | custom-call | tf_op jit(solution)/shard_map/parameters/pallas_call | solution.py:58
  1.8 2.6 %collective-permute-start = (f32[101,128]{1,0:T(8,128)}, f32[101,128]{1,0:T(8,128)S(1)}, u32[]{:S(2)}, u32[]{:S(2)}) collective-permute-start(f32[101,128]{1,0:T(8,128)} %get-tuple-element.29), channel_id=1, source_target_pairs={{0,2},{1,3},{2,0},{3,1},{4,6},{5,7},{6,4},{7,5},{8,10},{9,11},{10,... | collective-permute-start | bytes 155144 | tf_op jit(solution)/shard_map/ppermute | solution.py:26
  4.4 3.3 %split_columns.1 = (f32[34,32,128]{2,1,0:T(8,128)}, f32[34,32,128]{2,1,0:T(8,128)}, f32[16,32,128]{2,1,0:T(8,128)}, f32[34,32,128]{2,1,0:T(8,128)}, f32[18,32,128]{2,1,0:T(8,128)}, /*index=5*/f32[2,32,128]{2,1,0:T(8,128)}) custom-call(s32[1]{0:T(128)} %bitcast.place, f32[32,128,128]{2,1,0:T(8,128)} %bitcast.80), custom_call_target="tpu_custom_call" | custom-call | tf_op jit(solution)/shard_map/split_columns/pallas_call | solution.py:86
  8.7 2.4 %side_borders.1 = f32[4,129,128]{2,1,0:T(8,128)} custom-call(s32[1]{0:T(128)} %bitcast.place, s32[128]{0:T(128)} %fusion.30.lent_rows, f32[32,128,128]{2,1,0:T(8,128)} %bitcast.81, f32[2,32,128]{2,1,0:T(8,128)} %get-tuple-element.30.ends, f32[1,32]{1,0:T(1,128)} %gain.1), custom_call_target="tpu_custom_call" | custom-call | tf_op jit(solution)/shard_map/side_borders/pallas_call | solution.py:120
  11.1 5.3 %all-to-all-start = ((f32[4,129,128]{2,1,0:T(8,128)}), f32[4,129,128]{2,1,0:T(8,128)S(1)}, u32[]{:S(2)}, u32[]{:S(2)}) async-start(f32[4,129,128]{2,1,0:T(8,128)} %side_borders.1), calls=%async_computation | async-start | bytes 557056 | tf_op jit(solution)/shard_map/all_to_all | solution.py:22
  16.4 2.9 %collective-permute-start.3 = (f32[34,32,128]{2,1,0:T(8,128)}, f32[34,32,128]{2,1,0:T(8,128)S(1)}, u32[]{:S(2)}, u32[]{:S(2)}) collective-permute-start(f32[34,32,128]{2,1,0:T(8,128)} %get-tuple-element.33), channel_id=1, source_target_pairs={{0,3},{1,2},{2,1},{3,0},{4,7},{5,6},{6,5},{7,4},{8,11},{9,10},{10,... | collective-permute-start | bytes 1671176 | tf_op jit(solution)/shard_map/ppermute | solution.py:26
  19.3 1.5 %collective-permute-start.4 = (f32[18,32,128]{2,1,0:T(8,128)}, f32[18,32,128]{2,1,0:T(8,128)S(1)}, u32[]{:S(2)}, u32[]{:S(2)}) collective-permute-start(f32[18,32,128]{2,1,0:T(8,128)} %get-tuple-element.34), channel_id=1, source_target_pairs={{0,2},{1,3},{2,0},{3,1},{4,6},{5,7},{6,4},{7,5},{8,10},{9,11},{10,... | collective-permute-start | bytes 884744 | tf_op jit(solution)/shard_map/ppermute | solution.py:26
  21.0 5.9 %all-to-all-done = f32[4,129,128]{2,1,0:T(8,128)S(1)} async-done(((f32[4,129,128]{2,1,0:T(8,128)}), f32[4,129,128]{2,1,0:T(8,128)S(1)}, u32[]{:S(2)}, u32[]{:S(2)}) %all-to-all-start) | async-done | bytes 264224 | tf_op jit(solution)/shard_map/all_to_all | solution.py:22
  27.7 9.9 %all-gather = f32[32,32,128]{2,1,0:T(8,128)S(1)} all-gather(f32[4,32,128]{2,1,0:T(8,128)S(1)} %fusion), channel_id=2, replica_groups=mesh['tile'=8,'sect'=2,'lev'=2] {'tile'}, dimensions={0}, use_global_device_ids=true | all-gather | bytes 589824 | tf_op jit(solution)/shard_map/all_gather | solution.py:333
  39.6 6.2 %all-to-all-start.1 = ((f32[4,48,128]{2,1,0:T(8,128)}), f32[4,48,128]{2,1,0:T(8,128)S(1)}, u32[]{:S(2)}, u32[]{:S(2)}) async-start(f32[4,48,128]{2,1,0:T(8,128)} %pad_maximum_fusion.1), calls=%async_computation.1 | async-start | bytes 196608 | tf_op jit(solution)/shard_map/all_to_all | solution.py:22
  46.5 16.3 %collective-permute-done.4.q2 = f32[18,32,128]{2,1,0:T(8,128)S(1)} collective-permute-done((f32[18,32,128]{2,1,0:T(8,128)}, f32[18,32,128]{2,1,0:T(8,128)S(1)}, u32[]{:S(2)}, u32[]{:S(2)}) %collective-permute-start.4) | collective-permute-done | bytes 294944 | tf_op jit(solution)/shard_map/ppermute | solution.py:26
  62.8 2.8 %all-to-all-done.1.halos = f32[4,48,128]{2,1,0:T(8,128)S(1)} async-done(((f32[4,48,128]{2,1,0:T(8,128)}), f32[4,48,128]{2,1,0:T(8,128)S(1)}, u32[]{:S(2)}, u32[]{:S(2)}) %all-to-all-start.1) | async-done | bytes 98336 | tf_op jit(solution)/shard_map/all_to_all | solution.py:22
  65.6 6.5 %two_steps.1 = (f32[32,32,128]{2,1,0:T(8,128)}, f32[32,32,128]{2,1,0:T(8,128)}, f32[32,32,128]{2,1,0:T(8,128)S(1)}, f32[32,32,128]{2,1,0:T(8,128)S(1)}, f32[4,80,128]{2,1,0:T(8,128)}) custom-call(s32[1]{0:T(128)} %bitcast.place, f32[34,32,128]{2,1,0:T(8,128)S(1)} %copy-done, f32[34,32,128]{2,1,0:T(8,128)S(1)} %collective-permute-done.1.p1, ...), custom_call_target="tpu_custom_call" | custom-call | tf_op jit(solution)/shard_map/two_steps/pallas_call | solution.py:317
  72.1 5.2 %all-to-all-start.2 = ((f32[4,80,128]{2,1,0:T(8,128)}), f32[4,80,128]{2,1,0:T(8,128)S(1)}, u32[]{:S(2)}, u32[]{:S(2)}) async-start(f32[4,80,128]{2,1,0:T(8,128)} %get-tuple-element.44), calls=%async_computation.2 | async-start | bytes 327680 | tf_op jit(solution)/shard_map/all_to_all | solution.py:22
  77.3 0.9 slice_reduce_fusion.7
  78.9 2.9 %collective-permute-start.6 = (f32[32,32,128]{2,1,0:T(8,128)S(1)}, f32[32,32,128]{2,1,0:T(8,128)S(1)}, u32[]{:S(2)}, u32[]{:S(2)}) collective-permute-start(f32[32,32,128]{2,1,0:T(8,128)S(1)} %get-tuple-element.42), channel_id=1, source_target_pairs={{0,2},{1,3},{2,0},{3,1},{4,6},{5,7},{6,4},{7,5},{8,10},{9,11},{10,... | collective-permute-start | bytes 1572872 | tf_op jit(solution)/shard_map/ppermute | solution.py:26
  82.4 1.7 %all-to-all-done.2 = f32[4,80,128]{2,1,0:T(8,128)S(1)} async-done(((f32[4,80,128]{2,1,0:T(8,128)}), f32[4,80,128]{2,1,0:T(8,128)S(1)}, u32[]{:S(2)}, u32[]{:S(2)}) %all-to-all-start.2) | async-done | bytes 163872 | tf_op jit(solution)/shard_map/all_to_all | solution.py:22
  84.9 1.0 reshape.167
  86.7 10.9 %all-gather.1 = f32[32,32,128]{2,1,0:T(8,128)} all-gather(f32[4,32,128]{2,1,0:T(8,128)S(1)} %pad_maximum_fusion.2), channel_id=3, replica_groups=mesh['tile'=8,'sect'=2,'lev'=2] {'tile'}, dimensions={0}, use_global_device_ids=true | all-gather | bytes 589824 | tf_op jit(solution)/shard_map/all_gather | solution.py:333
  97.6 1.6 %gather_fusion.1 = f32[4,32,128]{2,1,0:T(8,128)S(1)} fusion(f32[8,4,32,128]{3,2,1,0:T(8,128)} %bitcast.84, s32[4]{0:T(128)S(1)} %fusion.31), kind=kCustom, calls=%fused_computation.1 | custom fusion | bytes 131104 | tf_op jit(solution)/shard_map/gather | solution.py:334
  99.5 2.5 %collective-permute-done.5.p1 = f32[32,32,128]{2,1,0:T(8,128)S(1)} collective-permute-done((f32[32,32,128]{2,1,0:T(8,128)}, f32[32,32,128]{2,1,0:T(8,128)S(1)}, u32[]{:S(2)}, u32[]{:S(2)}) %collective-permute-start.5) | collective-permute-done | bytes 524320 | tf_op jit(solution)/shard_map/ppermute | solution.py:26
  102.0 14.7 %collective-permute-done.6.p2 = f32[32,32,128]{2,1,0:T(8,128)S(1)} collective-permute-done((f32[32,32,128]{2,1,0:T(8,128)S(1)}, f32[32,32,128]{2,1,0:T(8,128)S(1)}, u32[]{:S(2)}, u32[]{:S(2)}) %collective-permute-start.6) | collective-permute-done | bytes 524320 | tf_op jit(solution)/shard_map/ppermute | solution.py:26
  116.7 10.8 %collective-permute-done.7.p3 = f32[32,32,128]{2,1,0:T(8,128)S(1)} collective-permute-done((f32[32,32,128]{2,1,0:T(8,128)S(1)}, f32[32,32,128]{2,1,0:T(8,128)S(1)}, u32[]{:S(2)}, u32[]{:S(2)}) %collective-permute-start.7) | collective-permute-done | bytes 524320 | tf_op jit(solution)/shard_map/ppermute | solution.py:26
  127.4 2.1 %join_columns.1 = f32[32,128,128]{2,1,0:T(8,128)} custom-call(s32[1]{0:T(128)} %bitcast.place, f32[32,32,128]{2,1,0:T(8,128)S(1)} %copy-done.1, f32[32,32,128]{2,1,0:T(8,128)S(1)} %collective-permute-done.5.p1, f32[32,32,128]{2,1,0:T(8,128)S(1)} %collective-permute-done.6.p2, f32[32,32,128]{2,1,0:T(8,128)S(1)} %collective-permute-done.7.p3, ...), custom_call_target="tpu_custom_call" | custom-call | tf_op jit(solution)/shard_map/join_columns/pallas_call | solution.py:151
  (85 shorter events, 7.6 us)
Async XLA Ops:
  1.8 6.3 %collective-permute-start = (f32[101,128]{1,0:T(8,128)}, f32[101,128]{1,0:T(8,128)S(1)}, u32[]{:S(2)}, u32[]{:S(2)}) collective-permute-start(f32[101,128]{1,0:T(8,128)} %get-tuple-element.29), channel_id=1, source_target_pairs={{0,2},{1,3},{2,0},{3,1},{4,6},{5,7},{6,4},{7,5},{8,10},{9,11},{10,... | collective-permute-start | bytes 155144 | tf_op jit(solution)/shard_map/ppermute | solution.py:26
  4.4 16.4 %copy-start.3 = (s32[1,1,128,128]{3,2,1,0:T(8,128)S(1)}, s32[1,1,128,128]{3,2,1,0:T(8,128)}, u32[]{:S(2)}) copy-start(s32[1,1,128,128]{3,2,1,0:T(8,128)} %param.11) | copy-start | bytes 196612
  4.4 16.4 %copy-start.4 = (f32[1,1,128,128]{3,2,1,0:T(8,128)S(1)}, f32[1,1,128,128]{3,2,1,0:T(8,128)}, u32[]{:S(2)}) copy-start(f32[1,1,128,128]{3,2,1,0:T(8,128)} %param.10) | copy-start | bytes 196612
  7.7 38.8 %collective-permute-start.2 = (f32[16,32,128]{2,1,0:T(8,128)}, f32[16,32,128]{2,1,0:T(8,128)S(1)}, u32[]{:S(2)}, u32[]{:S(2)}) collective-permute-start(f32[16,32,128]{2,1,0:T(8,128)} %get-tuple-element.32), channel_id=1, source_target_pairs={{0,2},{1,3},{2,0},{3,1},{4,6},{5,7},{6,4},{7,5},{8,10},{9,11},{10,... | collective-permute-start | bytes 786440 | tf_op jit(solution)/shard_map/ppermute | solution.py:26
  8.1 30.1 %copy-start.6 = (pred[4]{0:T(512)(128)(4,1)}, pred[4]{0:T(512)(128)(4,1)S(1)}, u32[]{:S(2)}) copy-start(pred[4]{0:T(512)(128)(4,1)S(1)} %get-tuple-element.92) | copy-start | bytes 16
  8.1 30.1 %copy-start.8 = (pred[4]{0:T(512)(128)(4,1)}, pred[4]{0:T(512)(128)(4,1)S(1)}, u32[]{:S(2)}) copy-start(pred[4]{0:T(512)(128)(4,1)S(1)} %get-tuple-element.93) | copy-start | bytes 16
  8.7 18.5 %copy-start.10 = (s32[1,1,128]{2,1,0:T(1,128)S(1)}, s32[1,1,128]{2,1,0:T(1,128)}, u32[]{:S(2)}) copy-start(s32[1,1,128]{2,1,0:T(1,128)} %param.12) | copy-start | bytes 1540
  8.7 18.7 %copy-start.5 = (f32[1,1,64,64]{3,2,1,0:T(8,128)S(1)}, f32[1,1,64,64]{3,2,1,0:T(8,128)}, u32[]{:S(2)}) copy-start(f32[1,1,64,64]{3,2,1,0:T(8,128)} %param.14) | copy-start | bytes 49156
  11.1 15.9 %all-to-all-start = ((f32[4,129,128]{2,1,0:T(8,128)}), f32[4,129,128]{2,1,0:T(8,128)S(1)}, u32[]{:S(2)}, u32[]{:S(2)}) async-start(f32[4,129,128]{2,1,0:T(8,128)} %side_borders.1), calls=%async_computation | async-start | bytes 557056 | tf_op jit(solution)/shard_map/all_to_all | solution.py:22
  16.4 49.2 %collective-permute-start.1 = (f32[34,32,128]{2,1,0:T(8,128)}, f32[34,32,128]{2,1,0:T(8,128)S(1)}, u32[]{:S(2)}, u32[]{:S(2)}) collective-permute-start(f32[34,32,128]{2,1,0:T(8,128)} %get-tuple-element.31), channel_id=1, source_target_pairs={{0,1},{1,0},{2,3},{3,2},{4,5},{5,4},{6,7},{7,6},{8,9},{9,8},{10,11... | collective-permute-start | bytes 1671176 | tf_op jit(solution)/shard_map/ppermute | solution.py:26
  16.4 49.2 %collective-permute-start.3 = (f32[34,32,128]{2,1,0:T(8,128)}, f32[34,32,128]{2,1,0:T(8,128)S(1)}, u32[]{:S(2)}, u32[]{:S(2)}) collective-permute-start(f32[34,32,128]{2,1,0:T(8,128)} %get-tuple-element.33), channel_id=1, source_target_pairs={{0,3},{1,2},{2,1},{3,0},{4,7},{5,6},{6,5},{7,4},{8,11},{9,10},{10,... | collective-permute-start | bytes 1671176 | tf_op jit(solution)/shard_map/ppermute | solution.py:26
  19.3 43.5 %collective-permute-start.4 = (f32[18,32,128]{2,1,0:T(8,128)}, f32[18,32,128]{2,1,0:T(8,128)S(1)}, u32[]{:S(2)}, u32[]{:S(2)}) collective-permute-start(f32[18,32,128]{2,1,0:T(8,128)} %get-tuple-element.34), channel_id=1, source_target_pairs={{0,2},{1,3},{2,0},{3,1},{4,6},{5,7},{6,4},{7,5},{8,10},{9,11},{10,... | collective-permute-start | bytes 884744 | tf_op jit(solution)/shard_map/ppermute | solution.py:26
  27.0 38.7 %copy-start = (f32[34,32,128]{2,1,0:T(8,128)S(1)}, f32[34,32,128]{2,1,0:T(8,128)}, u32[]{:S(2)}) copy-start(f32[34,32,128]{2,1,0:T(8,128)} %get-tuple-element.25.p0) | copy-start | bytes 1671172
  27.0 38.7 %copy-start.2 = (f32[101,128]{1,0:T(8,128)S(1)}, f32[101,128]{1,0:T(8,128)}, u32[]{:S(2)}) copy-start(f32[101,128]{1,0:T(8,128)} %get-tuple-element.35.my_pack) | copy-start | bytes 155140
  39.6 26.0 %all-to-all-start.1 = ((f32[4,48,128]{2,1,0:T(8,128)}), f32[4,48,128]{2,1,0:T(8,128)S(1)}, u32[]{:S(2)}, u32[]{:S(2)}) async-start(f32[4,48,128]{2,1,0:T(8,128)} %pad_maximum_fusion.1), calls=%async_computation.1 | async-start | bytes 196608 | tf_op jit(solution)/shard_map/all_to_all | solution.py:22
  72.1 27.2 %copy-start.7 = (pred[4]{0:T(512)(128)(4,1)S(1)}, pred[4]{0:T(512)(128)(4,1)}, u32[]{:S(2)}) copy-start(pred[4]{0:T(512)(128)(4,1)} %copy-done.6) | copy-start | bytes 16
  72.1 27.2 %copy-start.9 = (pred[4]{0:T(512)(128)(4,1)S(1)}, pred[4]{0:T(512)(128)(4,1)}, u32[]{:S(2)}) copy-start(pred[4]{0:T(512)(128)(4,1)} %copy-done.8) | copy-start | bytes 16
  72.1 55.3 %copy-start.1 = (f32[32,32,128]{2,1,0:T(8,128)S(1)}, f32[32,32,128]{2,1,0:T(8,128)}, u32[]{:S(2)}) copy-start(f32[32,32,128]{2,1,0:T(8,128)} %get-tuple-element.40.p0) | copy-start | bytes 1572868
  72.1 11.9 %all-to-all-start.2 = ((f32[4,80,128]{2,1,0:T(8,128)}), f32[4,80,128]{2,1,0:T(8,128)S(1)}, u32[]{:S(2)}, u32[]{:S(2)}) async-start(f32[4,80,128]{2,1,0:T(8,128)} %get-tuple-element.44), calls=%async_computation.2 | async-start | bytes 327680 | tf_op jit(solution)/shard_map/all_to_all | solution.py:22
  78.2 21.2 %copy-start.11 = (f32[128]{0:T(128)S(1)}, f32[128]{0:T(128)}, u32[]{:S(2)}) copy-start(f32[128]{0:T(128)} %get-tuple-element.45) | copy-start | bytes 1540
  78.2 21.2 %copy-start.12 = (f32[128]{0:T(128)S(1)}, f32[128]{0:T(128)}, u32[]{:S(2)}) copy-start(f32[128]{0:T(128)} %get-tuple-element.52) | copy-start | bytes 1540
  78.9 23.1 %collective-permute-start.5 = (f32[32,32,128]{2,1,0:T(8,128)}, f32[32,32,128]{2,1,0:T(8,128)S(1)}, u32[]{:S(2)}, u32[]{:S(2)}) collective-permute-start(f32[32,32,128]{2,1,0:T(8,128)} %get-tuple-element.41), channel_id=1, source_target_pairs={{0,1},{1,0},{2,3},{3,2},{4,5},{5,4},{6,7},{7,6},{8,9},{9,8},{10,11... | collective-permute-start | bytes 1572872 | tf_op jit(solution)/shard_map/ppermute | solution.py:26
  78.9 37.7 %collective-permute-start.6 = (f32[32,32,128]{2,1,0:T(8,128)S(1)}, f32[32,32,128]{2,1,0:T(8,128)S(1)}, u32[]{:S(2)}, u32[]{:S(2)}) collective-permute-start(f32[32,32,128]{2,1,0:T(8,128)S(1)} %get-tuple-element.42), channel_id=1, source_target_pairs={{0,2},{1,3},{2,0},{3,1},{4,6},{5,7},{6,4},{7,5},{8,10},{9,11},{10,... | collective-permute-start | bytes 1572872 | tf_op jit(solution)/shard_map/ppermute | solution.py:26
  81.8 45.6 %collective-permute-start.7 = (f32[32,32,128]{2,1,0:T(8,128)S(1)}, f32[32,32,128]{2,1,0:T(8,128)S(1)}, u32[]{:S(2)}, u32[]{:S(2)}) collective-permute-start(f32[32,32,128]{2,1,0:T(8,128)S(1)} %get-tuple-element.43), channel_id=1, source_target_pairs={{0,3},{1,2},{2,1},{3,0},{4,7},{5,6},{6,5},{7,4},{8,11},{9,10},{10,... | collective-permute-start | bytes 1572872 | tf_op jit(solution)/shard_map/ppermute | solution.py:26
  (3 other events, 24.2 us)

commit v9 on v5

--- a/solution.py
+++ b/solution.py
@@ -8,7 +8,7 @@
 Z = ("sect", "lev")
 PARTS = 4
 BLOCK = 16
-FIRST = 16
+FIRST = 24
 HIGHEST = lax.Precision.HIGHEST
 SMEM = pl.BlockSpec(memory_space=pltpu.SMEM)
 VMEM = pl.BlockSpec(memory_space=pltpu.VMEM)

time: 130 us -> 131 us (level)
    ppermute x8, waiting for transfers between devices: 49.1 us -> 43.5 us  [exchanged(): return lax.ppermute(block, Z, [(at, at ^ bits) for at in range(PARTS)])]
    all_to_all x3, waiting for transfers between devices: 11.6 us -> 17.2 us  [traded(): return lax.all_to_all(blocks, Z, 0, 0)]
where the time goes in v9:
time: 131 us; the launch traced here: 130 us
  waiting for transfers between devices  60.7 us (46%)
  starting transfers between devices  27.7 us (21%)
  blocking collectives  19.7 us (15%)
  Pallas kernels  16.4 us (13%)
  local copies, waits for them, and re-layouts  2.52 us (2%)
  other arithmetic  2.03 us (2%)
    ppermute x8, waiting for transfers between devices, exchanged(): return lax.ppermute(block, Z, [(at, at ^ bits) for at in range(PARTS)])  43.5 us
    all_gather x2, blocking collectives, tile_halo(): every = lax.all_gather(edges, 'tile', axis=0)  19.7 us
    all_to_all x3, waiting for transfers between devices, traded(): return lax.all_to_all(blocks, Z, 0, 0)  17.2 us
    all_to_all x3, starting transfers between devices, traded(): return lax.all_to_all(blocks, Z, 0, 0)  16.7 us
    ppermute x8, starting transfers between devices, exchanged(): return lax.ppermute(block, Z, [(at, at ^ bits) for at in range(PARTS)])  10.9 us
    pallas_call x1, Pallas kernels, two_steps(): pl.pallas_call(steps_kernel, out_shape=[part] * PARTS + [pltpu.VMEM((PART...  6.86 us
    pallas_call x1, Pallas kernels, split_columns(): pl.pallas_call(split_kernel, grid=(levels // BLOCK,), out_shape=[jax.Shap...  3.3 us
  transfers between devices with their start and end apart: 11, of which 7 were waited for; matrix products, arithmetic and copies ran while one was open for 4% of the time, Pallas kernels for 4%

profile of v9, /device:TPU:8, one launch (start us, length us, event | category | flops | bytes accessed | tf_op | source)
XLA Modules:
  0.0 129.9 jit_solution(14172026382557648861)
XLA Ops:
  0.0 1.8 %parameters.1 = (f32[101,128]{1,0:T(8,128)}, f32[101,128]{1,0:T(8,128)}) custom-call(s32[1]{0:T(128)} %bitcast.place, s32[128,128]{1,0:T(8,128)} %bitcast.86, f32[128,128]{1,0:T(8,128)} %bitcast.89, f32[64,64]{1,0:T(8,128)} %bitcast.92, s32[1,128]{1,0:T(1,128)} %bitcast.94), custom_call_target="tpu_custom_call" | custom-call | tf_op jit(solution)/shard_map/parameters/pallas_call | solution.py:58
  1.8 2.6 %collective-permute-start = (f32[101,128]{1,0:T(8,128)}, f32[101,128]{1,0:T(8,128)S(1)}, u32[]{:S(2)}, u32[]{:S(2)}) collective-permute-start(f32[101,128]{1,0:T(8,128)} %get-tuple-element.29), channel_id=1, source_target_pairs={{0,2},{1,3},{2,0},{3,1},{4,6},{5,7},{6,4},{7,5},{8,10},{9,11},{10,... | collective-permute-start | bytes 155144 | tf_op jit(solution)/shard_map/ppermute | solution.py:26
  4.4 3.3 %split_columns.1 = (f32[34,32,128]{2,1,0:T(8,128)}, f32[34,32,128]{2,1,0:T(8,128)}, f32[24,32,128]{2,1,0:T(8,128)}, f32[34,32,128]{2,1,0:T(8,128)}, f32[10,32,128]{2,1,0:T(8,128)}, /*index=5*/f32[2,32,128]{2,1,0:T(8,128)}) custom-call(s32[1]{0:T(128)} %bitcast.place, f32[32,128,128]{2,1,0:T(8,128)} %bitcast.80), custom_call_target="tpu_custom_call" | custom-call | tf_op jit(solution)/shard_map/split_columns/pallas_call | solution.py:86
  8.2 0.6 fusion.30.lent_rows
  8.8 2.3 %side_borders.1 = f32[4,129,128]{2,1,0:T(8,128)} custom-call(s32[1]{0:T(128)} %bitcast.place, s32[128]{0:T(128)} %fusion.30.lent_rows, f32[32,128,128]{2,1,0:T(8,128)} %bitcast.81, f32[2,32,128]{2,1,0:T(8,128)} %get-tuple-element.30.ends, f32[1,32]{1,0:T(1,128)} %gain.1), custom_call_target="tpu_custom_call" | custom-call | tf_op jit(solution)/shard_map/side_borders/pallas_call | solution.py:120
  11.1 5.3 %all-to-all-start = ((f32[4,129,128]{2,1,0:T(8,128)}), f32[4,129,128]{2,1,0:T(8,128)S(1)}, u32[]{:S(2)}, u32[]{:S(2)}) async-start(f32[4,129,128]{2,1,0:T(8,128)} %side_borders.1), calls=%async_computation | async-start | bytes 557056 | tf_op jit(solution)/shard_map/all_to_all | solution.py:22
  16.5 2.9 %collective-permute-start.3 = (f32[34,32,128]{2,1,0:T(8,128)}, f32[34,32,128]{2,1,0:T(8,128)S(1)}, u32[]{:S(2)}, u32[]{:S(2)}) collective-permute-start(f32[34,32,128]{2,1,0:T(8,128)} %get-tuple-element.33), channel_id=1, source_target_pairs={{0,3},{1,2},{2,1},{3,0},{4,7},{5,6},{6,5},{7,4},{8,11},{9,10},{10,... | collective-permute-start | bytes 1671176 | tf_op jit(solution)/shard_map/ppermute | solution.py:26
  19.4 1.5 %collective-permute-start.4 = (f32[10,32,128]{2,1,0:T(8,128)S(1)}, f32[10,32,128]{2,1,0:T(8,128)S(1)}, u32[]{:S(2)}, u32[]{:S(2)}) collective-permute-start(f32[10,32,128]{2,1,0:T(8,128)S(1)} %copy-done.9), channel_id=1, source_target_pairs={{0,2},{1,3},{2,0},{3,1},{4,6},{5,7},{6,4},{7,5},{8,10},{9,11},{10,... | collective-permute-start | bytes 491528 | tf_op jit(solution)/shard_map/ppermute | solution.py:26
  21.1 11.5 %all-to-all-done = f32[4,129,128]{2,1,0:T(8,128)S(1)} async-done(((f32[4,129,128]{2,1,0:T(8,128)}), f32[4,129,128]{2,1,0:T(8,128)S(1)}, u32[]{:S(2)}, u32[]{:S(2)}) %all-to-all-start) | async-done | bytes 264224 | tf_op jit(solution)/shard_map/all_to_all | solution.py:22
  33.3 9.9 %all-gather = f32[32,32,128]{2,1,0:T(8,128)S(1)} all-gather(f32[4,32,128]{2,1,0:T(8,128)S(1)} %fusion), channel_id=2, replica_groups=mesh['tile'=8,'sect'=2,'lev'=2] {'tile'}, dimensions={0}, use_global_device_ids=true | all-gather | bytes 589824 | tf_op jit(solution)/shard_map/all_gather | solution.py:333
  44.6 0.6 pad_maximum_fusion.1
  45.2 6.2 %all-to-all-start.1 = ((f32[4,48,128]{2,1,0:T(8,128)}), f32[4,48,128]{2,1,0:T(8,128)S(1)}, u32[]{:S(2)}, u32[]{:S(2)}) async-start(f32[4,48,128]{2,1,0:T(8,128)} %pad_maximum_fusion.1), calls=%async_computation.1 | async-start | bytes 196608 | tf_op jit(solution)/shard_map/all_to_all | solution.py:22
  51.5 11.3 %collective-permute-done.4.q2 = f32[10,32,128]{2,1,0:T(8,128)S(1)} collective-permute-done((f32[10,32,128]{2,1,0:T(8,128)S(1)}, f32[10,32,128]{2,1,0:T(8,128)S(1)}, u32[]{:S(2)}, u32[]{:S(2)}) %collective-permute-start.4) | collective-permute-done | bytes 163872 | tf_op jit(solution)/shard_map/ppermute | solution.py:26
  62.8 2.8 %all-to-all-done.1.halos = f32[4,48,128]{2,1,0:T(8,128)S(1)} async-done(((f32[4,48,128]{2,1,0:T(8,128)}), f32[4,48,128]{2,1,0:T(8,128)S(1)}, u32[]{:S(2)}, u32[]{:S(2)}) %all-to-all-start.1) | async-done | bytes 98336 | tf_op jit(solution)/shard_map/all_to_all | solution.py:22
  65.7 6.9 %two_steps.1 = (f32[32,32,128]{2,1,0:T(8,128)}, f32[32,32,128]{2,1,0:T(8,128)}, f32[32,32,128]{2,1,0:T(8,128)}, f32[32,32,128]{2,1,0:T(8,128)}, f32[4,80,128]{2,1,0:T(8,128)}) custom-call(s32[1]{0:T(128)} %bitcast.place, f32[34,32,128]{2,1,0:T(8,128)S(1)} %copy-done, f32[34,32,128]{2,1,0:T(8,128)S(1)} %collective-permute-done.1.p1, ...), custom_call_target="tpu_custom_call" | custom-call | tf_op jit(solution)/shard_map/two_steps/pallas_call | solution.py:317
  72.5 5.2 %all-to-all-start.2 = ((f32[4,80,128]{2,1,0:T(8,128)}), f32[4,80,128]{2,1,0:T(8,128)S(1)}, u32[]{:S(2)}, u32[]{:S(2)}) async-start(f32[4,80,128]{2,1,0:T(8,128)} %get-tuple-element.44), calls=%async_computation.2 | async-start | bytes 327680 | tf_op jit(solution)/shard_map/all_to_all | solution.py:22
  78.2 2.9 %collective-permute-start.6 = (f32[32,32,128]{2,1,0:T(8,128)}, f32[32,32,128]{2,1,0:T(8,128)S(1)}, u32[]{:S(2)}, u32[]{:S(2)}) collective-permute-start(f32[32,32,128]{2,1,0:T(8,128)} %get-tuple-element.42), channel_id=1, source_target_pairs={{0,2},{1,3},{2,0},{3,1},{4,6},{5,7},{6,4},{7,5},{8,10},{9,11},{10,... | collective-permute-start | bytes 1572872 | tf_op jit(solution)/shard_map/ppermute | solution.py:26
  81.1 0.6 collective-permute-start.7
  81.6 2.9 %all-to-all-done.2 = f32[4,80,128]{2,1,0:T(8,128)S(1)} async-done(((f32[4,80,128]{2,1,0:T(8,128)}), f32[4,80,128]{2,1,0:T(8,128)S(1)}, u32[]{:S(2)}, u32[]{:S(2)}) %all-to-all-start.2) | async-done | bytes 163872 | tf_op jit(solution)/shard_map/all_to_all | solution.py:22
  84.9 9.9 %all-gather.1 = f32[32,32,128]{2,1,0:T(8,128)S(1)} all-gather(f32[4,32,128]{2,1,0:T(8,128)S(1)} %pad_maximum_fusion.2), channel_id=3, replica_groups=mesh['tile'=8,'sect'=2,'lev'=2] {'tile'}, dimensions={0}, use_global_device_ids=true | all-gather | bytes 589824 | tf_op jit(solution)/shard_map/all_gather | solution.py:333
  95.6 5.9 %collective-permute-done.5.p1 = f32[32,32,128]{2,1,0:T(8,128)S(1)} collective-permute-done((f32[32,32,128]{2,1,0:T(8,128)}, f32[32,32,128]{2,1,0:T(8,128)S(1)}, u32[]{:S(2)}, u32[]{:S(2)}) %collective-permute-start.5) | collective-permute-done | bytes 524320 | tf_op jit(solution)/shard_map/ppermute | solution.py:26
  101.5 14.7 %collective-permute-done.6.p2 = f32[32,32,128]{2,1,0:T(8,128)S(1)} collective-permute-done((f32[32,32,128]{2,1,0:T(8,128)}, f32[32,32,128]{2,1,0:T(8,128)S(1)}, u32[]{:S(2)}, u32[]{:S(2)}) %collective-permute-start.6) | collective-permute-done | bytes 524320 | tf_op jit(solution)/shard_map/ppermute | solution.py:26
  116.2 11.6 %collective-permute-done.7.p3 = f32[32,32,128]{2,1,0:T(8,128)S(1)} collective-permute-done((f32[32,32,128]{2,1,0:T(8,128)}, f32[32,32,128]{2,1,0:T(8,128)S(1)}, u32[]{:S(2)}, u32[]{:S(2)}) %collective-permute-start.7) | collective-permute-done | bytes 524320 | tf_op jit(solution)/shard_map/ppermute | solution.py:26
  127.8 2.1 %join_columns.1 = f32[32,128,128]{2,1,0:T(8,128)} custom-call(s32[1]{0:T(128)} %bitcast.place, f32[32,32,128]{2,1,0:T(8,128)S(1)} %copy-done.1, f32[32,32,128]{2,1,0:T(8,128)S(1)} %collective-permute-done.5.p1, f32[32,32,128]{2,1,0:T(8,128)S(1)} %collective-permute-done.6.p2, f32[32,32,128]{2,1,0:T(8,128)S(1)} %collective-permute-done.7.p3, ...), custom_call_target="tpu_custom_call" | custom-call | tf_op jit(solution)/shard_map/join_columns/pallas_call | solution.py:151
  (75 shorter events, 4.4 us)
Async XLA Ops:
  0.0 8.1 %copy-start.8 = (s32[1,4]{1,0:T(1,128)S(1)}, s32[1,4]{1,0:T(1,128)}, u32[]{:S(2)}) copy-start(s32[1,4]{1,0:T(1,128)} %param.15) | copy-start | bytes 52
  0.0 8.1 %copy-start.7 = (s32[1,4]{1,0:T(1,128)S(1)}, s32[1,4]{1,0:T(1,128)}, u32[]{:S(2)}) copy-start(s32[1,4]{1,0:T(1,128)} %param.17) | copy-start | bytes 52
  0.0 8.1 %copy-start.10 = (s32[1,4]{1,0:T(1,128)S(1)}, s32[1,4]{1,0:T(1,128)}, u32[]{:S(2)}) copy-start(s32[1,4]{1,0:T(1,128)} %param.16) | copy-start | bytes 52
  1.8 6.3 %collective-permute-start = (f32[101,128]{1,0:T(8,128)}, f32[101,128]{1,0:T(8,128)S(1)}, u32[]{:S(2)}, u32[]{:S(2)}) collective-permute-start(f32[101,128]{1,0:T(8,128)} %get-tuple-element.29), channel_id=1, source_target_pairs={{0,2},{1,3},{2,0},{3,1},{4,6},{5,7},{6,4},{7,5},{8,10},{9,11},{10,... | collective-permute-start | bytes 155144 | tf_op jit(solution)/shard_map/ppermute | solution.py:26
  4.4 16.4 %copy-start.3 = (s32[1,1,128,128]{3,2,1,0:T(8,128)S(1)}, s32[1,1,128,128]{3,2,1,0:T(8,128)}, u32[]{:S(2)}) copy-start(s32[1,1,128,128]{3,2,1,0:T(8,128)} %param.11) | copy-start | bytes 196612
  4.4 16.4 %copy-start.4 = (f32[1,1,128,128]{3,2,1,0:T(8,128)S(1)}, f32[1,1,128,128]{3,2,1,0:T(8,128)}, u32[]{:S(2)}) copy-start(f32[1,1,128,128]{3,2,1,0:T(8,128)} %param.10) | copy-start | bytes 196612
  7.7 11.7 %copy-start.9 = (f32[10,32,128]{2,1,0:T(8,128)S(1)}, f32[10,32,128]{2,1,0:T(8,128)}, u32[]{:S(2)}) copy-start(f32[10,32,128]{2,1,0:T(8,128)} %get-tuple-element.34) | copy-start | bytes 491524
  7.7 55.1 %collective-permute-start.2 = (f32[24,32,128]{2,1,0:T(8,128)}, f32[24,32,128]{2,1,0:T(8,128)S(1)}, u32[]{:S(2)}, u32[]{:S(2)}) collective-permute-start(f32[24,32,128]{2,1,0:T(8,128)} %get-tuple-element.32), channel_id=1, source_target_pairs={{0,2},{1,3},{2,0},{3,1},{4,6},{5,7},{6,4},{7,5},{8,10},{9,11},{10,... | collective-permute-start | bytes 1179656 | tf_op jit(solution)/shard_map/ppermute | solution.py:26
  8.8 24.0 %copy-start.6 = (s32[1,1,128]{2,1,0:T(1,128)S(1)}, s32[1,1,128]{2,1,0:T(1,128)}, u32[]{:S(2)}) copy-start(s32[1,1,128]{2,1,0:T(1,128)} %param.12) | copy-start | bytes 1540
  8.8 24.2 %copy-start.5 = (f32[1,1,64,64]{3,2,1,0:T(8,128)S(1)}, f32[1,1,64,64]{3,2,1,0:T(8,128)}, u32[]{:S(2)}) copy-start(f32[1,1,64,64]{3,2,1,0:T(8,128)} %param.14) | copy-start | bytes 49156
  11.1 21.5 %all-to-all-start = ((f32[4,129,128]{2,1,0:T(8,128)}), f32[4,129,128]{2,1,0:T(8,128)S(1)}, u32[]{:S(2)}, u32[]{:S(2)}) async-start(f32[4,129,128]{2,1,0:T(8,128)} %side_borders.1), calls=%async_computation | async-start | bytes 557056 | tf_op jit(solution)/shard_map/all_to_all | solution.py:22
  16.4 49.2 %collective-permute-start.1 = (f32[34,32,128]{2,1,0:T(8,128)}, f32[34,32,128]{2,1,0:T(8,128)S(1)}, u32[]{:S(2)}, u32[]{:S(2)}) collective-permute-start(f32[34,32,128]{2,1,0:T(8,128)} %get-tuple-element.31), channel_id=1, source_target_pairs={{0,1},{1,0},{2,3},{3,2},{4,5},{5,4},{6,7},{7,6},{8,9},{9,8},{10,11... | collective-permute-start | bytes 1671176 | tf_op jit(solution)/shard_map/ppermute | solution.py:26
  16.5 49.2 %collective-permute-start.3 = (f32[34,32,128]{2,1,0:T(8,128)}, f32[34,32,128]{2,1,0:T(8,128)S(1)}, u32[]{:S(2)}, u32[]{:S(2)}) collective-permute-start(f32[34,32,128]{2,1,0:T(8,128)} %get-tuple-element.33), channel_id=1, source_target_pairs={{0,3},{1,2},{2,1},{3,0},{4,7},{5,6},{6,5},{7,4},{8,11},{9,10},{10,... | collective-permute-start | bytes 1671176 | tf_op jit(solution)/shard_map/ppermute | solution.py:26
  19.4 43.4 %collective-permute-start.4 = (f32[10,32,128]{2,1,0:T(8,128)S(1)}, f32[10,32,128]{2,1,0:T(8,128)S(1)}, u32[]{:S(2)}, u32[]{:S(2)}) collective-permute-start(f32[10,32,128]{2,1,0:T(8,128)S(1)} %copy-done.9), channel_id=1, source_target_pairs={{0,2},{1,3},{2,0},{3,1},{4,6},{5,7},{6,4},{7,5},{8,10},{9,11},{10,... | collective-permute-start | bytes 491528 | tf_op jit(solution)/shard_map/ppermute | solution.py:26
  32.6 33.1 %copy-start = (f32[34,32,128]{2,1,0:T(8,128)S(1)}, f32[34,32,128]{2,1,0:T(8,128)}, u32[]{:S(2)}) copy-start(f32[34,32,128]{2,1,0:T(8,128)} %get-tuple-element.25.p0) | copy-start | bytes 1671172
  32.6 33.0 %copy-start.2 = (f32[101,128]{1,0:T(8,128)S(1)}, f32[101,128]{1,0:T(8,128)}, u32[]{:S(2)}) copy-start(f32[101,128]{1,0:T(8,128)} %get-tuple-element.35.my_pack) | copy-start | bytes 155140
  45.2 20.4 %all-to-all-start.1 = ((f32[4,48,128]{2,1,0:T(8,128)}), f32[4,48,128]{2,1,0:T(8,128)S(1)}, u32[]{:S(2)}, u32[]{:S(2)}) async-start(f32[4,48,128]{2,1,0:T(8,128)} %pad_maximum_fusion.1), calls=%async_computation.1 | async-start | bytes 196608 | tf_op jit(solution)/shard_map/all_to_all | solution.py:22
  72.5 55.3 %copy-start.1 = (f32[32,32,128]{2,1,0:T(8,128)S(1)}, f32[32,32,128]{2,1,0:T(8,128)}, u32[]{:S(2)}) copy-start(f32[32,32,128]{2,1,0:T(8,128)} %get-tuple-element.40.p0) | copy-start | bytes 1572868
  72.5 12.0 %all-to-all-start.2 = ((f32[4,80,128]{2,1,0:T(8,128)}), f32[4,80,128]{2,1,0:T(8,128)S(1)}, u32[]{:S(2)}, u32[]{:S(2)}) async-start(f32[4,80,128]{2,1,0:T(8,128)} %get-tuple-element.44), calls=%async_computation.2 | async-start | bytes 327680 | tf_op jit(solution)/shard_map/all_to_all | solution.py:22
  78.1 23.5 %collective-permute-start.5 = (f32[32,32,128]{2,1,0:T(8,128)}, f32[32,32,128]{2,1,0:T(8,128)S(1)}, u32[]{:S(2)}, u32[]{:S(2)}) collective-permute-start(f32[32,32,128]{2,1,0:T(8,128)} %get-tuple-element.41), channel_id=1, source_target_pairs={{0,1},{1,0},{2,3},{3,2},{4,5},{5,4},{6,7},{7,6},{8,9},{9,8},{10,11... | collective-permute-start | bytes 1572872 | tf_op jit(solution)/shard_map/ppermute | solution.py:26
  78.2 38.1 %collective-permute-start.6 = (f32[32,32,128]{2,1,0:T(8,128)}, f32[32,32,128]{2,1,0:T(8,128)S(1)}, u32[]{:S(2)}, u32[]{:S(2)}) collective-permute-start(f32[32,32,128]{2,1,0:T(8,128)} %get-tuple-element.42), channel_id=1, source_target_pairs={{0,2},{1,3},{2,0},{3,1},{4,6},{5,7},{6,4},{7,5},{8,10},{9,11},{10,... | collective-permute-start | bytes 1572872 | tf_op jit(solution)/shard_map/ppermute | solution.py:26
  81.1 46.7 %collective-permute-start.7 = (f32[32,32,128]{2,1,0:T(8,128)}, f32[32,32,128]{2,1,0:T(8,128)S(1)}, u32[]{:S(2)}, u32[]{:S(2)}) collective-permute-start(f32[32,32,128]{2,1,0:T(8,128)} %get-tuple-element.43), channel_id=1, source_target_pairs={{0,3},{1,2},{2,1},{3,0},{4,7},{5,6},{6,5},{7,4},{8,11},{9,10},{10,... | collective-permute-start | bytes 1572872 | tf_op jit(solution)/shard_map/ppermute | solution.py:26
